TPU v7x, 32 devices: a whole 2x2x4 slice. The times are simulated.
32 devices in a mesh: dp: 8 (over z, x), row: 2 (over y), col: 2 (over core).
Axes of the slice: x: 2, y: 2, z: 4, core: 2. Of those that a mesh axis runs over, the one named last changes fastest.
Arguments:
- hidden_in: bfloat16 [2048, 768], P('dp', ('row', 'col')), may hold values from -6 to 6
- encoder_states: bfloat16 [4096, 768], P('dp', ('row', 'col')), may hold values from -6 to 6
- token_segments: int32 [8, 256], P('dp'), may hold values from 0 to 2, never falling along the last dimension, each value on 1 to 152 neighbouring positions
- source_segments: int32 [8, 512], P('dp'), may hold values from 0 to 2, never falling along the last dimension, each value on 1 to 304 neighbouring positions
- buckets: int32 [256, 256], replicated, may hold values from 0 to 31
- gain_self: float32 [768], P(('row', 'col')), may hold values from 0.5 to 1.5
- gain_cross: float32 [768], P(('row', 'col')), may hold values from 0.5 to 1.5
- gain_feed: float32 [768], P(('row', 'col')), may hold values from 0.5 to 1.5
- self_querykey: bfloat16 [768, 1536], P('row', 'col'), may hold values from -0.078125 to 0.078125
- self_value: bfloat16 [768, 768], P('row', 'col'), may hold values from -0.21875 to 0.21875
- self_output: bfloat16 [768, 768], P('col', 'row'), may hold values from -0.875 to 0.875
- cross_query: bfloat16 [768, 768], P('row', 'col'), may hold values from -0.0546875 to 0.0546875
- cross_keyvalue: bfloat16 [768, 1536], P('row', 'col'), may hold values from -0.15625 to 0.15625
- cross_output: bfloat16 [768, 768], P('col', 'row'), may hold values from -0.875 to 0.875
- gate_weight: bfloat16 [768, 2048], P('row', 'col'), may hold values from -0.21875 to 0.21875
- up_weight: bfloat16 [768, 2048], P('row', 'col'), may hold values from -0.21875 to 0.21875
- down_weight: bfloat16 [2048, 768], P('col', 'row'), may hold values from -0.125 to 0.125
- bias_table: float32 [32, 12], P(None, ('col', 'row')), may hold values from -6 to 6
- cotangent: bfloat16 [2048, 768], P('dp', ('row', 'col')), may hold values from -6 to 6
Outputs:
- hidden_out: bfloat16 [2048, 768], P('dp', ('row', 'col'))
- grad_hidden: float32 [2048, 768], P('dp', ('row', 'col'))
- grad_encoder: float32 [4096, 768], P('dp', ('row', 'col'))
- querykey_grad: float32 [768, 1536], P(('row', 'dp'), 'col')
- value_grad: float32 [768, 768], P(('row', 'dp'), 'col')
- output_grad: float32 [768, 768], P(('col', 'dp'), 'row')
- crossquery_grad: float32 [768, 768], P(('row', 'dp'), 'col')
- keyvalue_grad: float32 [768, 1536], P(('row', 'dp'), 'col')
- crossout_grad: float32 [768, 768], P(('col', 'dp'), 'row')
- gate_grad: float32 [768, 2048], P(('row', 'dp'), 'col')
- upweight_grad: float32 [768, 2048], P(('row', 'dp'), 'col')
- down_grad: float32 [2048, 768], P(('col', 'dp'), 'row')
- gainself_grad: float32 [768], P(('row', 'col'))
- gaincross_grad: float32 [768], P(('row', 'col'))
- gainfeed_grad: float32 [768], P(('row', 'col'))
- table_grad: float32 [32, 12], P(None, ('col', 'row'))
Inputs may be any that keep to these rules, and one draw needn't show every extreme that they name: `token_segments`: in each sequence the numbers never fall, every value from 0 to 2 occurs, and no document has more than 152 tokens. `source_segments`: in each sequence the numbers never fall, every value from 0 to 2 occurs, and no document has more than 304 positions.
All inputs are finite; a program needn't handle non-finite values.
Results may differ from a plain program's by a relative error of at most 0.02.
Values may be sent and summed in bfloat16 or wider, within the bound.
No kernel may reach another device: no remote copies, remote signals or barrier semaphores. Data moves between devices by JAX's collectives and lax.ppermute only.
A program may use at most 128 MiB of HBM per device.

v0:
```python
import math

import jax
import jax.numpy as jnp
from jax import lax
from jax.sharding import PartitionSpec as P

D = 768
DH = 64


EPS = 1e-06
ROOT = 0.7978845608028654
CUBIC = 0.044715


def gelu_tanh(value):
    return 0.5 * value * (1.0 + jnp.tanh(ROOT * (value + CUBIC * value * value * value)))


def gelu_slope(value):
    inner = jnp.tanh(ROOT * (value + CUBIC * value * value * value))
    return 0.5 * (1.0 + inner) + 0.5 * value * (1.0 - inner * inner) * ROOT * (
        1.0 + 3.0 * CUBIC * value * value
    )


def matmul(left, right):
    return jnp.dot(left, right, preferred_element_type=jnp.float32)


def matmul_back(left, right):
    return lax.dot_general(
        left, right, (((1,), (1,)), ((), ())), preferred_element_type=jnp.float32
    )


def outer_sum(left, right):
    return lax.dot_general(
        left, right, (((0,), (0,)), ((), ())), preferred_element_type=jnp.float32
    )


def feature_total(values):
    return lax.psum(values, ("row", "col"))


def gather_features(values):
    return lax.all_gather(values, "col", axis=1, tiled=True)


def gather_heads(values):
    return lax.all_gather(values, "row", axis=1, tiled=True)


def sum_features(terms):
    return lax.psum_scatter(terms, "col", scatter_dimension=1, tiled=True)


def sum_heads(terms):
    return lax.psum_scatter(
        terms.astype(jnp.bfloat16), "row", scatter_dimension=1, tiled=True
    ).astype(jnp.float32)


def sum_pair(first, second):
    return (
        lax.psum_scatter(first, "row", scatter_dimension=1, tiled=True),
        lax.psum_scatter(second, "row", scatter_dimension=1, tiled=True),
    )


def gather_pair(first, second):
    return (
        lax.all_gather(first, "row", axis=1, tiled=True),
        lax.all_gather(second, "row", axis=1, tiled=True),
    )


def rms_norm(resid, gain):
    total = feature_total(jnp.sum(resid * resid, axis=1))
    scale = lax.rsqrt(total / D + EPS)
    return ((resid * scale[:, None] * gain).astype(jnp.bfloat16), scale)


def rms_back(upstream, resid, scale, gain):
    normed = resid * scale[:, None]
    scaled = upstream * gain
    total = feature_total(jnp.sum(scaled * normed, axis=1))
    grad = scale[:, None] * (scaled - normed * (total / D)[:, None])
    return (grad, jnp.sum(upstream * normed, axis=0))


def masked_scores(queries, keys, bias, allowed):
    scores = jnp.einsum("qhd,khd->hqk", queries, keys, preferred_element_type=jnp.float32) + bias
    return jnp.where(allowed[None], scores, -jnp.inf)


def attend(scores, values):
    top = jnp.max(scores, axis=2, keepdims=True)
    logsum = top[:, :, 0] + jnp.log(jnp.sum(jnp.exp(scores - top), axis=2))
    probs = jnp.exp(scores - logsum[:, :, None]).astype(jnp.bfloat16)
    mixed = jnp.einsum("hqk,khd->qhd", probs, values, preferred_element_type=jnp.float32)
    return (mixed.astype(jnp.bfloat16), logsum)


def attend_back(scores, logsum, queries, keys, values, mixed, upstream):
    probs = jnp.exp(scores - logsum[:, :, None])
    drift = jnp.einsum("qhd,khd->hqk", upstream, values, preferred_element_type=jnp.float32)
    centre = jnp.sum(upstream.astype(jnp.float32) * mixed.astype(jnp.float32), axis=2)
    dscores = probs * (drift - jnp.transpose(centre)[:, :, None])
    lowered = dscores.astype(jnp.bfloat16)
    grad_query = jnp.einsum(
        "hqk,khd->qhd", lowered, keys, preferred_element_type=jnp.float32
    ).astype(jnp.bfloat16)
    grad_key = jnp.einsum(
        "hqk,qhd->khd", lowered, queries, preferred_element_type=jnp.float32
    ).astype(jnp.bfloat16)
    grad_value = jnp.einsum(
        "hqk,qhd->khd", probs.astype(jnp.bfloat16), upstream, preferred_element_type=jnp.float32
    ).astype(jnp.bfloat16)
    return (grad_query, grad_key, grad_value, dscores)


def bucket_bias(buckets, table):
    length = buckets.shape[0]
    block = math.gcd(length, 128)
    blocks = buckets.reshape(length // block, block, buckets.shape[1])
    labels = jnp.arange(table.shape[0], dtype=jnp.int32)

    def one_block(block_ids):
        onehot = (block_ids[:, :, None] == labels).astype(jnp.float32)
        return jnp.einsum("ikb,bh->hik", onehot, table, precision=lax.Precision.HIGHEST)

    parts = lax.map(one_block, blocks)
    return jnp.transpose(parts, (1, 0, 2, 3)).reshape(table.shape[1], length, buckets.shape[1])


def bucket_grad(buckets, grid, count):
    length = buckets.shape[0]
    block = math.gcd(length, 128)
    blocks = buckets.reshape(length // block, block, buckets.shape[1])
    cells = jnp.transpose(
        grid.reshape(grid.shape[0], length // block, block, grid.shape[2]), (1, 0, 2, 3)
    )
    labels = jnp.arange(count, dtype=jnp.int32)

    def one_block(total, pieces):
        block_ids, block_grid = pieces
        onehot = (block_ids[:, :, None] == labels).astype(jnp.float32)
        return (
            total + jnp.einsum("hik,ikb->bh", block_grid, onehot, precision=lax.Precision.HIGHEST),
            None,
        )

    total, unused = lax.scan(
        one_block, jnp.zeros((count, grid.shape[0]), jnp.float32), (blocks, cells)
    )
    return total


def shards(
    hidden_in,
    encoder_states,
    token_segments,
    source_segments,
    buckets,
    gain_self,
    gain_cross,
    gain_feed,
    self_querykey,
    self_value,
    self_output,
    cross_query,
    cross_keyvalue,
    cross_output,
    gate_weight,
    up_weight,
    down_weight,
    bias_table,
    cotangent,
):
    tokens = hidden_in.shape[0]
    sources = encoder_states.shape[0]
    sequences = token_segments.shape[0]
    length = token_segments.shape[1]
    source_length = source_segments.shape[1]
    heads = bias_table.shape[1]
    places = jnp.arange(length, dtype=jnp.int32)
    causal = places[None, :] <= places[:, None]
    position_bias = bucket_bias(buckets, bias_table)

    def self_allowed(segment):
        return causal & (segment[:, None] == segment[None, :])

    resid_in = hidden_in.astype(jnp.float32)
    normed_self, scale_self = rms_norm(resid_in, gain_self)
    inputs_self = gather_features(normed_self)
    query_key, value_rows = sum_pair(
        matmul(inputs_self, self_querykey), matmul(inputs_self, self_value)
    )
    query_key = query_key.astype(jnp.bfloat16).reshape(sequences, length, heads, 2, DH)
    value_rows = value_rows.astype(jnp.bfloat16).reshape(sequences, length, heads, DH)
    self_queries = query_key[:, :, :, 0]
    self_keys = query_key[:, :, :, 1]

    def self_forward(pieces):
        queries, keys, values, segment = pieces
        return attend(masked_scores(queries, keys, position_bias, self_allowed(segment)), values)

    self_mixed, self_lse = lax.map(
        self_forward, (self_queries, self_keys, value_rows, token_segments)
    )
    heads_self = gather_heads(self_mixed.reshape(tokens, heads * DH))
    resid_attn = resid_in + sum_features(matmul(heads_self, self_output))
    normed_cross, scale_cross = rms_norm(resid_attn, gain_cross)
    inputs_cross, inputs_source = (
        lax.all_gather(normed_cross, "col", axis=1, tiled=True),
        lax.all_gather(encoder_states, "col", axis=1, tiled=True),
    )
    cross_q, cross_kv = sum_pair(
        matmul(inputs_cross, cross_query), matmul(inputs_source, cross_keyvalue)
    )
    cross_q = cross_q.astype(jnp.bfloat16).reshape(sequences, length, heads, DH)
    cross_kv = cross_kv.astype(jnp.bfloat16).reshape(sequences, source_length, heads, 2, DH)
    cross_keys = cross_kv[:, :, :, 0]
    cross_values = cross_kv[:, :, :, 1]

    def cross_forward(pieces):
        queries, keys, values, segment, source = pieces
        return attend(
            masked_scores(queries, keys, 0.0, segment[:, None] == source[None, :]), values
        )

    cross_mixed, cross_lse = lax.map(
        cross_forward, (cross_q, cross_keys, cross_values, token_segments, source_segments)
    )
    heads_cross = gather_heads(cross_mixed.reshape(tokens, heads * DH))
    resid_cross = resid_attn + sum_features(matmul(heads_cross, cross_output))
    normed_feed, scale_feed = rms_norm(resid_cross, gain_feed)
    inputs_feed = gather_features(normed_feed)
    gate_act, up_act = sum_pair(matmul(inputs_feed, gate_weight), matmul(inputs_feed, up_weight))
    gelu_gate = gelu_tanh(gate_act)
    feed_hidden = (gelu_gate * up_act).astype(jnp.bfloat16)
    heads_feed = gather_heads(feed_hidden)
    hidden_out = (resid_cross + sum_features(matmul(heads_feed, down_weight))).astype(jnp.bfloat16)
    upstream_feed = gather_features(cotangent)
    down_local = outer_sum(heads_feed, upstream_feed)
    grad_feed = sum_heads(matmul_back(upstream_feed, down_weight))
    gate_delta = (grad_feed * up_act * gelu_slope(gate_act)).astype(jnp.bfloat16)
    up_delta = (grad_feed * gelu_gate).astype(jnp.bfloat16)
    wide_gate, wide_up = gather_pair(gate_delta, up_delta)
    gate_local = outer_sum(inputs_feed, wide_gate)
    up_local = outer_sum(inputs_feed, wide_up)
    grad_normed_feed = sum_features(
        matmul_back(wide_gate, gate_weight) + matmul_back(wide_up, up_weight)
    )
    back_feed, feed_gain_local = rms_back(grad_normed_feed, resid_cross, scale_feed, gain_feed)
    grad_resid_cross = cotangent.astype(jnp.float32) + back_feed
    upstream_cross = gather_features(grad_resid_cross.astype(jnp.bfloat16))
    crossout_local = outer_sum(heads_cross, upstream_cross)
    cross_delta = (
        sum_heads(matmul_back(upstream_cross, cross_output))
        .astype(jnp.bfloat16)
        .reshape(sequences, length, heads, DH)
    )

    def cross_backward(pieces):
        queries, keys, values, segment, source, logsum, mixed, upstream = pieces
        scores = masked_scores(queries, keys, 0.0, segment[:, None] == source[None, :])
        grad_query, grad_key, grad_value, unused = attend_back(
            scores, logsum, queries, keys, values, mixed, upstream
        )
        return (grad_query, jnp.stack((grad_key, grad_value), axis=2))

    cross_dq, cross_dkv = lax.map(
        cross_backward,
        (
            cross_q,
            cross_keys,
            cross_values,
            token_segments,
            source_segments,
            cross_lse,
            cross_mixed,
            cross_delta,
        ),
    )
    wide_query, wide_keyvalue = gather_pair(
        cross_dq.reshape(tokens, heads * DH), cross_dkv.reshape(sources, heads * 2 * DH)
    )
    crossquery_local = outer_sum(inputs_cross, wide_query)
    keyvalue_local = outer_sum(inputs_source, wide_keyvalue)
    grad_normed_cross, grad_encoder = (
        lax.psum_scatter(
            matmul_back(wide_query, cross_query).astype(jnp.bfloat16),
            "col",
            scatter_dimension=1,
            tiled=True,
        ).astype(jnp.float32),
        lax.psum_scatter(
            matmul_back(wide_keyvalue, cross_keyvalue).astype(jnp.bfloat16),
            "col",
            scatter_dimension=1,
            tiled=True,
        ).astype(jnp.float32),
    )
    back_cross, cross_gain_local = rms_back(grad_normed_cross, resid_attn, scale_cross, gain_cross)
    grad_resid_attn = grad_resid_cross + back_cross
    upstream_self = gather_features(grad_resid_attn.astype(jnp.bfloat16))
    output_local = outer_sum(heads_self, upstream_self)
    self_delta = (
        sum_heads(matmul_back(upstream_self, self_output))
        .astype(jnp.bfloat16)
        .reshape(sequences, length, heads, DH)
    )

    def self_backward(total, pieces):
        queries, keys, values, segment, logsum, mixed, upstream = pieces
        scores = masked_scores(queries, keys, position_bias, self_allowed(segment))
        grad_query, grad_key, grad_value, dscores = attend_back(
            scores, logsum, queries, keys, values, mixed, upstream
        )
        return (total + dscores, (jnp.stack((grad_query, grad_key), axis=2), grad_value))

    start_grid = jnp.zeros((heads, length, length), jnp.float32)
    grid, (grad_query_key, grad_value_rows) = lax.scan(
        self_backward,
        start_grid,
        (self_queries, self_keys, value_rows, token_segments, self_lse, self_mixed, self_delta),
    )
    table_local = bucket_grad(buckets, grid, bias_table.shape[0])
    wide_querykey, wide_value = gather_pair(
        grad_query_key.reshape(tokens, heads * 2 * DH), grad_value_rows.reshape(tokens, heads * DH)
    )
    querykey_local = outer_sum(inputs_self, wide_querykey)
    value_local = outer_sum(inputs_self, wide_value)
    grad_normed_self = sum_features(
        matmul_back(wide_querykey, self_querykey) + matmul_back(wide_value, self_value)
    )
    back_self, self_gain_local = rms_back(grad_normed_self, resid_in, scale_self, gain_self)
    grad_hidden = grad_resid_attn + back_self
    small_sums = lax.psum((self_gain_local, cross_gain_local, feed_gain_local, table_local), "dp")
    summed = tuple(
        (
            lax.psum_scatter(querykey_local, "dp", scatter_dimension=0, tiled=True),
            lax.psum_scatter(value_local, "dp", scatter_dimension=0, tiled=True),
            lax.psum_scatter(output_local, "dp", scatter_dimension=0, tiled=True),
            lax.psum_scatter(crossquery_local, "dp", scatter_dimension=0, tiled=True),
            lax.psum_scatter(keyvalue_local, "dp", scatter_dimension=0, tiled=True),
            lax.psum_scatter(crossout_local, "dp", scatter_dimension=0, tiled=True),
            lax.psum_scatter(gate_local, "dp", scatter_dimension=0, tiled=True),
            lax.psum_scatter(up_local, "dp", scatter_dimension=0, tiled=True),
            lax.psum_scatter(down_local, "dp", scatter_dimension=0, tiled=True),
        )
    )
    return (
        hidden_out,
        grad_hidden,
        grad_encoder,
        summed[0],
        summed[1],
        summed[2],
        summed[3],
        summed[4],
        summed[5],
        summed[6],
        summed[7],
        summed[8],
        small_sums[0],
        small_sums[1],
        small_sums[2],
        small_sums[3],
    )


def solution(mesh):
    placed = (
        P("dp", ("row", "col")),
        P("dp", ("row", "col")),
        P("dp", None),
        P("dp", None),
        P(),
        P(("row", "col")),
        P(("row", "col")),
        P(("row", "col")),
        P("row", "col"),
        P("row", "col"),
        P("col", "row"),
        P("row", "col"),
        P("row", "col"),
        P("col", "row"),
        P("row", "col"),
        P("row", "col"),
        P("col", "row"),
        P(None, ("col", "row")),
        P("dp", ("row", "col")),
    )
    return jax.shard_map(
        shards,
        mesh=mesh,
        in_specs=placed,
        out_specs=(
            P("dp", ("row", "col")),
            P("dp", ("row", "col")),
            P("dp", ("row", "col")),
            P(("row", "dp"), "col"),
            P(("row", "dp"), "col"),
            P(("col", "dp"), "row"),
            P(("row", "dp"), "col"),
            P(("row", "dp"), "col"),
            P(("col", "dp"), "row"),
            P(("row", "dp"), "col"),
            P(("row", "dp"), "col"),
            P(("col", "dp"), "row"),
            P(("row", "col")),
            P(("row", "col")),
            P(("row", "col")),
            P(None, ("col", "row")),
        ),
        check_vma=False,
    )
```

profile of v0, /device:TPU:0, one launch (start us, length us, event | category | flops | bytes accessed | tf_op | source)
XLA Modules:
  0.0 947.8 jit_solution(7130075582314416726)
XLA Ops:
  8.3 8.4 psum.70
  28.7 6.7 reduce-scatter.28.cloned.1.call-done
  36.4 18.8 %reduce-scatter.30.cloned.1.call-done = f32[256,384]{1,0:T(8,128)} async-done(((f32[256,768]{1,0:T(8,128)}), f32[256,384]{1,0:T(8,128)}) %reduce-scatter.30.cloned.1.call-update) | async-done | bytes 393232 | tf_op jit(solution)/shard_map/reduce_scatter | solution.py:68
  73.5 7.3 psum.71
  85.5 16.4 %reduce-scatter.34.cloned.1.call-done = f32[512,384]{1,0:T(8,128)} async-done(((f32[512,768]{1,0:T(8,128)}), f32[512,384]{1,0:T(8,128)}) %reduce-scatter.34.cloned.1.call-update) | async-done | bytes 786448 | tf_op jit(solution)/shard_map/reduce_scatter | solution.py:69
  104.1 13.8 %reduce-scatter.36.cloned.1.call-done = f32[256,192]{0,1:T(8,128)} async-done(((f32[256,384]{0,1:T(8,128)}), f32[256,192]{0,1:T(8,128)}) %reduce-scatter.36.cloned.1.call-update) | async-done | bytes 196624 | tf_op jit(solution)/shard_map/reduce_scatter | solution.py:68
  138.8 7.3 psum.72
  155.1 22.7 %reduce-scatter.42.cloned.1.call-done = f32[256,512]{1,0:T(8,128)} async-done(((f32[256,1024]{1,0:T(8,128)}), f32[256,512]{1,0:T(8,128)}) %reduce-scatter.42.cloned.1.call-update) | async-done | bytes 524304 | tf_op jit(solution)/shard_map/reduce_scatter | solution.py:69
  177.8 22.7 %reduce-scatter.40.cloned.1.call-done = f32[256,512]{1,0:T(8,128)} async-done(((f32[256,1024]{1,0:T(8,128)}), f32[256,512]{1,0:T(8,128)}) %reduce-scatter.40.cloned.1.call-update) | async-done | bytes 524304 | tf_op jit(solution)/shard_map/reduce_scatter | solution.py:68
  202.9 8.6 all_gather.56
  212.7 7.7 all_gather.57
  222.4 8.0 reduce-scatter.48.cloned.1.call-done
  231.6 7.3 psum.73
  244.7 11.2 %reduce-scatter.50.cloned.1.call-done = bf16[256,192]{0,1:T(8,128)(2,1)} async-done(((bf16[256,384]{0,1:T(8,128)(2,1)}), bf16[256,192]{0,1:T(8,128)(2,1)}) %reduce-scatter.50.cloned.1.call-update) | async-done | bytes 98320 | tf_op jit(solution)/shard_map/reduce_scatter | solution.py:61
  259.6 5.5 all_gather.59
  266.8 7.6 all_gather.54
  282.3 5.9 psum.74
  293.7 14.1 %all_gather.63 = bf16[512,768]{0,1:T(8,128)(2,1)S(1)} all-gather(bf16[512,384]{0,1:T(8,128)(2,1)S(1)} %bitcast.188), channel_id=1, replica_groups=mesh['dp'=8,'row'=2,'col'=2] {'row'}, dimensions={1}, use_global_device_ids=true | all-gather | bytes 1179648 | tf_op jit(solution)/shard_map/all_gather | solution.py:76
  315.1 5.4 all_gather.62
  320.6 6.3 all_gather.61
  351.5 6.6 while.7
  359.3 22.2 %all-reduce = (f32[192]{0:T(256)}, f32[192]{0:T(256)}, f32[192]{0:T(256)}, f32[32,3]{0,1:T(4,128)}) all-reduce(f32[192]{0:T(256)S(1)} %get-tuple-element.274, f32[192]{0:T(256)S(1)} %get-tuple-element.272, f32[192]{0:T(256)S(1)} %get-tuple-element.270, ...), channel_id=1, replica_groups=mesh['dp'=8,'row'=2,'col'=2] {'dp'}, use_global_device_ids=true, to_apply=%region_46.47 | all-reduce | flops 672 | bytes 5376 | tf_op jit(solution)/shard_map/psum | solution.py:343
  381.5 5.7 psum.75
  388.9 15.0 %reduce-scatter.68.cloned.1.call-done = f32[48,384]{1,0:T(8,128)} async-done(((f32[384,384]{1,0:T(8,128)}), f32[48,384]{1,0:T(8,128)}) %reduce-scatter.68.cloned.1.call-update) | async-done | bytes 73744 | tf_op jit(solution)/shard_map/reduce_scatter | solution.py:351
  404.0 65.5 %reduce-scatter.66.cloned.1.call-done = f32[48,384]{1,0:T(8,128)} async-done(((f32[384,384]{1,0:T(8,128)}), f32[48,384]{1,0:T(8,128)}) %reduce-scatter.66.cloned.1.call-update) | async-done | bytes 73744 | tf_op jit(solution)/shard_map/reduce_scatter | solution.py:349
  469.4 65.6 %reduce-scatter.64.cloned.1.call-done = f32[48,384]{1,0:T(8,128)} async-done(((f32[384,384]{1,0:T(8,128)}), f32[48,384]{1,0:T(8,128)}) %reduce-scatter.64.cloned.1.call-update) | async-done | bytes 73744 | tf_op jit(solution)/shard_map/reduce_scatter | solution.py:348
  535.1 68.5 %reduce-scatter.74.cloned.1.call-done = f32[128,384]{1,0:T(8,128)} async-done(((f32[1024,384]{1,0:T(8,128)}), f32[128,384]{1,0:T(8,128)}) %reduce-scatter.74.cloned.1.call-update) | async-done | bytes 196624 | tf_op jit(solution)/shard_map/reduce_scatter | solution.py:354
  603.6 68.4 %reduce-scatter.72.cloned.1.call-done = f32[48,1024]{1,0:T(8,128)} async-done(((f32[384,1024]{1,0:T(8,128)}), f32[48,1024]{1,0:T(8,128)}) %reduce-scatter.72.cloned.1.call-update) | async-done | bytes 196624 | tf_op jit(solution)/shard_map/reduce_scatter | solution.py:353
  672.0 68.4 %reduce-scatter.70.cloned.1.call-done = f32[48,1024]{1,0:T(8,128)} async-done(((f32[384,1024]{1,0:T(8,128)}), f32[48,1024]{1,0:T(8,128)}) %reduce-scatter.70.cloned.1.call-update) | async-done | bytes 196624 | tf_op jit(solution)/shard_map/reduce_scatter | solution.py:352
  740.4 65.4 %reduce-scatter.62.cloned.1.call-done = f32[48,384]{1,0:T(8,128)} async-done(((f32[384,384]{1,0:T(8,128)}), f32[48,384]{1,0:T(8,128)}) %reduce-scatter.62.cloned.1.call-update) | async-done | bytes 73744 | tf_op jit(solution)/shard_map/reduce_scatter | solution.py:347
  805.8 67.6 %reduce-scatter.76.cloned.1.call-done = f32[48,768]{1,0:T(8,128)} async-done(((f32[384,768]{1,0:T(8,128)}), f32[48,768]{1,0:T(8,128)}) %reduce-scatter.76.cloned.1.call-update) | async-done | bytes 147472
  873.4 67.9 %reduce-scatter.60.cloned.1.call-done = f32[48,768]{1,0:T(8,128)} async-done(((f32[384,768]{1,0:T(8,128)}), f32[48,768]{1,0:T(8,128)}) %reduce-scatter.60.cloned.1.call-update) | async-done | bytes 147472 | tf_op jit(solution)/shard_map/reduce_scatter | solution.py:346
  (282 shorter events, 144.0 us)
Async XLA Ops:
  7.2 145.2 %copy-start = (bf16[384,1024]{1,0:T(8,128)(2,1)S(1)}, bf16[384,1024]{1,0:T(8,128)(2,1)}, u32[]{:S(2)}) copy-start(bf16[384,1024]{1,0:T(8,128)(2,1)} %param.37) | copy-start | bytes 2359300
  7.2 28.2 %reduce-scatter.28.cloned.1.call-start = ((), (), s32[]{:S(2)}) async-start(), calls=%async_computation.25 | async-start | bytes 589824 | tf_op jit(solution)/shard_map/reduce_scatter | solution.py:69
  21.8 33.4 %reduce-scatter.30.cloned.1.call-start = ((), (), s32[]{:S(2)}) async-start(), calls=%async_computation.26 | async-start | bytes 1179648 | tf_op jit(solution)/shard_map/reduce_scatter | solution.py:68
  23.2 49.4 %reduce-scatter.32.cloned.1.call-start = ((), (), s32[]{:S(2)}) async-start(), calls=%async_computation.27 | async-start | bytes 589824 | tf_op jit(solution)/shard_map/reduce_scatter | solution.py:57
  36.3 20.8 %copy-start.49 = (bf16[256,192]{0,1:T(8,128)(2,1)}, bf16[256,192]{0,1:T(8,128)(2,1)S(1)}, u32[]{:S(2)}) copy-start(bf16[256,192]{0,1:T(8,128)(2,1)S(1)} %convert_element_type.169) | copy-start | bytes 294916
  64.6 37.4 %reduce-scatter.34.cloned.1.call-start = ((), (), s32[]{:S(2)}) async-start(), calls=%async_computation.28 | async-start | bytes 2359296 | tf_op jit(solution)/shard_map/reduce_scatter | solution.py:69
  69.3 48.6 %reduce-scatter.36.cloned.1.call-start = ((), (), s32[]{:S(2)}) async-start(), calls=%async_computation.29 | async-start | bytes 589824 | tf_op jit(solution)/shard_map/reduce_scatter | solution.py:68
  73.5 29.6 %copy-start.5 = (f32[256,192]{0,1:T(8,128)}, f32[256,192]{0,1:T(8,128)S(1)}, u32[]{:S(2)}) copy-start(f32[256,192]{0,1:T(8,128)S(1)} %get-tuple-element.301) | copy-start | bytes 589828
  84.7 52.4 %reduce-scatter.38.cloned.1.call-start = ((), (), s32[]{:S(2)}) async-start(), calls=%async_computation.30 | async-start | bytes 589824 | tf_op jit(solution)/shard_map/reduce_scatter | solution.py:57
  129.1 17.0 %copy-start.56 = (f32[192]{0:T(256)S(1)}, f32[192]{0:T(256)}, u32[]{:S(2)}) copy-start(f32[192]{0:T(256)} %param.30) | copy-start | bytes 2308
  129.1 26.0 %reduce-scatter.46.cloned.1.call-start = ((), (), s32[]{:S(2)}) async-start(), calls=%async_computation.34 | async-start | bytes 786432 | tf_op jit(solution)/shard_map/reduce_scatter | solution.py:61
  134.4 43.3 %reduce-scatter.42.cloned.1.call-start = ((), (), s32[]{:S(2)}) async-start(), calls=%async_computation.32 | async-start | bytes 1572864 | tf_op jit(solution)/shard_map/reduce_scatter | solution.py:69
  152.3 48.1 %reduce-scatter.40.cloned.1.call-start = ((), (), s32[]{:S(2)}) async-start(), calls=%async_computation.31 | async-start | bytes 1572864 | tf_op jit(solution)/shard_map/reduce_scatter | solution.py:68
  154.8 75.6 %reduce-scatter.48.cloned.1.call-start = ((), (), s32[]{:S(2)}) async-start(), calls=%async_computation.35 | async-start | bytes 589824 | tf_op jit(solution)/shard_map/reduce_scatter | solution.py:57
  202.9 18.3 %copy-start.20 = (bf16[384,1024]{1,0:T(8,128)(2,1)S(1)}, bf16[384,1024]{1,0:T(8,128)(2,1)}, u32[]{:S(2)}) copy-start(bf16[384,1024]{1,0:T(8,128)(2,1)} %param.38) | copy-start | bytes 2359300
  222.4 33.4 %reduce-scatter.50.cloned.1.call-start = ((), (), s32[]{:S(2)}) async-start(), calls=%async_computation.36 | async-start | bytes 294912 | tf_op jit(solution)/shard_map/reduce_scatter | solution.py:61
  244.6 35.9 %reduce-scatter.52.cloned.1.call-start = ((), (), s32[]{:S(2)}) async-start(), calls=%async_computation.37 | async-start | bytes 294912 | tf_op jit(solution)/shard_map/reduce_scatter | solution.py:295
  266.7 21.5 %reduce-scatter.44.cloned.1.call-start = ((), (), s32[]{:S(2)}) async-start(), calls=%async_computation.33 | async-start | bytes 589824 | tf_op jit(solution)/shard_map/reduce_scatter | solution.py:57
  277.5 33.6 %reduce-scatter.54.cloned.1.call-start = ((), (), s32[]{:S(2)}) async-start(), calls=%async_computation.38 | async-start | bytes 294912 | tf_op jit(solution)/shard_map/reduce_scatter | solution.py:61
  293.7 56.1 %reduce-scatter.58.cloned.1.call-start = ((), (), s32[]{:S(2)}) async-start(), calls=%async_computation.40 | async-start | bytes 589824 | tf_op jit(solution)/shard_map/reduce_scatter | solution.py:301
  293.7 17.4 %copy-start.52 = (bf16[3,64,256]{2,1,0:T(8,128)(2,1)S(1)}, bf16[3,64,256]{2,1,0:T(8,128)(2,1)}, u32[]{:S(2)}) copy-start(bf16[3,64,256]{2,1,0:T(8,128)(2,1)} %copy-done.51) | copy-start | bytes 294916
  311.1 47.1 %reduce-scatter.56.cloned.1.call-start = ((), (), s32[]{:S(2)}) async-start(), calls=%async_computation.39 | async-start | bytes 589824 | tf_op jit(solution)/shard_map/reduce_scatter | solution.py:57
  328.3 75.7 %reduce-scatter.68.cloned.1.call-start = ((), (), s32[]{:S(2)}) async-start(), calls=%async_computation.45 | async-start | bytes 663552 | tf_op jit(solution)/shard_map/reduce_scatter | solution.py:351
  329.6 139.8 %reduce-scatter.66.cloned.1.call-start = ((), (), s32[]{:S(2)}) async-start(), calls=%async_computation.44 | async-start | bytes 663552 | tf_op jit(solution)/shard_map/reduce_scatter | solution.py:349
  331.9 203.2 %reduce-scatter.64.cloned.1.call-start = ((), (), s32[]{:S(2)}) async-start(), calls=%async_computation.43 | async-start | bytes 663552 | tf_op jit(solution)/shard_map/reduce_scatter | solution.py:348
  334.0 269.6 %reduce-scatter.74.cloned.1.call-start = ((), (), s32[]{:S(2)}) async-start(), calls=%async_computation.48 | async-start | bytes 1769472 | tf_op jit(solution)/shard_map/reduce_scatter | solution.py:354
  335.7 336.3 %reduce-scatter.72.cloned.1.call-start = ((), (), s32[]{:S(2)}) async-start(), calls=%async_computation.47 | async-start | bytes 1769472 | tf_op jit(solution)/shard_map/reduce_scatter | solution.py:353
  338.5 401.9 %reduce-scatter.70.cloned.1.call-start = ((), (), s32[]{:S(2)}) async-start(), calls=%async_computation.46 | async-start | bytes 1769472 | tf_op jit(solution)/shard_map/reduce_scatter | solution.py:352
  340.1 465.8 %reduce-scatter.62.cloned.1.call-start = ((), (), s32[]{:S(2)}) async-start(), calls=%async_computation.42 | async-start | bytes 663552 | tf_op jit(solution)/shard_map/reduce_scatter | solution.py:347
  341.3 532.2 %reduce-scatter.76.cloned.1.call-start = ((), (), s32[]{:S(2)}) async-start(), calls=%async_computation.49 | async-start | bytes 1327104
  346.8 594.5 %reduce-scatter.60.cloned.1.call-start = ((), (), s32[]{:S(2)}) async-start(), calls=%async_computation.41 | async-start | bytes 1327104 | tf_op jit(solution)/shard_map/reduce_scatter | solution.py:346
  351.5 35.7 %copy-start.53 = (f32[256,192]{0,1:T(8,128)S(1)}, f32[256,192]{0,1:T(8,128)}, u32[]{:S(2)}) copy-start(f32[256,192]{0,1:T(8,128)} %get-tuple-element.297) | copy-start | bytes 589828
  (55 other events, 251.8 us)
Sparse Core Ops, SparseCore 0:
  21.9 13.4 reduce-scatter.27
  37.6 17.4 reduce-scatter.29
  64.7 7.7 reduce-scatter.31
  74.7 27.2 reduce-scatter.33
  104.6 13.1 reduce-scatter.35
  129.3 7.7 reduce-scatter.37
  139.3 15.7 reduce-scatter.45
  157.3 20.3 reduce-scatter.41
  180.0 20.3 reduce-scatter.39
  222.5 7.8 reduce-scatter.47
  244.7 11.0 reduce-scatter.49
  266.9 7.6 reduce-scatter.51
  277.7 8.6 reduce-scatter.43
  293.8 13.2 reduce-scatter.53
  311.2 7.8 reduce-scatter.57
  328.4 7.8 reduce-scatter.55
  340.0 63.8 reduce-scatter.67
  407.7 61.6 reduce-scatter.65
  473.3 61.7 reduce-scatter.63
  538.9 64.5 reduce-scatter.73
  607.6 64.3 reduce-scatter.71
  676.0 64.3 reduce-scatter.69
  744.3 61.5 reduce-scatter.61
  809.6 63.7 reduce-scatter.75
  877.4 63.8 reduce-scatter.59
where the time goes:
time: 949 us; the launch traced here: 948 us
  waiting for transfers between devices  679 us (72%)
  blocking collectives  144 us (15%)
  matrix products  63.3 us (7%)
  other arithmetic  25.9 us (3%)
  local copies, waits for them, and re-layouts  19.9 us (2%)
  between operations  14.9 us (2%)
    reduce_scatter x1, waiting for transfers between devices, shards(): lax.psum_scatter(down_local, 'dp', scatter_dimension=0, tiled=True)  68.5 us
    reduce_scatter x1, waiting for transfers between devices, shards(): lax.psum_scatter(up_local, 'dp', scatter_dimension=0, tiled=True)  68.4 us
    reduce_scatter x1, waiting for transfers between devices, shards(): lax.psum_scatter(gate_local, 'dp', scatter_dimension=0, tiled=True)  68.4 us
    unnamed x26, waiting for transfers between devices  68 us
    reduce_scatter x1, waiting for transfers between devices, shards(): lax.psum_scatter(querykey_local, 'dp', scatter_dimension=0, tiled=True)  67.9 us
    reduce_scatter x1, waiting for transfers between devices, shards(): lax.psum_scatter(output_local, 'dp', scatter_dimension=0, tiled=True)  65.6 us
    reduce_scatter x1, waiting for transfers between devices, shards(): lax.psum_scatter(crossquery_local, 'dp', scatter_dimension=0, tiled=True)  65.5 us
    reduce_scatter x1, waiting for transfers between devices, shards(): lax.psum_scatter(value_local, 'dp', scatter_dimension=0, tiled=True)  65.4 us
  transfers between devices with their start and end apart: 25, of which 20 were waited for; matrix products, arithmetic and copies ran while one was open for 7% of the time, Pallas kernels for 0%

commit v1 on v0

v1 whole, which is shorter than its diff:
```python
import jax
import jax.numpy as jnp
from jax import lax
from jax.experimental import pallas as pl
from jax.experimental.pallas import tpu as pltpu
from jax.sharding import PartitionSpec as P


BF = jnp.bfloat16
F32 = jnp.float32
EPS = 1e-06
ROOT = 0.7978845608028654
CUBIC = 0.044715
MASKED = -1e30
SWAP = [(0, 1), (1, 0)]


def nn(left, right):
    return jnp.dot(left, right, preferred_element_type=F32)


def nt(left, right):
    return lax.dot_general(left, right, (((1,), (1,)), ((), ())), preferred_element_type=F32)


def tn(left, right):
    return lax.dot_general(left, right, (((0,), (0,)), ((), ())), preferred_element_type=F32)


def call(kernel, outs, *args):
    flat = [jax.ShapeDtypeStruct(shape, dtype) for shape, dtype in outs]
    space = pl.BlockSpec(memory_space=pltpu.VMEM)
    return pl.pallas_call(
        kernel,
        out_shape=flat,
        in_specs=[space] * len(args),
        out_specs=[space] * len(flat),
        compiler_params=pltpu.CompilerParams(vmem_limit_bytes=60 * 1024 * 1024),
    )(*args)


def row_swap(values):
    return lax.ppermute(values, "row", SWAP)


def col_swap(values):
    return lax.ppermute(values, "col", SWAP)


def own_rows(ref, base=0):
    half = 128
    start = base + lax.axis_index("col") * half
    return ref[pl.ds(pl.multiple_of(start, 16), half), :]


def each_side(axis, body):
    index = lax.axis_index(axis)
    for side in (0, 1):
        pl.when(index == side)(lambda side=side: body(side))


def swapped(ref, left, right):
    width = left.shape[1]
    ref[:, :width] = right.astype(BF)
    ref[:, width:] = left.astype(BF)


def each_replica(body):
    for part in range(4):
        pl.when(lax.axis_index("dp") % 4 == part)(lambda part=part: body(part))


def weight_parts(keep_body, send_body):
    def of_row(side):
        keep_body(side)
        each_replica(lambda part: send_body(1 - side, part))

    each_side("row", of_row)


def keep_cols(src, keep, at, width, side):
    keep[:, at : at + width] = src[:, side * width : (side + 1) * width]


def send_cols(src, send, at, width, side, part):
    rows = src.shape[0] // 4
    send[:, at : at + width] = src[
        part * rows : (part + 1) * rows, side * width : (side + 1) * width
    ]


def keep_out(src, keep, at, side):
    rows = src.shape[0] // 2
    width = src.shape[1] // 2
    for block in (0, 1):
        keep[block * rows : (block + 1) * rows, at : at + width] = src[
            side * rows : (side + 1) * rows, block * width : (block + 1) * width
        ]


def send_out(src, send, at, side, part):
    rows = src.shape[0] // 4
    width = src.shape[1] // 2
    start = side * 2 * rows + part % 2 * rows
    send[:, at : at + width] = src[
        start : start + rows, part // 2 * width : (part // 2 + 1) * width
    ]


def join_parts(parts, out):
    rows = parts[0].shape[0]
    place = lax.axis_index("dp") % 4
    for away, part in enumerate(parts):
        start = jnp.bitwise_xor(place, away) * rows
        out[pl.ds(pl.multiple_of(start, 16), rows), :] = part[...]


def assemble(own, recv, own_peer, recv_peer):
    core = lax.axis_index("col")
    first = core == 0
    quarters = (
        jnp.where(first, own[...], own_peer[...]),
        jnp.where(first, own_peer[...], own[...]),
        jnp.where(first, recv[...], recv_peer[...]),
        jnp.where(first, recv_peer[...], recv[...]),
    )
    return jnp.concatenate(quarters, axis=0)


def pack_three(wide, narrow, out, keep, send):
    def keep_body(side):
        keep_cols(wide, keep, 0, 384, side)
        keep_cols(narrow, keep, 384, 192, side)
        keep_out(out, keep, 576, side)

    def send_body(side, part):
        send_cols(wide, send, 0, 384, side, part)
        send_cols(narrow, send, 384, 192, side, part)
        send_out(out, send, 576, side, part)

    weight_parts(keep_body, send_body)


def prep_self(hidden, gs, gc, gf, qk, v, wo, packed, keep, send):
    tokens = hidden.shape[1]
    packed[:, :tokens] = hidden[...]
    gains = jnp.concatenate([gs[...], gc[...], gf[...]], axis=0)
    high = gains.astype(BF)
    low = (gains - high.astype(F32)).astype(BF)
    rows = jnp.concatenate(
        [high.astype(F32), low.astype(F32), jnp.zeros((10, gains.shape[1]), F32)], axis=0
    ).astype(BF)
    line = lax.broadcasted_iota(jnp.int32, (16, 16), 0)
    place = lax.broadcasted_iota(jnp.int32, (16, 16), 1)
    packed[:, tokens:] = tn(rows, jnp.where(line == place, 1.0, 0.0).astype(BF)).astype(BF)

    pack_three(qk, v, wo, keep, send)


def prep_cross(enc, cot, q, kv, wo, packed, keep, send):
    packed[:, : enc.shape[1]] = enc[...]
    packed[:, enc.shape[1] :] = cot[...]

    pack_three(kv, q, wo, keep, send)


def prep_feed(gate, up, down, keep, send, keep_down, send_down):
    def keep_body(side):
        keep_cols(gate, keep, 0, 512, side)
        keep_cols(up, keep, 512, 512, side)
        keep_down[...] = down[side * 512 : (side + 1) * 512, :]

    def send_body(side, part):
        send_cols(gate, send, 0, 512, side, part)
        send_cols(up, send, 512, 512, side, part)
        at = side * 512 + part * 128
        send_down[...] = down[at : at + 128, :]

    weight_parts(keep_body, send_body)


def masks(buckets, table, peer_table, segment, source, bias_out, cross_out):
    core = lax.axis_index("col")
    ids = own_rows(buckets)
    rows, cols = ids.shape
    line = lax.broadcasted_iota(jnp.int32, (rows, cols), 0) + core * rows
    place = lax.broadcasted_iota(jnp.int32, (rows, cols), 1)
    keys = segment[...]
    mine = jnp.sum(
        jnp.where(place == line, jnp.broadcast_to(keys, (rows, cols)).astype(F32), 0.0),
        axis=1,
        keepdims=True,
    )
    allowed = (place <= line) & (keys.astype(F32) == mine)
    for head in range(6):
        ref = table if head < 3 else peer_table
        entries = jnp.broadcast_to(ref[head % 3 : head % 3 + 1, :], (rows, 128))
        parts = [
            jnp.take_along_axis(
                entries, ids[:, at : at + 128], axis=1, mode="promise_in_bounds"
            )
            for at in range(0, cols, 128)
        ]
        bias_out[head] = jnp.where(allowed, jnp.concatenate(parts, axis=1), MASKED)
    cross_out[...] = jnp.where(source[...].astype(F32) == mine, 0.0, MASKED)


def gain_row(gains, which):
    return gains[which : which + 1, :]


def norm(resid, gain):
    scale = lax.rsqrt(jnp.mean(resid * resid, axis=1, keepdims=True) + EPS)
    return resid * scale * gain, scale


def norm_back(upstream, resid, gain):
    scale = lax.rsqrt(jnp.mean(resid * resid, axis=1, keepdims=True) + EPS)
    normed = resid * scale
    scaled = upstream * gain
    grad = scale * (scaled - normed * jnp.mean(scaled * normed, axis=1, keepdims=True))
    return grad, jnp.sum(upstream * normed, axis=0, keepdims=True)


def project(left, top, bottom, at, width):
    return nn(left[:, :384], top[:, at : at + width]) + nn(left[:, 384:], bottom[:, at : at + width])


def softmax(scores):
    top = jnp.max(scores, axis=1, keepdims=True)
    weights = jnp.exp(scores - top)
    total = jnp.sum(weights, axis=1, keepdims=True)
    return (weights * (1.0 / total)).astype(BF), top + jnp.log(total)


def out_project(mixed, a0, a1, b0, b1, keep, send):
    first, second = mixed[:, :192], mixed[:, 192:]
    parts = []
    for a, b in ((a0, b0), (a1, b1)):
        for block in (0, 1):
            lines = slice(block * 192, (block + 1) * 192)
            parts.append(nn(first, a[lines, 576:]) + nn(second, b[lines, 576:]))
    mine = jnp.concatenate(parts[:2], axis=1)
    theirs = jnp.concatenate(parts[2:], axis=1)
    keep[:, :384] = mine
    keep[:, 384:] = theirs
    swapped(send, mine, theirs)


def out_back(upstream, w0, w1):
    total = None
    for half, w in ((0, w0), (1, w1)):
        for block in (0, 1):
            at = half * 384 + block * 192
            term = nt(upstream[:, at : at + 192], w[block * 192 : (block + 1) * 192, 576:])
            total = term if total is None else total + term
    return total


def self_forward(
    own, recv, own_peer, recv_peer, a0, b0, p0, p1, p2, p3, q0, q1, q2, q3, bias, x_out, gains_out, a1, b1, normed_out, ya, yb, mixed_out, lse_out, keep, send,
):
    join_parts((p0, p1, p2, p3), a1)
    join_parts((q0, q1, q2, q3), b1)
    tokens = normed_out.shape[0]
    whole = assemble(own, recv, own_peer, recv_peer).astype(F32)
    resid = jnp.transpose(whole[:, :tokens])
    x_out[...] = resid.astype(BF)
    parts = whole[:, tokens:].astype(BF)
    line = lax.broadcasted_iota(jnp.int32, (16, 16), 0)
    place = lax.broadcasted_iota(jnp.int32, (16, 16), 1)
    chosen = (line == place) | ((line == place - 3) & (place < 6))
    chosen = jnp.where(chosen & (line < 3), 1.0, 0.0).astype(BF)
    gains_out[...] = nt(chosen, parts)
    normed = norm(resid, gain_row(gains_out, 0))[0].astype(BF)
    normed_out[...] = normed
    ya[...] = project(normed, a0, a1, 0, 576).astype(BF)
    yb[...] = project(normed, b0, b1, 0, 576).astype(BF)
    mixed = []
    for head in range(6):
        y = ya if head < 3 else yb
        at = (head % 3) * 128
        mine = own_rows(y)
        scores = nt(mine[:, at : at + 64], y[:, at + 64 : at + 128]) + bias[head]
        probs, lse = softmax(scores)
        lse_out[head] = lse
        at = 384 + (head % 3) * 64
        mixed.append(nn(probs, y[:, at : at + 64]))
    mixed = jnp.concatenate(mixed, axis=1).astype(BF)
    mixed_out[...] = mixed
    out_project(mixed, a0, a1, b0, b1, keep, send)


def encode_keys(
    own, recv, own_peer, recv_peer, a0, b0, p0, p1, p2, p3, q0, q1, q2, q3, ec, a1, b1, kva, kvb,
):
    join_parts((p0, p1, p2, p3), a1)
    join_parts((q0, q1, q2, q3), b1)
    rows = kva.shape[0]
    whole = assemble(own, recv, own_peer, recv_peer).astype(F32)
    ec[...] = jnp.transpose(whole).astype(BF)
    enc = ec[:rows, :]
    kva[...] = project(enc, a0, a1, 0, 384).astype(BF)
    kvb[...] = project(enc, b0, b1, 0, 384).astype(BF)


def cross_forward(
    xg, gains, part, recv, a0, a1, b0, b1, kva, kvb, mask, resid_out, normed_out, q_out, mixed_out,
    lse_out, keep, send,
):
    resid = own_rows(xg).astype(F32) + part[...] + recv[...].astype(F32)
    resid_out[...] = resid
    normed = norm(resid, gain_row(gains, 1))[0].astype(BF)
    normed_out[...] = normed
    queries = jnp.concatenate(
        [project(normed, a0, a1, 384, 192), project(normed, b0, b1, 384, 192)], axis=1
    ).astype(BF)
    q_out[...] = queries
    mixed = []
    for head in range(6):
        kv = kva if head < 3 else kvb
        at = (head % 3) * 128
        scores = nt(queries[:, head * 64 : head * 64 + 64], kv[:, at : at + 64]) + mask[...]
        probs, lse = softmax(scores)
        lse_out[head] = lse
        mixed.append(nn(probs, kv[:, at + 64 : at + 128]))
    mixed = jnp.concatenate(mixed, axis=1).astype(BF)
    mixed_out[...] = mixed
    out_project(mixed, a0, a1, b0, b1, keep, send)


def feed_upstream(ec, da0, db0, *refs):
    parts, (fa1, fb1, da1, db1, out) = refs[:16], refs[16:]
    for at, ref in enumerate((fa1, fb1, da1, db1)):
        join_parts(parts[at * 4 : at * 4 + 4], ref)
    cot = own_rows(ec, ec.shape[0] - 256)
    out[:, :512] = nt(cot[:, :384], da0[...]) + nt(cot[:, 384:], da1[...])
    out[:, 512:] = nt(cot[:, :384], db0[...]) + nt(cot[:, 384:], db1[...])


def feed_forward(
    xg, gains, prior, part, recv, fa0, fa1, fb0, fb1, upstream, resid_out, normed_out, hidden_out,
    gate_out, up_out, keep, send,
):
    resid = prior[...] + part[...] + recv[...].astype(F32)
    resid_out[...] = resid
    normed = norm(resid, gain_row(gains, 2))[0].astype(BF)
    normed_out[...] = normed
    deltas = []
    for side, (w0, w1) in enumerate(((fa0, fa1), (fb0, fb1))):
        lanes = slice(side * 512, side * 512 + 512)
        gate = project(normed, w0, w1, 0, 512)
        up = project(normed, w0, w1, 512, 512)
        inner = jnp.tanh(ROOT * (gate + CUBIC * gate * gate * gate))
        gelu = 0.5 * gate * (1.0 + inner)
        slope = 0.5 * (1.0 + inner) + 0.5 * gate * (1.0 - inner * inner) * ROOT * (
            1.0 + 3.0 * CUBIC * gate * gate
        )
        grad = upstream[:, lanes]
        hidden_out[:, lanes] = (gelu * up).astype(BF)
        gate_delta = (grad * up * slope).astype(BF)
        up_delta = (grad * gelu).astype(BF)
        gate_out[:, lanes] = gate_delta
        up_out[:, lanes] = up_delta
        deltas.append((gate_delta, up_delta))
    (ga, ua), (gb, ub) = deltas
    mine = nt(ga, fa0[:, :512]) + nt(ua, fa0[:, 512:]) + nt(gb, fb0[:, :512]) + nt(ub, fb0[:, 512:])
    theirs = (
        nt(ga, fa1[:, :512]) + nt(ua, fa1[:, 512:]) + nt(gb, fb1[:, :512]) + nt(ub, fb1[:, 512:])
    )
    keep[:, :384] = mine
    keep[:, 384:] = theirs
    swapped(send, mine, theirs)


def feed_grads(normed, gate, up, in_keep, in_send):
    left = normed[...]
    for ref, lanes in ((in_send, slice(512, 1024)), (in_keep, slice(0, 512))):
        ref[:, :512] = tn(left, gate[:, lanes]).astype(BF)
        ref[:, 512:] = tn(left, up[:, lanes]).astype(BF)


def feed_out(hidden, ec, resid, da0, da1, db0, db1, out_keep, out_send, last_keep, last_send):
    cot = own_rows(ec, ec.shape[0] - 256)
    out_send[...] = tn(hidden[:, 512:], cot).astype(BF)
    out_keep[...] = tn(hidden[:, :512], cot).astype(BF)
    last_send[...] = (nn(hidden[:, :512], da1[...]) + nn(hidden[:, 512:], db1[...])).astype(BF)
    last_keep[...] = (
        nn(hidden[:, :512], da0[...]) + nn(hidden[:, 512:], db0[...]) + resid[:, :384]
    )


def last_out(part, recv, keep, send):
    total = jnp.transpose(part[...] + recv[...].astype(F32)).astype(BF)

    def body(side):
        keep[...] = total[side * 192 : side * 192 + 192, :]
        send[...] = total[(1 - side) * 192 : (2 - side) * 192, :]

    each_side("col", body)


def store_grads(ref, left, wide, narrow, narrow_left):
    ref[:768, :] = tn(left, wide).astype(BF)
    thin = tn(narrow_left, narrow).astype(BF)
    ref[768:, :192] = thin[:384, :]
    ref[768:, 192:] = thin[384:, :]


def cross_backward(
    xg, gains, ec, part, recv, resid_in, a0, a1, b0, b1, q, kva, kvb, lse, mask, mixed, resid_out,
    upstream_out, gain_out, delta_out, dscores_out, probs_out, dq_out, keep, send,
):
    back, gain = norm_back(part[...] + recv[...].astype(F32), resid_in[...], gain_row(gains, 2))
    gain_out[...] = jnp.broadcast_to(gain, gain_out.shape)
    resid = own_rows(ec, ec.shape[0] - 256).astype(F32) + back
    resid_out[...] = resid
    upstream = resid.astype(BF)
    upstream_out[...] = upstream
    delta = jnp.concatenate(
        [out_back(upstream, a0, a1), out_back(upstream, b0, b1)], axis=1
    ).astype(BF)
    delta_out[...] = delta
    grads = []
    for head in range(6):
        kv = kva if head < 3 else kvb
        at = (head % 3) * 128
        lanes = slice(head * 64, head * 64 + 64)
        scores = nt(q[:, lanes], kv[:, at : at + 64]) + mask[...]
        probs = jnp.exp(scores - lse[head])
        probs_out[head] = probs.astype(BF)
        drift = nt(delta[:, lanes], kv[:, at + 64 : at + 128])
        centre = jnp.sum(
            delta[:, lanes].astype(F32) * mixed[:, lanes].astype(F32), axis=1, keepdims=True
        )
        low = (probs * (drift - centre)).astype(BF)
        dscores_out[head] = low
        grads.append(nn(low, kv[:, at : at + 64]))
    grads = jnp.concatenate(grads, axis=1).astype(BF)
    dq_out[...] = grads
    first, second = grads[:, :192], grads[:, 192:]
    mine = nt(first, a0[:, 384:576]) + nt(second, b0[:, 384:576])
    theirs = nt(first, a1[:, 384:576]) + nt(second, b1[:, 384:576])
    keep[:, :384] = mine
    keep[:, 384:] = theirs
    swapped(send, mine, theirs)


def cross_grads(
    ec, normed, q, delta, dscores, probs, dq, mixed, upstream, a0, a1, b0, b1, in_keep, in_send,
    out_keep, out_send, enc_keep, enc_send,
):
    rows = ec.shape[0] - 256
    enc = ec[:rows, :]
    left = normed[...]
    both = []
    for first in (0, 3):
        parts = []
        for head in range(first, first + 3):
            lanes = slice(head * 64, head * 64 + 64)
            parts.append(tn(dscores[head], q[:, lanes]))
            parts.append(tn(probs[head], delta[:, lanes]))
        both.append(jnp.concatenate(parts, axis=1).astype(BF))
    for ref, side in ((in_send, 1), (in_keep, 0)):
        store_grads(ref, enc, both[side], dq[:, side * 192 : side * 192 + 192], left)
    out_send[...] = tn(mixed[:, 192:], upstream[...]).astype(BF)
    out_keep[...] = tn(mixed[:, :192], upstream[...]).astype(BF)
    for half, (a, b) in enumerate(((a0, b0), (a1, b1))):
        total = nt(a[:, :384], both[0]) + nt(b[:, :384], both[1])

        def body(side, half=half, total=total):
            enc_keep[half] = total[side * 192 : side * 192 + 192, :]
            enc_send[half] = total[(1 - side) * 192 : (2 - side) * 192, :].astype(BF)

        each_side("col", body)


def self_backward(
    xg, gains, part, recv, upper, resid_in, a0, a1, b0, b1, normed, ya, yb, bias, lse, mixed, resid_out,
    gain_out, dscores_out, dya, dyb, in_keep, in_send, out_keep, out_send,
):
    back, gain = norm_back(part[...] + recv[...].astype(F32), resid_in[...], gain_row(gains, 1))
    gain_out[...] = jnp.broadcast_to(gain, gain_out.shape)
    resid = upper[...] + back
    resid_out[...] = resid
    upstream = resid.astype(BF)
    delta = jnp.concatenate(
        [out_back(upstream, a0, a1), out_back(upstream, b0, b1)], axis=1
    ).astype(BF)
    out_send[...] = tn(mixed[:, 192:], upstream).astype(BF)
    out_keep[...] = tn(mixed[:, :192], upstream).astype(BF)
    core = lax.axis_index("col").astype(F32)
    for y, dy, first in ((yb, dyb, 3), (ya, dya, 0)):
        mine = own_rows(y)
        pairs, values = [], []
        for head in range(first, first + 3):
            at = (head % 3) * 128
            vat = 384 + (head % 3) * 64
            lanes = slice(head * 64, head * 64 + 64)
            queries = mine[:, at : at + 64]
            scores = nt(queries, y[:, at + 64 : at + 128]) + bias[head]
            probs = jnp.exp(scores - lse[head])
            up = delta[:, lanes]
            drift = nt(up, y[:, vat : vat + 64])
            centre = jnp.sum(
                up.astype(F32) * mixed[:, lanes].astype(F32), axis=1, keepdims=True
            )
            dscores = probs * (drift - centre)
            dscores_out[head] = dscores
            low = dscores.astype(BF)
            dq = nn(low, y[:, at + 64 : at + 128])
            dq = jnp.concatenate([dq * (1.0 - core), dq * core], axis=0)
            pairs.append(jnp.concatenate([dq, tn(low, queries)], axis=1))
            values.append(tn(probs.astype(BF), up))
        dy[...] = jnp.concatenate(pairs + values, axis=1).astype(BF)
    left = normed[...]
    for ref, dy in ((in_send, dyb), (in_keep, dya)):
        store_grads(ref, left, dy[:, :384], dy[:, 384:], left)


def self_inputs(dya, dyb, a0, a1, b0, b1, keep, send):
    da, db = dya[...], dyb[...]
    totals = [nt(da, a[:, :576]) + nt(db, b[:, :576]) for a, b in ((a0, b0), (a1, b1))]

    def body(side):
        mine = slice(side * 128, side * 128 + 128)
        theirs = slice((1 - side) * 128, (1 - side) * 128 + 128)
        for at, total in ((0, totals[0]), (384, totals[1])):
            keep[:, at : at + 384] = total[mine, :]
            send[:, at : at + 384] = total[theirs, :].astype(BF)

    each_side("col", body)


def self_sum(part, other, keep, send):
    total = part[...] + other[...].astype(F32)
    keep[...] = total
    swapped(send, total[:, :384], total[:, 384:])


def table_sums(buckets, dscores, out):
    ids = own_rows(buckets)
    totals = []
    for head in range(6):
        grid = dscores[head]
        sums = []
        for label in range(32):
            chosen = jnp.where(ids == label, grid, 0.0)
            sums.append(jnp.sum(chosen, axis=0, keepdims=True))
        totals.append(jnp.sum(jnp.concatenate(sums, axis=0), axis=1, keepdims=True))
    place = lax.broadcasted_iota(jnp.int32, (32, 128), 1)
    for side in (0, 1):
        table = jnp.zeros((32, 128), F32)
        for head in range(3):
            table = jnp.where(place == head, totals[side * 3 + head], table)
        out[side] = table


def last_norm(
    xg, gains, part, recv, upper, gain_feed, gain_cross, tables, keep, send, small_keep,
    small_send,
):
    resid = own_rows(xg).astype(F32)
    back, gain = norm_back(part[...] + recv[...].astype(F32), resid, gain_row(gains, 0))
    total = jnp.transpose((upper[...] + back)[:, :384])

    def body(side):
        keep[...] = total[side * 192 : side * 192 + 192, :]
        send[...] = total[(1 - side) * 192 : (2 - side) * 192, :]

    each_side("col", body)
    rows = []
    for values in (gain, gain_cross[:1, :], gain_feed[:1, :]):
        rows += [values[:, at : at + 128] for at in (0, 128, 256)]
    rows = jnp.concatenate(rows + [jnp.zeros((7, 128), F32)], axis=0)
    small_keep[:16, :] = rows
    small_send[:16, :] = rows
    small_keep[16:, :] = tables[0]
    small_send[16:, :] = tables[1]


def finish_early(feed_keep, feed_recv, cross_keep, cross_recv, mine, send):
    for half, ref in ((0, mine), (1, send)):
        feed = feed_keep[half].astype(F32) + feed_recv[half].astype(F32)
        wide = cross_keep[half].astype(F32) + cross_recv[half].astype(F32)
        thin = cross_keep[2].astype(F32) + cross_recv[2].astype(F32)
        ref[:, :1024] = feed.astype(ref.dtype)
        ref[:, 1024:1408] = wide.astype(ref.dtype)
        ref[:, 1408:] = thin[:, half * 192 : half * 192 + 192].astype(ref.dtype)


def finish_self(keep, recv, mine, send):
    for half, ref in ((0, mine), (1, send)):
        wide = keep[half].astype(F32) + recv[half].astype(F32)
        thin = keep[2].astype(F32) + recv[2].astype(F32)
        ref[:, :384] = wide.astype(ref.dtype)
        ref[:, 384:] = thin[:, half * 192 : half * 192 + 192].astype(ref.dtype)


def place_columns(widths, mine, recv, *outs):
    def body(side):
        at = 0
        for width, out in zip(widths, outs):
            first = mine[:, at : at + width]
            second = recv[:, at : at + width].astype(F32)
            if side:
                first, second = second, first
            out[:, :width] = first
            out[:, width:] = second
            at += width

    each_side("row", body)


def place_early(mine, recv, *outs):
    place_columns((512, 512, 384, 192), mine, recv, *outs)


def place_self(mine, recv, *outs):
    place_columns((384, 192), mine, recv, *outs)


def finish_out(feed_keep, feed_recv, rest_keep, rest_recv, first, second):
    total = jnp.concatenate(
        [
            feed_keep[...].astype(F32) + feed_recv[...].astype(F32),
            rest_keep[...].astype(F32) + rest_recv[...].astype(F32),
        ],
        axis=0,
    ).astype(BF)
    swap = (lax.axis_index("dp") + lax.axis_index("row")) % 2

    def body(side):
        for ref, half in ((first, side), (second, 1 - side)):
            ref[...] = total[:, half * 384 : half * 384 + 384]

    for side in (0, 1):
        pl.when(swap == side)(lambda side=side: body(side))


def place_rows(first, second, *outs):
    def body(side):
        at = 0
        for out in outs:
            size = out.shape[0] // 2
            parts = [ref[at : at + size, :].astype(F32) for ref in (first, second)]
            if side:
                parts = parts[::-1]
            out[:size, :] = parts[0]
            out[size:, :] = parts[1]
            at += size

    each_side("row", body)


def build(replicas):
    bits = replicas.bit_length() - 1
    assert 1 << bits == replicas and replicas % 2 == 0

    def replica_swap(values, bit):
        return lax.ppermute(values, "dp", [(i, i ^ (1 << bit)) for i in range(replicas)])

    def scatter(values, axis, order):
        place = lax.axis_index("dp")
        shape = values.shape
        values = values.reshape(shape[:axis] + (2,) * bits + shape[axis + 1 :])
        left = list(range(bits - 1, -1, -1))
        for bit in order:
            at = axis + left.index(bit)
            left.remove(bit)
            mine = (place >> bit) & 1
            keep = lax.dynamic_index_in_dim(values, mine, at, keepdims=False)
            send = lax.dynamic_index_in_dim(values, 1 - mine, at, keepdims=False)
            recv = replica_swap(send, bit)
            values = (keep.astype(F32) + recv.astype(F32)).astype(BF)
        return keep, recv

    def spread(values):
        direct = row_swap(values)
        beside = replica_swap(direct, 0)
        parts = (direct, beside, replica_swap(direct, 1), replica_swap(beside, 1))
        return parts, tuple(col_swap(part) for part in parts)

    def core_sum(keep, send):
        return (keep.astype(F32) + col_swap(send).astype(F32)).astype(BF)

    def layer(
        hidden_in, encoder_states, token_segments, source_segments, buckets, gain_self, gain_cross,
        gain_feed, self_querykey, self_value, self_output, cross_query, cross_keyvalue,
        cross_output, gate_weight, up_weight, down_weight, bias_table, cotangent,
    ):
        core = lax.axis_index("col")
        forward = list(range(bits))
        backward = list(range(1, bits)) + [0]

        packed, s_keep, s_send = call(
            prep_self,
            [((192, 272), BF), ((384, 768), BF), ((96, 768), BF)],
            hidden_in.T, gain_self[None], gain_cross[None], gain_feed[None], self_querykey,
            self_value, self_output,
        )
        x_row = row_swap(packed)
        s_parts, s_peers = spread(s_send)
        s_other = col_swap(s_keep)
        table = jnp.pad(bias_table.T, ((0, 5), (0, 96)))
        peer_table = col_swap(table)
        bias, mask = call(
            masks, [((6, 128, 256), F32), ((128, 512), F32)],
            buckets, table, peer_table, token_segments, source_segments,
        )

        e_pack, c_keep, c_send = call(
            prep_cross,
            [((192, 768), BF), ((384, 768), BF), ((96, 768), BF)],
            encoder_states.T, cotangent.T, cross_query, cross_keyvalue, cross_output,
        )
        e_row = row_swap(e_pack)
        c_parts, c_peers = spread(c_send)
        c_other = col_swap(c_keep)

        f_keep, f_send, d_keep, d_send = call(
            prep_feed,
            [((384, 1024), BF), ((96, 1024), BF), ((512, 384), BF), ((128, 384), BF)],
            gate_weight, up_weight, down_weight,
        )
        d_parts, d_peers = spread(d_send)
        f_parts, f_peers = spread(f_send)
        f_other = col_swap(f_keep)
        d_other = col_swap(d_keep)

        part_shape = [((128, 768), F32), ((128, 768), BF)]
        matrix = [((384, 768), BF), ((384, 768), BF)]
        xg, gains, s_a1, s_b1, normed_self, ya, yb, self_mixed, self_lse, part, send = call(
            self_forward,
            [((256, 768), BF), ((16, 768), F32)] + matrix + [((256, 768), BF), ((256, 576), BF),
             ((256, 576), BF), ((128, 384), BF), ((6, 128, 1), F32)] + part_shape,
            packed, x_row, col_swap(packed), col_swap(x_row), s_keep, s_other,
            *s_parts, *s_peers, bias,
        )
        sw = (s_keep, s_a1, s_other, s_b1)
        recv = row_swap(send)
        ec, c_a1, c_b1, kva, kvb = call(
            encode_keys,
            [((768, 768), BF)] + matrix + [((512, 384), BF), ((512, 384), BF)],
            e_pack, e_row, col_swap(e_pack), col_swap(e_row), c_keep, c_other,
            *c_parts, *c_peers,
        )
        cw = (c_keep, c_a1, c_other, c_b1)
        resid_attn, normed_cross, cross_q, cross_mixed, cross_lse, part, send = call(
            cross_forward,
            [((128, 768), F32), ((128, 768), BF), ((128, 384), BF), ((128, 384), BF),
             ((6, 128, 1), F32)] + part_shape,
            xg, gains, part, recv, *cw, kva, kvb, mask,
        )
        recv = row_swap(send)
        f_a1, f_b1, d_a1, d_b1, upstream = call(
            feed_upstream,
            [((384, 1024), BF), ((384, 1024), BF), ((512, 384), BF), ((512, 384), BF),
             ((128, 1024), F32)],
            ec, d_keep, d_other, *f_parts, *f_peers, *d_parts, *d_peers,
        )
        dw = (d_keep, d_a1, d_other, d_b1)
        resid_cross, normed_feed, hidden, gate_delta, up_delta, part, send = call(
            feed_forward,
            [((128, 768), F32), ((128, 768), BF), ((128, 1024), BF), ((128, 1024), BF),
             ((128, 1024), BF)] + part_shape,
            xg, gains, resid_attn, part, recv, f_keep, f_a1, f_other, f_b1, upstream,
        )
        recv = row_swap(send)
        fi_keep, fi_send = call(
            feed_grads, [((768, 1024), BF), ((768, 1024), BF)],
            normed_feed, gate_delta, up_delta,
        )
        in_feed = core_sum(fi_keep, fi_send)
        fo_keep, fo_send, last_keep, last_send = call(
            feed_out,
            [((512, 768), BF), ((512, 768), BF), ((128, 384), F32), ((128, 384), BF)],
            hidden, ec, resid_cross, *dw,
        )
        out_feed = core_sum(fo_keep, fo_send)

        (grad_cross, upstream_cross, gain_feed_sum, cross_delta, dscores, probs, cross_dq, part,
         send) = call(
            cross_backward,
            [((128, 768), F32), ((128, 768), BF), ((8, 768), F32), ((128, 384), BF),
             ((6, 128, 512), BF), ((6, 128, 512), BF), ((128, 384), BF)] + part_shape,
            xg, gains, ec, part, recv, resid_cross, *cw, cross_q, kva, kvb, cross_lse, mask,
            cross_mixed,
        )
        recv = row_swap(send)
        ci_keep, ci_send, co_keep, co_send, enc_keep, enc_send = call(
            cross_grads,
            [((1152, 384), BF), ((1152, 384), BF), ((192, 768), BF), ((192, 768), BF),
             ((2, 192, 512), F32), ((2, 192, 512), BF)],
            ec, normed_cross, cross_q, cross_delta, dscores, probs, cross_dq, cross_mixed,
            upstream_cross, *cw,
        )
        in_cross = core_sum(ci_keep, ci_send)
        out_cross = core_sum(co_keep, co_send)

        (grad_attn, gain_cross_sum, dscores, dya, dyb, si_keep, si_send, so_keep, so_send) = call(
            self_backward,
            [((128, 768), F32), ((8, 768), F32), ((6, 128, 256), F32), ((256, 576), BF),
             ((256, 576), BF), ((1152, 384), BF), ((1152, 384), BF), ((192, 768), BF),
             ((192, 768), BF)],
            xg, gains, part, recv, grad_cross, resid_attn, *sw, normed_self, ya, yb, bias,
            self_lse, self_mixed,
        )
        in_self = core_sum(si_keep, si_send)
        out_self = core_sum(so_keep, so_send)
        keep, send = call(self_inputs, part_shape, dya, dyb, *sw)
        keep, send = call(self_sum, part_shape, keep, col_swap(send))
        recv = row_swap(send)
        (tables,) = call(table_sums, [((2, 32, 128), F32)], buckets, dscores)
        grad_keep, grad_send, small_keep, small_send = call(
            last_norm,
            [((192, 128), F32), ((192, 128), F32), ((48, 128), F32), ((48, 128), F32)],
            xg, gains, keep, recv, grad_attn, gain_feed_sum, gain_cross_sum, tables,
        )

        def join(mine, theirs):
            return jnp.where(
                core == 0,
                jnp.concatenate((mine, theirs), axis=1),
                jnp.concatenate((theirs, mine), axis=1),
            ).T

        grad_hidden = join(grad_keep, col_swap(grad_send))

        out_keep, out_send = call(
            last_out, [((192, 128), BF), ((192, 128), BF)],
            last_keep, row_swap(last_send),
        )
        hidden_out = join(out_keep, col_swap(out_send))

        enc = enc_keep + col_swap(enc_send).astype(F32)
        grad_encoder = (enc[0] + row_swap(enc[1].astype(BF)).astype(F32)).T

        total = small_keep + col_swap(small_send)
        for bit in range(bits):
            total = total + replica_swap(total, bit)
        gain_grads = lax.dynamic_slice_in_dim(total[:9].reshape(3, 384), core * 192, 192, axis=1)
        table_grad = total[16:, :3]

        per = 384 // replicas
        wide = 512 // replicas
        short = 192 // replicas

        def blocks_of(values):
            return values.reshape(replicas, values.shape[0] // replicas, 768)

        feed_pair = scatter(in_feed.reshape(2, replicas, per, 1024), 1, forward)
        out_pair = scatter(blocks_of(out_feed), 0, backward)
        cross_pair = scatter(in_cross.reshape(3, replicas, per, 384), 1, forward)
        self_pair = scatter(in_self.reshape(3, replicas, per, 384), 1, forward)
        rest_pair = scatter(
            jnp.concatenate((blocks_of(out_cross), blocks_of(out_self)), axis=1), 0, forward
        )

        mine, send = call(
            finish_early, [((per, 1600), F32), ((per, 1600), BF)],
            *feed_pair, *cross_pair,
        )
        gate_grad, up_grad, keyvalue_grad, crossquery_grad = call(
            place_early,
            [((per, 1024), F32), ((per, 1024), F32), ((per, 768), F32), ((per, 384), F32)],
            mine, row_swap(send),
        )
        mine, send = call(
            finish_self, [((per, 576), F32), ((per, 576), BF)], *self_pair
        )
        querykey_grad, value_grad = call(
            place_self,
            [((per, 768), F32), ((per, 384), F32)],
            mine, row_swap(send),
        )

        sends = call(
            finish_out, [((wide + 2 * short, 384), BF)] * 2, *out_pair, *rest_pair
        )
        got = []
        for shift in (0, 1):
            moves = []
            for source in range(2 * replicas):
                replica, side = divmod(source, 2)
                block = side * replicas + replica
                moves.append((source, (block // 2) * 2 + ((block % 2) ^ shift)))
            got.append(lax.ppermute(sends[shift], ("dp", "row"), moves))
        down_grad, crossout_grad, output_grad = call(
            place_rows,
            [((2 * wide, 384), F32), ((2 * short, 384), F32), ((2 * short, 384), F32)], *got,
        )

        return (
            hidden_out, grad_hidden, grad_encoder, querykey_grad, value_grad, output_grad,
            crossquery_grad, keyvalue_grad, crossout_grad, gate_grad, up_grad, down_grad,
            gain_grads[0], gain_grads[1], gain_grads[2], table_grad,
        )

    return layer


def solution(mesh):
    tokens = P("dp", ("row", "col"))
    inward = P("row", "col")
    outward = P("col", "row")
    features = P(("row", "col"))
    inward_grad = P(("row", "dp"), "col")
    outward_grad = P(("col", "dp"), "row")
    bias = P(None, ("col", "row"))
    return jax.shard_map(
        build(mesh.shape["dp"]),
        mesh=mesh,
        in_specs=(
            tokens, tokens, P("dp", None), P("dp", None), P(), features, features, features,
            inward, inward, outward, inward, inward, outward, inward, inward, outward, bias,
            tokens,
        ),
        out_specs=(
            tokens, tokens, tokens, inward_grad, inward_grad, outward_grad, inward_grad,
            inward_grad, outward_grad, inward_grad, inward_grad, outward_grad, features, features,
            features, bias,
        ),
        check_vma=False,
    )
```

time: 949 us -> 296 us (0.31)
  waiting for transfers between devices: 679 us -> 102 us
  blocking collectives: 144 us -> 0 us
  Pallas kernels: 0 us -> 90 us
  starting transfers between devices: 1.04 us -> 72.6 us
  matrix products: 63.3 us -> 0 us
  other arithmetic: 25.9 us -> 11.6 us
  between operations: 14.9 us -> 1.41 us
    reduce_scatter x24 -> x0, waiting for transfers between devices: 611 us -> none  [the longest x1 68.5 us: shards(): lax.psum_scatter(down_local, 'dp', scatter_dimension=0, tiled=True)]
    ppermute x0 -> x83, waiting for transfers between devices: none -> 102 us  [the longest x30 80.1 us: replica_swap(): lax.ppermute(values, 'dp', [(i, i ^ 1 << bit) for i in range(replicas)])]
    pallas_call x0 -> x25, Pallas kernels: none -> 90 us  [call(): pl.pallas_call(kernel, out_shape=flat, in_specs=[space] * len(args), out_...]
    all_gather x16 -> x0, blocking collectives: 79.7 us -> none  [the longest x3 27.2 us: gather_pair(): lax.all_gather(second, 'row', axis=1, tiled=True)]
    ppermute x0 -> x83, starting transfers between devices: none -> 72.6 us  [the longest x30 40 us: replica_swap(): lax.ppermute(values, 'dp', [(i, i ^ 1 << bit) for i in range(replicas)])]
    unnamed x26 -> x0, waiting for transfers between devices: 68 us -> none
    psum x7 -> x0, blocking collectives: 64.1 us -> none  [the longest x6 41.9 us: feature_total(): return lax.psum(values, ('row', 'col'))]
    dot_general x43 -> x0, matrix products: 63.3 us -> none  [the longest x9 16.4 us: outer_sum(): lax.dot_general(left, right, (((0,), (0,)), ((), ())), preferred_element_...]
  transfers between devices with their start and end apart: 25 -> 83, of which waited for: 20 -> 33; matrix products, arithmetic and copies ran while one was open for 7% -> 6% of each run, Pallas kernels for 0% -> 22%
where the time goes in v1:
time: 296 us; the launch traced here: 295 us
  waiting for transfers between devices  102 us (34%)
  Pallas kernels  90 us (30%)
  starting transfers between devices  72.6 us (25%)
  local copies, waits for them, and re-layouts  16.8 us (6%)
  other arithmetic  11.6 us (4%)
    pallas_call x25, Pallas kernels, call(): pl.pallas_call(kernel, out_shape=flat, in_specs=[space] * len(args), out_...  90 us
    ppermute x30, waiting for transfers between devices, replica_swap(): lax.ppermute(values, 'dp', [(i, i ^ 1 << bit) for i in range(replicas)])  80.1 us
    ppermute x30, starting transfers between devices, replica_swap(): lax.ppermute(values, 'dp', [(i, i ^ 1 << bit) for i in range(replicas)])  40 us
    ppermute x15, starting transfers between devices, row_swap(): return lax.ppermute(values, 'row', SWAP)  22.7 us
    ppermute x15, waiting for transfers between devices, row_swap(): return lax.ppermute(values, 'row', SWAP)  19.9 us
    unnamed x130, local copies, waits for them, and re-layouts  11.4 us
    convert_element_type x6, other arithmetic, core_sum(): return (keep.astype(F32) + col_swap(send).astype(F32)).astype(BF)  6.29 us
    ppermute x36, starting transfers between devices, col_swap(): return lax.ppermute(values, 'col', SWAP)  6.2 us
  transfers between devices with their start and end apart: 83, of which 33 were waited for; matrix products, arithmetic and copies ran while one was open for 6% of the time, Pallas kernels for 22%

profile of v1, /device:TPU:0, one launch (start us, length us, event | category | flops | bytes accessed | tf_op | source)
XLA Modules:
  0.0 294.9 jit_solution(4714621300662675961)
XLA Ops:
  0.7 2.8 shard_map.312
  3.5 3.1 %collective-permute-start.36 = (bf16[128,384]{1,0:T(8,128)(2,1)}, bf16[128,384]{1,0:T(8,128)(2,1)S(1)}, u32[]{:S(2)}, u32[]{:S(2)}) collective-permute-start(bf16[128,384]{1,0:T(8,128)(2,1)} %get-tuple-element.141), channel_id=1, source_target_pairs={{0,2},{2,0},{1,3},{3,1},{4,6},{6,4},{5,7},{7,5},{8,10},{10,8},{9,1... | collective-permute-start | bytes 294920 | tf_op jit(solution)/shard_map/ppermute | solution.py:43
  6.5 2.6 shard_map.306
  19.2 3.2 %collective-permute-done.18.p0 = bf16[96,768]{1,0:T(8,128)(2,1)S(1)} collective-permute-done((bf16[96,768]{1,0:T(8,128)(2,1)}, bf16[96,768]{1,0:T(8,128)(2,1)S(1)}, u32[]{:S(2)}, u32[]{:S(2)}) %collective-permute-start.18) | collective-permute-done | bytes 147488 | tf_op jit(solution)/shard_map/ppermute | solution.py:43
  50.1 2.9 collective-permute-done.21.p3
  56.8 5.5 %shard_map.308 = (bf16[256,768]{1,0:T(8,128)(2,1)}, f32[16,768]{1,0:T(8,128)}, bf16[384,768]{1,0:T(8,128)(2,1)}, bf16[384,768]{1,0:T(8,128)(2,1)}, bf16[256,768]...) custom-call(bf16[192,272]{1,0:T(8,128)(2,1)} %get-tuple-element.118., ...), custom_call_target="tpu_custom_call" | custom-call | tf_op jit(solution)/shard_map/pallas_call | solution.py:33
  65.9 4.3 %shard_map.310 = (bf16[768,768]{1,0:T(8,128)(2,1)}, bf16[384,768]{1,0:T(8,128)(2,1)}, bf16[384,768]{1,0:T(8,128)(2,1)}, bf16[512,384]{1,0:T(8,128)(2,1)}, bf16[512,384]{1,0:T(8,128)(2,1)}) custom-call(bf16[192,768]{1,0:T(8,128)(2,1)} %get-tuple-element.127.own, bf16[192,768]{1,0:T(8,128)(2,1)} %copy-done.11, bf16[192,768]{1,0:T(8,128)(2,1)} %copy-done.10, ...), custom_call_target="tpu_custom_call" | custom-call | tf_op jit(solution)/shard_map/pallas_call | solution.py:33
  70.4 3.5 %collective-permute-done.31.refs_3_ = bf16[96,1024]{1,0:T(8,128)(2,1)S(1)} collective-permute-done((bf16[96,1024]{1,0:T(8,128)(2,1)}, bf16[96,1024]{1,0:T(8,128)(2,1)S(1)}, u32[]{:S(2)}, u32[]{:S(2)}) %collective-permute-start.31) | collective-permute-done | bytes 196640 | tf_op jit(solution)/shard_map/ppermute | solution.py:661
  74.3 6.3 %shard_map.311 = (f32[128,768]{1,0:T(8,128)}, bf16[128,768]{1,0:T(8,128)(2,1)}, bf16[128,384]{1,0:T(8,128)(2,1)}, bf16[128,384]{1,0:T(8,128)(2,1)}, f32[6,128,1]...) custom-call(bf16[256,768]{1,0:T(8,128)(2,1)} %get-tuple-element.122.xg, ...), custom_call_target="tpu_custom_call" | custom-call | tf_op jit(solution)/shard_map/pallas_call | solution.py:33
  83.1 4.2 %shard_map.313 = (bf16[384,1024]{1,0:T(8,128)(2,1)}, bf16[384,1024]{1,0:T(8,128)(2,1)}, bf16[512,384]{1,0:T(8,128)(2,1)}, bf16[512,384]{1,0:T(8,128)(2,1)}, f32[128,1024]{1,0:T(8,128)}) custom-call(bf16[768,768]{1,0:T(8,128)(2,1)} %get-tuple-element.138.ec, bf16[512,384]{1,0:T(8,128)(2,1)} %get-tuple-element.139.da0, bf16[512,384]{1,0:T(8,128)(2,1)} %copy-done.4, ...), custom_call_target="tpu_custom_call" | custom-call | tf_op jit(solution)/shard_map/pallas_call | solution.py:33
  88.5 5.2 %shard_map.314 = (f32[128,768]{1,0:T(8,128)}, bf16[128,768]{1,0:T(8,128)(2,1)}, bf16[128,1024]{1,0:T(8,128)(2,1)}, bf16[128,1024]{1,0:T(8,128)(2,1)}, bf16[128,1...) custom-call(bf16[256,768]{1,0:T(8,128)(2,1)} %get-tuple-element.122.xg, ...), custom_call_target="tpu_custom_call" | custom-call | tf_op jit(solution)/shard_map/pallas_call | solution.py:33
  95.2 5.0 %collective-permute-done.47.recv = bf16[128,768]{1,0:T(8,128)(2,1)S(1)} collective-permute-done((bf16[128,768]{1,0:T(8,128)(2,1)}, bf16[128,768]{1,0:T(8,128)(2,1)S(1)}, u32[]{:S(2)}, u32[]{:S(2)}) %collective-permute-start.47) | collective-permute-done | bytes 196640 | tf_op jit(solution)/shard_map/ppermute | solution.py:43
  100.9 6.4 %shard_map.317 = (f32[128,768]{1,0:T(8,128)}, bf16[128,768]{1,0:T(8,128)(2,1)}, f32[8,768]{1,0:T(8,128)}, bf16[128,384]{1,0:T(8,128)(2,1)}, bf16[6,128,512]{2,1,...) custom-call(bf16[256,768]{1,0:T(8,128)(2,1)} %get-tuple-element.122., ...), custom_call_target="tpu_custom_call" | custom-call | tf_op jit(solution)/shard_map/pallas_call | solution.py:33
  107.3 7.7 %shard_map.323 = (bf16[1152,384]{1,0:T(8,128)(2,1)}, bf16[1152,384]{1,0:T(8,128)(2,1)}, bf16[192,768]{1,0:T(8,128)(2,1)}, bf16[192,768]{1,0:T(8,128)(2,1)}, f32[...) custom-call(bf16[768,768]{1,0:T(8,128)(2,1)} %get-tuple-element.138.ec, bf16[128,768]{1,0:T(8,128)(2,1)} %get-tuple-element.180.normed, ...), custom_call_target="tpu_custom_call" | custom-call | tf_op jit(solution)/shard_map/pallas_call | solution.py:33
  115.0 3.6 %shard_map.315 = (bf16[512,768]{1,0:T(8,128)(2,1)}, bf16[512,768]{1,0:T(8,128)(2,1)}, f32[128,384]{1,0:T(8,128)}, bf16[128,384]{1,0:T(8,128)(2,1)}) custom-call(bf16[128,1024]{1,0:T(8,128)(2,1)} %get-tuple-element.145.hidden, bf16[768,768]{1,0:T(8,128)(2,1)} %get-tuple-element.138.ec, f32[128,768]{1,0:T(8,128)} %get-tuple-element.146.resid.resid_in, ...), custom_call_target="tpu_custom_call" | custom-call | tf_op jit(solution)/shard_map/pallas_call | solution.py:33
  120.7 3.8 %collective-permute-done.45.recv = bf16[128,384]{1,0:T(8,128)(2,1)S(1)} collective-permute-done((bf16[128,384]{1,0:T(8,128)(2,1)}, bf16[128,384]{1,0:T(8,128)(2,1)S(1)}, u32[]{:S(2)}, u32[]{:S(2)}) %collective-permute-start.45) | collective-permute-done | bytes 98336 | tf_op jit(solution)/shard_map/ppermute | solution.py:43
  127.4 3.4 %shard_map.328 = (bf16[768,1024]{1,0:T(8,128)(2,1)}, bf16[768,1024]{1,0:T(8,128)(2,1)}) custom-call(bf16[128,768]{1,0:T(8,128)(2,1)} %get-tuple-element.203.normed, bf16[128,1024]{1,0:T(8,128)(2,1)} %get-tuple-element.204.gate, bf16[128,1024]{1,0:T(8,128)(2,1)} %get-tuple-element.205.up), custom_call_target="tpu_custom_call" | custom-call | tf_op jit(solution)/shard_map/pallas_call | solution.py:33
  133.6 7.7 %shard_map.318 = (f32[128,768]{1,0:T(8,128)}, f32[8,768]{1,0:T(8,128)}, f32[6,128,256]{2,1,0:T(8,128)}, bf16[256,576]{1,0:T(8,128)(2,1)}, bf16[256,576]{1,0:T(8,...) custom-call(bf16[256,768]{1,0:T(8,128)(2,1)} %get-tuple-element.122., ...), custom_call_target="tpu_custom_call" | custom-call | tf_op jit(solution)/shard_map/pallas_call | solution.py:33
  141.3 4.7 %shard_map.321.tables = f32[2,32,128]{2,1,0:T(8,128)} custom-call(s32[256,256]{1,0:T(8,128)} %buckets.3, f32[6,128,256]{2,1,0:T(8,128)} %get-tuple-element.177.dscores), custom_call_target="tpu_custom_call" | custom-call | tf_op jit(solution)/shard_map/pallas_call | solution.py:33
  146.0 3.7 %shard_map.319 = (f32[128,768]{1,0:T(8,128)}, bf16[128,768]{1,0:T(8,128)(2,1)}) custom-call(bf16[256,576]{1,0:T(8,128)(2,1)} %get-tuple-element.168.dya, bf16[256,576]{1,0:T(8,128)(2,1)} %get-tuple-element.169.dyb, bf16[384,768]{1,0:T(8,128)(2,1)} %get-tuple-element.119.a0, bf16[384,768]{1,0:T(8,128)(2,1)} %get-tuple-element.161.a1, ...), custom_call_target="tpu_custom_call" | custom-call | tf_op jit(solution)/shard_map/pallas_call | solution.py:33
  156.3 4.9 %collective-permute-done.50.recv = bf16[128,768]{1,0:T(8,128)(2,1)S(1)} collective-permute-done((bf16[128,768]{1,0:T(8,128)(2,1)}, bf16[128,768]{1,0:T(8,128)(2,1)S(1)}, u32[]{:S(2)}, u32[]{:S(2)}) %collective-permute-start.50) | collective-permute-done | bytes 196640 | tf_op jit(solution)/shard_map/ppermute | solution.py:43
  161.8 2.6 shard_map.322
  176.7 2.6 collective-permute-start.82
  186.4 10.0 %collective-permute-done.66 = bf16[2,48,768]{2,1,0:T(8,128)(2,1)S(1)} collective-permute-done((bf16[2,48,768]{2,1,0:T(8,128)(2,1)S(1)}, bf16[2,48,768]{2,1,0:T(8,128)(2,1)S(1)}, u32[]{:S(2)}, u32[]{:S(2)}) %collective-permute-start.66) | collective-permute-done | bytes 147488 | tf_op jit(solution)/shard_map/ppermute | solution.py:661
  197.1 2.6 collective-permute-start.67
  205.0 7.1 %collective-permute-done.61 = bf16[2,64,768]{2,1,0:T(8,128)(2,1)S(1)} collective-permute-done((bf16[2,64,768]{2,1,0:T(8,128)(2,1)S(1)}, bf16[2,64,768]{2,1,0:T(8,128)(2,1)S(1)}, u32[]{:S(2)}, u32[]{:S(2)}) %collective-permute-start.61) | collective-permute-done | bytes 196640 | tf_op jit(solution)/shard_map/ppermute | solution.py:661
  213.3 11.3 %collective-permute-done.75 = bf16[3,2,2,48,384]{4,3,0,1,2:T(8,128)(2,1)S(1)} collective-permute-done((bf16[3,2,2,48,384]{4,3,0,1,2:T(8,128)(2,1)S(1)}, bf16[3,2,2,48,384]{4,3,0,1,2:T(8,128)(2,1)S(1)}, u32[]{:S(2)}, u32[]{:S(2)}) %collective-permute-start.75) | collective-permute-done | bytes 442400 | tf_op jit(solution)/shard_map/ppermute | solution.py:661
  227.0 13.6 %collective-permute-done.71 = bf16[2,2,2,48,1024]{4,3,0,1,2:T(8,128)(2,1)S(1)} collective-permute-done((bf16[2,2,2,48,1024]{4,3,0,1,2:T(8,128)(2,1)S(1)}, bf16[2,2,2,48,1024]{4,3,0,1,2:T(8,128)(2,1)S(1)}, u32[]{:S(2)}, u32[]{:S(2)}) %collective-permute-start.71) | collective-permute-done | bytes 786464 | tf_op jit(solution)/shard_map/ppermute | solution.py:661
  243.9 8.9 %collective-permute-done.72 = bf16[2,2,48,1024]{3,2,0,1:T(8,128)(2,1)S(1)} collective-permute-done((bf16[2,2,48,1024]{3,2,0,1:T(8,128)(2,1)S(1)}, bf16[2,2,48,1024]{3,2,0,1:T(8,128)(2,1)S(1)}, u32[]{:S(2)}, u32[]{:S(2)}) %collective-permute-start.72) | collective-permute-done | bytes 393248 | tf_op jit(solution)/shard_map/ppermute | solution.py:661
  259.6 6.0 %collective-permute-done.77.cross_recv = bf16[3,48,384]{2,1,0:T(8,128)(2,1)S(1)} collective-permute-done((bf16[3,48,384]{2,1,0:T(8,128)(2,1)S(1)}, bf16[3,48,384]{2,1,0:T(8,128)(2,1)S(1)}, u32[]{:S(2)}, u32[]{:S(2)}) %collective-permute-start.77) | collective-permute-done | bytes 110624 | tf_op jit(solution)/shard_map/ppermute | solution.py:661
  265.6 2.6 collective-permute-done.73.feed_recv
  281.8 4.5 %collective-permute-start.58 = (bf16[48,576]{1,0:T(8,128)(2,1)}, bf16[48,576]{1,0:T(8,128)(2,1)S(1)}, u32[]{:S(2)}, u32[]{:S(2)}) collective-permute-start(bf16[48,576]{1,0:T(8,128)(2,1)} %get-tuple-element.191), channel_id=1, source_target_pairs={{0,2},{2,0},{1,3},{3,1},{4,6},{6,4},{5,7},{7,5},{8,10},{10,8},{9,1... | collective-permute-start | bytes 165896 | tf_op jit(solution)/shard_map/ppermute | solution.py:43
  (336 shorter events, 127.0 us)
Async XLA Ops:
  3.5 11.1 %collective-permute-start.36 = (bf16[128,384]{1,0:T(8,128)(2,1)}, bf16[128,384]{1,0:T(8,128)(2,1)S(1)}, u32[]{:S(2)}, u32[]{:S(2)}) collective-permute-start(bf16[128,384]{1,0:T(8,128)(2,1)} %get-tuple-element.141), channel_id=1, source_target_pairs={{0,2},{2,0},{1,3},{3,1},{4,6},{6,4},{5,7},{7,5},{8,10},{10,8},{9,1... | collective-permute-start | bytes 294920 | tf_op jit(solution)/shard_map/ppermute | solution.py:43
  14.6 13.9 %collective-permute-start.28 = (bf16[96,1024]{1,0:T(8,128)(2,1)S(1)}, bf16[96,1024]{1,0:T(8,128)(2,1)}, u32[]{:S(2)}, u32[]{:S(2)}) collective-permute-start(bf16[96,1024]{1,0:T(8,128)(2,1)S(1)} %copy-done.62), channel_id=1, source_target_pairs={{0,2},{2,0},{1,3},{3,1},{4,6},{6,4},{5,7},{7,5},{8,10},{10,8},{9,1... | collective-permute-start | bytes 589832 | tf_op jit(solution)/shard_map/ppermute | solution.py:43
  39.1 14.5 %collective-permute-start.3 = (bf16[384,768]{1,0:T(8,128)(2,1)}, bf16[384,768]{1,0:T(8,128)(2,1)S(1)}, u32[]{:S(2)}, u32[]{:S(2)}) collective-permute-start(bf16[384,768]{1,0:T(8,128)(2,1)} %get-tuple-element.119.a0), channel_id=1, source_target_pairs={{0,1},{1,0},{2,3},{3,2},{4,5},{5,4},{6,7},{7,6},{8,9},{9,8},{10,11... | collective-permute-start | bytes 1769480 | tf_op jit(solution)/shard_map/ppermute | solution.py:47
  45.0 19.4 %collective-permute-start.17 = (bf16[384,768]{1,0:T(8,128)(2,1)}, bf16[384,768]{1,0:T(8,128)(2,1)S(1)}, u32[]{:S(2)}, u32[]{:S(2)}) collective-permute-start(bf16[384,768]{1,0:T(8,128)(2,1)} %get-tuple-element.126.a0), channel_id=1, source_target_pairs={{0,1},{1,0},{2,3},{3,2},{4,5},{5,4},{6,7},{7,6},{8,9},{9,8},{10,11... | collective-permute-start | bytes 1769480 | tf_op jit(solution)/shard_map/ppermute | solution.py:47
  49.5 37.8 %collective-permute-start.44 = (bf16[384,1024]{1,0:T(8,128)(2,1)S(1)}, bf16[384,1024]{1,0:T(8,128)(2,1)S(1)}, u32[]{:S(2)}, u32[]{:S(2)}) collective-permute-start(bf16[384,1024]{1,0:T(8,128)(2,1)S(1)} %copy-done.6), channel_id=1, source_target_pairs={{0,1},{1,0},{2,3},{3,2},{4,5},{5,4},{6,7},{7,6},{8,9},{9,8},{10,11... | collective-permute-start | bytes 2359304 | tf_op jit(solution)/shard_map/ppermute | solution.py:47
  53.0 11.0 %collective-permute-start.16 = (bf16[192,768]{1,0:T(8,128)(2,1)S(1)}, bf16[192,768]{1,0:T(8,128)(2,1)}, u32[]{:S(2)}, u32[]{:S(2)}) collective-permute-start(bf16[192,768]{1,0:T(8,128)(2,1)S(1)} %collective-permute-done.14.recv), channel_id=1, source_target_pairs={{0,1},{1,0},{2,3},{3,2},{4,5},{5,4},{6,7},{7,6},{8,9},{9,8},{10,11... | collective-permute-start | bytes 884744 | tf_op jit(solution)/shard_map/ppermute | solution.py:47
  53.1 27.6 %collective-permute-start.27 = (bf16[512,384]{1,0:T(8,128)(2,1)S(1)}, bf16[512,384]{1,0:T(8,128)(2,1)S(1)}, u32[]{:S(2)}, u32[]{:S(2)}) collective-permute-start(bf16[512,384]{1,0:T(8,128)(2,1)S(1)} %copy-done.3), channel_id=1, source_target_pairs={{0,1},{1,0},{2,3},{3,2},{4,5},{5,4},{6,7},{7,6},{8,9},{9,8},{10,11... | collective-permute-start | bytes 1179656 | tf_op jit(solution)/shard_map/ppermute | solution.py:47
  70.3 11.9 %collective-permute-start.33 = (bf16[96,1024]{1,0:T(8,128)(2,1)}, bf16[96,1024]{1,0:T(8,128)(2,1)S(1)}, u32[]{:S(2)}, u32[]{:S(2)}) collective-permute-start(bf16[96,1024]{1,0:T(8,128)(2,1)} %collective-permute-done.29.refs_1_), channel_id=1, source_target_pairs={{0,1},{1,0},{2,3},{3,2},{4,5},{5,4},{6,7},{7,6},{8,9},{9,8},{10,11... | collective-permute-start | bytes 589832 | tf_op jit(solution)/shard_map/ppermute | solution.py:47
  115.0 34.6 %collective-permute-start.63 = (bf16[192,768]{1,0:T(8,128)(2,1)}, bf16[192,768]{1,0:T(8,128)(2,1)S(1)}, u32[]{:S(2)}, u32[]{:S(2)}) collective-permute-start(bf16[192,768]{1,0:T(8,128)(2,1)} %get-tuple-element.197), channel_id=1, source_target_pairs={{0,1},{1,0},{2,3},{3,2},{4,5},{5,4},{6,7},{7,6},{8,9},{9,8},{10,11... | collective-permute-start | bytes 884744 | tf_op jit(solution)/shard_map/ppermute | solution.py:47
  119.8 13.1 %collective-permute-start.48 = (bf16[128,768]{1,0:T(8,128)(2,1)S(1)}, bf16[128,768]{1,0:T(8,128)(2,1)S(1)}, u32[]{:S(2)}, u32[]{:S(2)}) collective-permute-start(bf16[128,768]{1,0:T(8,128)(2,1)S(1)} %copy-done.61), channel_id=1, source_target_pairs={{0,2},{2,0},{1,3},{3,1},{4,6},{6,4},{5,7},{7,5},{8,10},{10,8},{9,1... | collective-permute-start | bytes 589832 | tf_op jit(solution)/shard_map/ppermute | solution.py:43
  126.9 22.8 %collective-permute-start.52 = (bf16[2,192,512]{2,1,0:T(8,128)(2,1)}, bf16[2,192,512]{2,1,0:T(8,128)(2,1)S(1)}, u32[]{:S(2)}, u32[]{:S(2)}) collective-permute-start(bf16[2,192,512]{2,1,0:T(8,128)(2,1)} %get-tuple-element.187), channel_id=1, source_target_pairs={{0,1},{1,0},{2,3},{3,2},{4,5},{5,4},{6,7},{7,6},{8,9},{9,8},{10,11... | collective-permute-start | bytes 1179656 | tf_op jit(solution)/shard_map/ppermute | solution.py:47
  127.4 39.7 %collective-permute-start.59 = (bf16[512,768]{1,0:T(8,128)(2,1)}, bf16[512,768]{1,0:T(8,128)(2,1)}, u32[]{:S(2)}, u32[]{:S(2)}) collective-permute-start(bf16[512,768]{1,0:T(8,128)(2,1)} %get-tuple-element.195), channel_id=1, source_target_pairs={{0,1},{1,0},{2,3},{3,2},{4,5},{5,4},{6,7},{7,6},{8,9},{9,8},{10,11... | collective-permute-start | bytes 2359304 | tf_op jit(solution)/shard_map/ppermute | solution.py:47
  130.9 71.6 %collective-permute-start.70 = (bf16[768,1024]{1,0:T(8,128)(2,1)}, bf16[768,1024]{1,0:T(8,128)(2,1)S(1)}, u32[]{:S(2)}, u32[]{:S(2)}) collective-permute-start(bf16[768,1024]{1,0:T(8,128)(2,1)} %get-tuple-element.207), channel_id=1, source_target_pairs={{0,1},{1,0},{2,3},{3,2},{4,5},{5,4},{6,7},{7,6},{8,9},{9,8},{10,11... | collective-permute-start | bytes 4718600 | tf_op jit(solution)/shard_map/ppermute | solution.py:47
  132.9 51.2 %collective-permute-start.74 = (bf16[1152,384]{1,0:T(8,128)(2,1)}, bf16[1152,384]{1,0:T(8,128)(2,1)}, u32[]{:S(2)}, u32[]{:S(2)}) collective-permute-start(bf16[1152,384]{1,0:T(8,128)(2,1)} %get-tuple-element.209), channel_id=1, source_target_pairs={{0,1},{1,0},{2,3},{3,2},{4,5},{5,4},{6,7},{7,6},{8,9},{9,8},{10,11... | collective-permute-start | bytes 2654216 | tf_op jit(solution)/shard_map/ppermute | solution.py:47
  151.3 49.0 %collective-permute-start.54 = (bf16[1152,384]{1,0:T(8,128)(2,1)}, bf16[1152,384]{1,0:T(8,128)(2,1)}, u32[]{:S(2)}, u32[]{:S(2)}) collective-permute-start(bf16[1152,384]{1,0:T(8,128)(2,1)} %get-tuple-element.189), channel_id=1, source_target_pairs={{0,1},{1,0},{2,3},{3,2},{4,5},{5,4},{6,7},{7,6},{8,9},{9,8},{10,11... | collective-permute-start | bytes 2654216 | tf_op jit(solution)/shard_map/ppermute | solution.py:47
  181.4 104.9 %collective-permute-start.51 = (f32[192,128]{1,0:T(8,128)S(1)}, f32[192,128]{1,0:T(8,128)S(1)}, u32[]{:S(2)}, u32[]{:S(2)}) collective-permute-start(f32[192,128]{1,0:T(8,128)S(1)} %copy-done.63), channel_id=1, source_target_pairs={{0,1},{1,0},{2,3},{3,2},{4,5},{5,4},{6,7},{7,6},{8,9},{9,8},{10,11... | collective-permute-start | bytes 294920 | tf_op jit(solution)/shard_map/ppermute | solution.py:47
  181.5 18.2 %collective-permute-start.60 = (bf16[2,2,64,768]{3,2,1,0:T(8,128)(2,1)}, bf16[2,2,64,768]{3,2,1,0:T(8,128)(2,1)S(1)}, u32[]{:S(2)}, u32[]{:S(2)}) collective-permute-start(bf16[2,2,64,768]{3,2,1,0:T(8,128)(2,1)} %dynamic-slice_bitcast_fusion.1), channel_id=1, source_target_pairs={{0,8},{4,12},{8,0},{12,4},{16,24},{20,28},{24,16},{28,20},{1,9},{5... | collective-permute-start | bytes 1179656 | tf_op jit(solution)/shard_map/ppermute | solution.py:661
  184.1 12.3 %collective-permute-start.66 = (bf16[2,48,768]{2,1,0:T(8,128)(2,1)S(1)}, bf16[2,48,768]{2,1,0:T(8,128)(2,1)S(1)}, u32[]{:S(2)}, u32[]{:S(2)}) collective-permute-start(bf16[2,48,768]{2,1,0:T(8,128)(2,1)S(1)} %dynamic-slice_bitcast_fusion.7), channel_id=1, source_target_pairs={{0,8},{4,12},{8,0},{12,4},{16,24},{20,28},{24,16},{28,20},{1,9},{5... | collective-permute-start | bytes 442376 | tf_op jit(solution)/shard_map/ppermute | solution.py:661
  197.1 76.3 %collective-permute-start.67 = (bf16[48,768]{1,0:T(8,128)(2,1)S(1)}, bf16[48,768]{1,0:T(8,128)(2,1)S(1)}, u32[]{:S(2)}, u32[]{:S(2)}) collective-permute-start(bf16[48,768]{1,0:T(8,128)(2,1)S(1)} %get-tuple-element.252), channel_id=1, source_target_pairs={{0,16},{4,20},{8,24},{12,28},{16,0},{20,4},{24,8},{28,12},{1,17},{... | collective-permute-start | bytes 221192 | tf_op jit(solution)/shard_map/ppermute | solution.py:661
  199.8 12.3 %collective-permute-start.61 = (bf16[2,64,768]{2,1,0:T(8,128)(2,1)S(1)}, bf16[2,64,768]{2,1,0:T(8,128)(2,1)S(1)}, u32[]{:S(2)}, u32[]{:S(2)}) collective-permute-start(bf16[2,64,768]{2,1,0:T(8,128)(2,1)S(1)} %dynamic-slice_bitcast_fusion.6), channel_id=1, source_target_pairs={{0,16},{4,20},{8,24},{12,28},{16,0},{20,4},{24,8},{28,12},{1,17},{... | collective-permute-start | bytes 589832 | tf_op jit(solution)/shard_map/ppermute | solution.py:661
  202.0 23.1 %collective-permute-start.55 = (bf16[3,2,2,48,384]{4,3,0,1,2:T(8,128)(2,1)S(1)}, bf16[3,2,2,48,384]{4,3,0,1,2:T(8,128)(2,1)S(1)}, u32[]{:S(2)}, u32[]{:S(2)}) collective-permute-start(bf16[3,2,2,48,384]{4,3,0,1,2:T(8,128)(2,1)S(1)} %bitcast.122), channel_id=1, source_target_pairs={{0,4},{4,0},{8,12},{12,8},{16,20},{20,16},{24,28},{28,24},{1,5},{5... | collective-permute-start | bytes 1327112 | tf_op jit(solution)/shard_map/ppermute | solution.py:661
  202.4 22.1 %collective-permute-start.75 = (bf16[3,2,2,48,384]{4,3,0,1,2:T(8,128)(2,1)S(1)}, bf16[3,2,2,48,384]{4,3,0,1,2:T(8,128)(2,1)S(1)}, u32[]{:S(2)}, u32[]{:S(2)}) collective-permute-start(bf16[3,2,2,48,384]{4,3,0,1,2:T(8,128)(2,1)S(1)} %bitcast.123), channel_id=1, source_target_pairs={{0,4},{4,0},{8,12},{12,8},{16,20},{20,16},{24,28},{28,24},{1,5},{5... | collective-permute-start | bytes 1327112 | tf_op jit(solution)/shard_map/ppermute | solution.py:661
  212.1 28.5 %collective-permute-start.71 = (bf16[2,2,2,48,1024]{4,3,0,1,2:T(8,128)(2,1)S(1)}, bf16[2,2,2,48,1024]{4,3,0,1,2:T(8,128)(2,1)S(1)}, u32[]{:S(2)}, u32[]{:S(2)}) collective-permute-start(bf16[2,2,2,48,1024]{4,3,0,1,2:T(8,128)(2,1)S(1)} %bitcast.121), channel_id=1, source_target_pairs={{0,4},{4,0},{8,12},{12,8},{16,20},{20,16},{24,28},{28,24},{1,5},{5... | collective-permute-start | bytes 2359304 | tf_op jit(solution)/shard_map/ppermute | solution.py:661
  224.6 48.9 %collective-permute-start.62 = (bf16[64,768]{1,0:T(8,128)(2,1)S(1)}, bf16[64,768]{1,0:T(8,128)(2,1)S(1)}, u32[]{:S(2)}, u32[]{:S(2)}) collective-permute-start(bf16[64,768]{1,0:T(8,128)(2,1)S(1)} %get-tuple-element.250), channel_id=1, source_target_pairs={{0,4},{4,0},{8,12},{12,8},{16,20},{20,16},{24,28},{28,24},{1,5},{5... | collective-permute-start | bytes 294920 | tf_op jit(solution)/shard_map/ppermute | solution.py:661
  225.1 17.6 %collective-permute-start.76 = (bf16[3,2,48,384]{3,2,0,1:T(8,128)(2,1)S(1)}, bf16[3,2,48,384]{3,2,0,1:T(8,128)(2,1)S(1)}, u32[]{:S(2)}, u32[]{:S(2)}) collective-permute-start(bf16[3,2,48,384]{3,2,0,1:T(8,128)(2,1)S(1)} %dynamic-slice_bitcast_fusion.2), channel_id=1, source_target_pairs={{0,8},{4,12},{8,0},{12,4},{16,24},{20,28},{24,16},{28,20},{1,9},{5... | collective-permute-start | bytes 663560 | tf_op jit(solution)/shard_map/ppermute | solution.py:661
  241.0 11.9 %collective-permute-start.72 = (bf16[2,2,48,1024]{3,2,0,1:T(8,128)(2,1)S(1)}, bf16[2,2,48,1024]{3,2,0,1:T(8,128)(2,1)S(1)}, u32[]{:S(2)}, u32[]{:S(2)}) collective-permute-start(bf16[2,2,48,1024]{3,2,0,1:T(8,128)(2,1)S(1)} %dynamic-slice_bitcast_fusion), channel_id=1, source_target_pairs={{0,8},{4,12},{8,0},{12,4},{16,24},{20,28},{24,16},{28,20},{1,9},{5... | collective-permute-start | bytes 1179656 | tf_op jit(solution)/shard_map/ppermute | solution.py:661
  242.7 13.5 %collective-permute-start.56 = (bf16[3,2,48,384]{3,2,0,1:T(8,128)(2,1)S(1)}, bf16[3,2,48,384]{3,2,0,1:T(8,128)(2,1)S(1)}, u32[]{:S(2)}, u32[]{:S(2)}) collective-permute-start(bf16[3,2,48,384]{3,2,0,1:T(8,128)(2,1)S(1)} %dynamic-slice_bitcast_fusion.3), channel_id=1, source_target_pairs={{0,8},{4,12},{8,0},{12,4},{16,24},{20,28},{24,16},{28,20},{1,9},{5... | collective-permute-start | bytes 663560 | tf_op jit(solution)/shard_map/ppermute | solution.py:661
  252.8 12.8 %collective-permute-start.77 = (bf16[3,48,384]{2,1,0:T(8,128)(2,1)S(1)}, bf16[3,48,384]{2,1,0:T(8,128)(2,1)S(1)}, u32[]{:S(2)}, u32[]{:S(2)}) collective-permute-start(bf16[3,48,384]{2,1,0:T(8,128)(2,1)S(1)} %get-tuple-element.246), channel_id=1, source_target_pairs={{0,16},{4,20},{8,24},{12,28},{16,0},{20,4},{24,8},{28,12},{1,17},{... | collective-permute-start | bytes 331784 | tf_op jit(solution)/shard_map/ppermute | solution.py:661
  256.3 12.0 %collective-permute-start.73 = (bf16[2,48,1024]{2,1,0:T(8,128)(2,1)S(1)}, bf16[2,48,1024]{2,1,0:T(8,128)(2,1)S(1)}, u32[]{:S(2)}, u32[]{:S(2)}) collective-permute-start(bf16[2,48,1024]{2,1,0:T(8,128)(2,1)S(1)} %get-tuple-element.244), channel_id=1, source_target_pairs={{0,16},{4,20},{8,24},{12,28},{16,0},{20,4},{24,8},{28,12},{1,17},{... | collective-permute-start | bytes 589832 | tf_op jit(solution)/shard_map/ppermute | solution.py:661
  265.6 13.9 %collective-permute-start.57 = (bf16[3,48,384]{2,1,0:T(8,128)(2,1)S(1)}, bf16[3,48,384]{2,1,0:T(8,128)(2,1)S(1)}, u32[]{:S(2)}, u32[]{:S(2)}) collective-permute-start(bf16[3,48,384]{2,1,0:T(8,128)(2,1)S(1)} %get-tuple-element.248), channel_id=1, source_target_pairs={{0,16},{4,20},{8,24},{12,28},{16,0},{20,4},{24,8},{28,12},{1,17},{... | collective-permute-start | bytes 331784 | tf_op jit(solution)/shard_map/ppermute | solution.py:661
  270.9 21.4 %collective-permute-start.78 = (bf16[48,1600]{1,0:T(8,128)(2,1)}, bf16[48,1600]{1,0:T(8,128)(2,1)S(1)}, u32[]{:S(2)}, u32[]{:S(2)}) collective-permute-start(bf16[48,1600]{1,0:T(8,128)(2,1)} %get-tuple-element.211), channel_id=1, source_target_pairs={{0,2},{2,0},{1,3},{3,1},{4,6},{6,4},{5,7},{7,5},{8,10},{10,8},{9,1... | collective-permute-start | bytes 460808 | tf_op jit(solution)/shard_map/ppermute | solution.py:43
  275.8 11.2 %collective-permute-start.68 = (bf16[112,384]{1,0:T(8,128)(2,1)}, bf16[112,384]{1,0:T(8,128)(2,1)S(1)}, u32[]{:S(2)}, u32[]{:S(2)}) collective-permute-start(bf16[112,384]{1,0:T(8,128)(2,1)} %get-tuple-element.200), channel_id=1, source_target_pairs={{0,0},{2,16},{4,2},{6,18},{8,4},{10,20},{12,6},{14,22},{16,8},{18,... | collective-permute-start | bytes 258056 | tf_op jit(solution)/shard_map/ppermute | solution.py:888
  (115 other events, 928.4 us)

commit v2 on v1

--- a/solution.py
+++ b/solution.py
@@ -27,16 +27,24 @@
     return lax.dot_general(left, right, (((0,), (0,)), ((), ())), preferred_element_type=F32)
 
 
-def call(kernel, outs, *args):
-    flat = [jax.ShapeDtypeStruct(shape, dtype) for shape, dtype in outs]
+def far(values):
+    return pltpu.with_memory_space_constraint(values, pltpu.HBM)
+
+
+def call(kernel, outs, *args, hbm=()):
+    flat = [
+        (pltpu.HBM if at in hbm else jax.ShapeDtypeStruct)(shape, dtype)
+        for at, (shape, dtype) in enumerate(outs)
+    ]
     space = pl.BlockSpec(memory_space=pltpu.VMEM)
-    return pl.pallas_call(
+    got = pl.pallas_call(
         kernel,
         out_shape=flat,
         in_specs=[space] * len(args),
         out_specs=[space] * len(flat),
-        compiler_params=pltpu.CompilerParams(vmem_limit_bytes=60 * 1024 * 1024),
+        compiler_params=pltpu.CompilerParams(vmem_limit_bytes=16 * 1024 * 1024),
     )(*args)
+    return [far(out) if at in hbm else out for at, out in enumerate(got)]
 
 
 def row_swap(values):
@@ -690,13 +698,19 @@
         cross_output, gate_weight, up_weight, down_weight, bias_table, cotangent,
     ):
         core = lax.axis_index("col")
+        (buckets, self_querykey, self_value, self_output, cross_query, cross_keyvalue,
+         cross_output, gate_weight, up_weight, down_weight, token_segments, source_segments) = map(
+            far,
+            (buckets, self_querykey, self_value, self_output, cross_query, cross_keyvalue,
+             cross_output, gate_weight, up_weight, down_weight, token_segments, source_segments),
+        )
         forward = list(range(bits))
         backward = list(range(1, bits)) + [0]
 
         packed, s_keep, s_send = call(
             prep_self,
             [((192, 272), BF), ((384, 768), BF), ((96, 768), BF)],
-            hidden_in.T, gain_self[None], gain_cross[None], gain_feed[None], self_querykey,
+            far(hidden_in.T), far(gain_self[None]), far(gain_cross[None]), far(gain_feed[None]), self_querykey,
             self_value, self_output,
         )
         x_row = row_swap(packed)
@@ -706,13 +720,13 @@
         peer_table = col_swap(table)
         bias, mask = call(
             masks, [((6, 128, 256), F32), ((128, 512), F32)],
-            buckets, table, peer_table, token_segments, source_segments,
+            buckets, table, peer_table, token_segments, source_segments, hbm=(0, 1),
         )
 
         e_pack, c_keep, c_send = call(
             prep_cross,
             [((192, 768), BF), ((384, 768), BF), ((96, 768), BF)],
-            encoder_states.T, cotangent.T, cross_query, cross_keyvalue, cross_output,
+            far(encoder_states.T), far(cotangent.T), cross_query, cross_keyvalue, cross_output,
         )
         e_row = row_swap(e_pack)
         c_parts, c_peers = spread(c_send)
@@ -735,47 +749,46 @@
             [((256, 768), BF), ((16, 768), F32)] + matrix + [((256, 768), BF), ((256, 576), BF),
              ((256, 576), BF), ((128, 384), BF), ((6, 128, 1), F32)] + part_shape,
             packed, x_row, col_swap(packed), col_swap(x_row), s_keep, s_other,
-            *s_parts, *s_peers, bias,
-        )
-        sw = (s_keep, s_a1, s_other, s_b1)
+            *s_parts, *s_peers, bias, hbm=(0, 1, 2, 3, 4, 5, 6, 7, 8),
+        )
+        sw = (far(s_keep), s_a1, far(s_other), s_b1)
         recv = row_swap(send)
         ec, c_a1, c_b1, kva, kvb = call(
             encode_keys,
             [((768, 768), BF)] + matrix + [((512, 384), BF), ((512, 384), BF)],
             e_pack, e_row, col_swap(e_pack), col_swap(e_row), c_keep, c_other,
-            *c_parts, *c_peers,
-        )
-        cw = (c_keep, c_a1, c_other, c_b1)
+            *c_parts, *c_peers, hbm=(0, 1, 2, 3, 4),
+        )
+        cw = (far(c_keep), c_a1, far(c_other), c_b1)
         resid_attn, normed_cross, cross_q, cross_mixed, cross_lse, part, send = call(
             cross_forward,
             [((128, 768), F32), ((128, 768), BF), ((128, 384), BF), ((128, 384), BF),
              ((6, 128, 1), F32)] + part_shape,
-            xg, gains, part, recv, *cw, kva, kvb, mask,
+            xg, gains, part, recv, *cw, kva, kvb, mask, hbm=(0, 1, 2, 3, 4),
         )
         recv = row_swap(send)
         f_a1, f_b1, d_a1, d_b1, upstream = call(
             feed_upstream,
             [((384, 1024), BF), ((384, 1024), BF), ((512, 384), BF), ((512, 384), BF),
              ((128, 1024), F32)],
-            ec, d_keep, d_other, *f_parts, *f_peers, *d_parts, *d_peers,
-        )
-        dw = (d_keep, d_a1, d_other, d_b1)
+            ec, d_keep, d_other, *f_parts, *f_peers, *d_parts, *d_peers, hbm=(2, 3),
+        )
+        dw = (far(d_keep), d_a1, far(d_other), d_b1)
         resid_cross, normed_feed, hidden, gate_delta, up_delta, part, send = call(
             feed_forward,
             [((128, 768), F32), ((128, 768), BF), ((128, 1024), BF), ((128, 1024), BF),
              ((128, 1024), BF)] + part_shape,
-            xg, gains, resid_attn, part, recv, f_keep, f_a1, f_other, f_b1, upstream,
+            xg, gains, resid_attn, part, recv, f_keep, f_a1, f_other, f_b1, upstream, hbm=(0, 2),
         )
         recv = row_swap(send)
         fi_keep, fi_send = call(
             feed_grads, [((768, 1024), BF), ((768, 1024), BF)],
-            normed_feed, gate_delta, up_delta,
-        )
+            normed_feed, gate_delta, up_delta,)
         in_feed = core_sum(fi_keep, fi_send)
         fo_keep, fo_send, last_keep, last_send = call(
             feed_out,
             [((512, 768), BF), ((512, 768), BF), ((128, 384), F32), ((128, 384), BF)],
-            hidden, ec, resid_cross, *dw,
+            hidden, ec, resid_cross, *dw, hbm=(2,),
         )
         out_feed = core_sum(fo_keep, fo_send)
 
@@ -785,7 +798,7 @@
             [((128, 768), F32), ((128, 768), BF), ((8, 768), F32), ((128, 384), BF),
              ((6, 128, 512), BF), ((6, 128, 512), BF), ((128, 384), BF)] + part_shape,
             xg, gains, ec, part, recv, resid_cross, *cw, cross_q, kva, kvb, cross_lse, mask,
-            cross_mixed,
+            cross_mixed, hbm=(0, 2),
         )
         recv = row_swap(send)
         ci_keep, ci_send, co_keep, co_send, enc_keep, enc_send = call(
@@ -793,8 +806,7 @@
             [((1152, 384), BF), ((1152, 384), BF), ((192, 768), BF), ((192, 768), BF),
              ((2, 192, 512), F32), ((2, 192, 512), BF)],
             ec, normed_cross, cross_q, cross_delta, dscores, probs, cross_dq, cross_mixed,
-            upstream_cross, *cw,
-        )
+            upstream_cross, *cw,)
         in_cross = core_sum(ci_keep, ci_send)
         out_cross = core_sum(co_keep, co_send)
 
@@ -804,7 +816,7 @@
              ((256, 576), BF), ((1152, 384), BF), ((1152, 384), BF), ((192, 768), BF),
              ((192, 768), BF)],
             xg, gains, part, recv, grad_cross, resid_attn, *sw, normed_self, ya, yb, bias,
-            self_lse, self_mixed,
+            self_lse, self_mixed, hbm=(0, 1),
         )
         in_self = core_sum(si_keep, si_send)
         out_self = core_sum(so_keep, so_send)

time: 296 us -> 270 us (0.912)
  Pallas kernels: 90 us -> 64.4 us
  local copies, waits for them, and re-layouts: 16.8 us -> 7.6 us
  waiting for transfers between devices: 102 us -> 108 us
    pallas_call x25, Pallas kernels: 90 us -> 64.4 us  [call(): pl.pallas_call(kernel, out_shape=flat, in_specs=[space] * len(args), out_...]
    unnamed x130 -> x42, local copies, waits for them, and re-layouts: 11.4 us -> 4.73 us
    ppermute x30, waiting for transfers between devices: 80.1 us -> 84.6 us  [replica_swap(): lax.ppermute(values, 'dp', [(i, i ^ 1 << bit) for i in range(replicas)])]
    ppermute x15, waiting for transfers between devices: 19.9 us -> 23 us  [row_swap(): return lax.ppermute(values, 'row', SWAP)]
  transfers between devices with their start and end apart: 83 -> 83, of which waited for: 33 -> 31; matrix products, arithmetic and copies ran while one was open for 6% -> 7% of each run, Pallas kernels for 22% -> 17%
where the time goes in v2:
time: 270 us; the launch traced here: 269 us
  waiting for transfers between devices  108 us (40%)
  starting transfers between devices  73.9 us (27%)
  Pallas kernels  64.4 us (24%)
  other arithmetic  13.3 us (5%)
  local copies, waits for them, and re-layouts  7.6 us (3%)
    ppermute x30, waiting for transfers between devices, replica_swap(): lax.ppermute(values, 'dp', [(i, i ^ 1 << bit) for i in range(replicas)])  84.6 us
    pallas_call x25, Pallas kernels, call(): pl.pallas_call(kernel, out_shape=flat, in_specs=[space] * len(args), out_...  64.4 us
    ppermute x30, starting transfers between devices, replica_swap(): lax.ppermute(values, 'dp', [(i, i ^ 1 << bit) for i in range(replicas)])  40.4 us
    ppermute x15, starting transfers between devices, row_swap(): return lax.ppermute(values, 'row', SWAP)  23.8 us
    ppermute x15, waiting for transfers between devices, row_swap(): return lax.ppermute(values, 'row', SWAP)  23 us
    convert_element_type x6, other arithmetic, core_sum(): return (keep.astype(F32) + col_swap(send).astype(F32)).astype(BF)  6.23 us
    ppermute x36, starting transfers between devices, col_swap(): return lax.ppermute(values, 'col', SWAP)  6 us
  transfers between devices with their start and end apart: 83, of which 31 were waited for; matrix products, arithmetic and copies ran while one was open for 7% of the time, Pallas kernels for 17%

profile of v2, /device:TPU:0, one launch (start us, length us, event | category | flops | bytes accessed | tf_op | source)
XLA Modules:
  0.0 268.9 jit_solution(10778923653324868082)
XLA Ops:
  2.4 3.1 %collective-permute-start.36 = (bf16[128,384]{1,0:T(8,128)(2,1)S(1)}, bf16[128,384]{1,0:T(8,128)(2,1)S(1)}, u32[]{:S(2)}, u32[]{:S(2)}) collective-permute-start(bf16[128,384]{1,0:T(8,128)(2,1)S(1)} %get-tuple-element.141), channel_id=1, source_target_pairs={{0,2},{2,0},{1,3},{3,1},{4,6},{6,4},{5,7},{7,5},{8,10},{10,8},{9,1... | collective-permute-start | bytes 294920 | tf_op jit(solution)/shard_map/ppermute | solution.py:51
  17.2 3.2 %collective-permute-done.18.p0 = bf16[96,768]{1,0:T(8,128)(2,1)S(1)} collective-permute-done((bf16[96,768]{1,0:T(8,128)(2,1)S(1)}, bf16[96,768]{1,0:T(8,128)(2,1)S(1)}, u32[]{:S(2)}, u32[]{:S(2)}) %collective-permute-start.18) | collective-permute-done | bytes 147488 | tf_op jit(solution)/shard_map/ppermute | solution.py:51
  47.8 3.2 %collective-permute-done.21.p3 = bf16[96,768]{1,0:T(8,128)(2,1)S(1)} collective-permute-done((bf16[96,768]{1,0:T(8,128)(2,1)S(1)}, bf16[96,768]{1,0:T(8,128)(2,1)S(1)}, u32[]{:S(2)}, u32[]{:S(2)}) %collective-permute-start.21) | collective-permute-done | bytes 147488 | tf_op jit(solution)/shard_map/ppermute | solution.py:669
  51.5 2.7 shard_map.307
  54.2 4.3 %shard_map.308 = (bf16[256,768]{1,0:T(8,128)(2,1)}, f32[16,768]{1,0:T(8,128)}, bf16[384,768]{1,0:T(8,128)(2,1)}, bf16[384,768]{1,0:T(8,128)(2,1)}, bf16[256,768]...) custom-call(bf16[192,272]{1,0:T(8,128)(2,1)S(1)} %get-tuple-element., ...), custom_call_target="tpu_custom_call" | custom-call | tf_op jit(solution)/shard_map/pallas_call | solution.py:40
  62.0 2.6 shard_map.310
  66.3 3.5 %collective-permute-done.31.refs_3_ = bf16[96,1024]{1,0:T(8,128)(2,1)S(1)} collective-permute-done((bf16[96,1024]{1,0:T(8,128)(2,1)S(1)}, bf16[96,1024]{1,0:T(8,128)(2,1)S(1)}, u32[]{:S(2)}, u32[]{:S(2)}) %collective-permute-start.31) | collective-permute-done | bytes 196640 | tf_op jit(solution)/shard_map/ppermute | solution.py:669
  70.4 5.8 %shard_map.311 = (f32[128,768]{1,0:T(8,128)}, bf16[128,768]{1,0:T(8,128)(2,1)}, bf16[128,384]{1,0:T(8,128)(2,1)}, bf16[128,384]{1,0:T(8,128)(2,1)}, f32[6,128,1]...) custom-call(bf16[256,768]{1,0:T(8,128)(2,1)} %get-tuple-element.122.xg, ...), custom_call_target="tpu_custom_call" | custom-call | tf_op jit(solution)/shard_map/pallas_call | solution.py:40
  77.6 2.6 shard_map.313
  80.2 2.8 %collective-permute-done.26.recv = bf16[128,768]{1,0:T(8,128)(2,1)S(1)} collective-permute-done((bf16[128,768]{1,0:T(8,128)(2,1)S(1)}, bf16[128,768]{1,0:T(8,128)(2,1)S(1)}, u32[]{:S(2)}, u32[]{:S(2)}) %collective-permute-start.26) | collective-permute-done | bytes 196640 | tf_op jit(solution)/shard_map/ppermute | solution.py:51
  83.0 3.7 %shard_map.314 = (f32[128,768]{1,0:T(8,128)}, bf16[128,768]{1,0:T(8,128)(2,1)S(1)}, bf16[128,1024]{1,0:T(8,128)(2,1)}, bf16[128,1024]{1,0:T(8,128)(2,1)S(1)}, bf...) custom-call(bf16[256,768]{1,0:T(8,128)(2,1)} %get-tuple-element.122.xg, ...), custom_call_target="tpu_custom_call" | custom-call | tf_op jit(solution)/shard_map/pallas_call | solution.py:40
  88.1 4.6 %collective-permute-done.47.recv = bf16[128,768]{1,0:T(8,128)(2,1)S(1)} collective-permute-done((bf16[128,768]{1,0:T(8,128)(2,1)S(1)}, bf16[128,768]{1,0:T(8,128)(2,1)S(1)}, u32[]{:S(2)}, u32[]{:S(2)}) %collective-permute-start.47) | collective-permute-done | bytes 196640 | tf_op jit(solution)/shard_map/ppermute | solution.py:51
  92.6 6.1 %shard_map.317 = (f32[128,768]{1,0:T(8,128)}, bf16[128,768]{1,0:T(8,128)(2,1)S(1)}, f32[8,768]{1,0:T(8,128)}, bf16[128,384]{1,0:T(8,128)(2,1)S(1)}, bf16[6,128,5...) custom-call(bf16[256,768]{1,0:T(8,128)(2,1)} %get-tuple-element.122., ...), custom_call_target="tpu_custom_call" | custom-call | tf_op jit(solution)/shard_map/pallas_call | solution.py:40
  99.4 6.2 %shard_map.323 = (bf16[1152,384]{1,0:T(8,128)(2,1)S(1)}, bf16[1152,384]{1,0:T(8,128)(2,1)S(1)}, bf16[192,768]{1,0:T(8,128)(2,1)S(1)}, bf16[192,768]{1,0:T(8,128)...) custom-call(bf16[768,768]{1,0:T(8,128)(2,1)} %get-tuple-element.138.ec, ...), custom_call_target="tpu_custom_call" | custom-call | tf_op jit(solution)/shard_map/pallas_call | solution.py:40
  105.7 4.2 %shard_map.315 = (bf16[512,768]{1,0:T(8,128)(2,1)S(1)}, bf16[512,768]{1,0:T(8,128)(2,1)}, f32[128,384]{1,0:T(8,128)}, bf16[128,384]{1,0:T(8,128)(2,1)S(1)}) custom-call(bf16[128,1024]{1,0:T(8,128)(2,1)} %get-tuple-element.145.hidden, bf16[768,768]{1,0:T(8,128)(2,1)} %get-tuple-element.138.ec, f32[128,768]{1,0:T(8,128)} %get-tuple-element.146.resid.resid_in, ...), custom_call_target="tpu_custom_call" | custom-call | tf_op jit(solution)/shard_map/pallas_call | solution.py:40
  112.9 3.4 %collective-permute-done.45.recv = bf16[128,384]{1,0:T(8,128)(2,1)S(1)} collective-permute-done((bf16[128,384]{1,0:T(8,128)(2,1)S(1)}, bf16[128,384]{1,0:T(8,128)(2,1)S(1)}, u32[]{:S(2)}, u32[]{:S(2)}) %collective-permute-start.45) | collective-permute-done | bytes 98336 | tf_op jit(solution)/shard_map/ppermute | solution.py:51
  122.5 7.0 %shard_map.318 = (f32[128,768]{1,0:T(8,128)}, f32[8,768]{1,0:T(8,128)}, f32[6,128,256]{2,1,0:T(8,128)S(1)}, bf16[256,576]{1,0:T(8,128)(2,1)S(1)}, bf16[256,576]{...) custom-call(bf16[256,768]{1,0:T(8,128)(2,1)} %get-tuple-element.122., ...), custom_call_target="tpu_custom_call" | custom-call | tf_op jit(solution)/shard_map/pallas_call | solution.py:40
  129.5 3.8 %shard_map.321.tables = f32[2,32,128]{2,1,0:T(8,128)S(1)} custom-call(s32[256,256]{1,0:T(8,128)} %buckets.3, f32[6,128,256]{2,1,0:T(8,128)S(1)} %get-tuple-element.177.dscores), custom_call_target="tpu_custom_call" | custom-call | tf_op jit(solution)/shard_map/pallas_call | solution.py:40
  133.3 2.7 shard_map.319
  141.2 5.2 %collective-permute-done.50.recv = bf16[128,768]{1,0:T(8,128)(2,1)S(1)} collective-permute-done((bf16[128,768]{1,0:T(8,128)(2,1)S(1)}, bf16[128,768]{1,0:T(8,128)(2,1)S(1)}, u32[]{:S(2)}, u32[]{:S(2)}) %collective-permute-start.50) | collective-permute-done | bytes 196640 | tf_op jit(solution)/shard_map/ppermute | solution.py:51
  152.1 3.1 %collective-permute-done.80 = f32[48,128]{1,0:T(8,128)S(1)} collective-permute-done((f32[48,128]{1,0:T(8,128)S(1)}, f32[48,128]{1,0:T(8,128)S(1)}, u32[]{:S(2)}, u32[]{:S(2)}) %collective-permute-start.80) | collective-permute-done | bytes 24608 | tf_op jit(solution)/shard_map/ppermute | solution.py:669
  171.0 10.2 %collective-permute-done.66 = bf16[2,48,768]{2,1,0:T(8,128)(2,1)S(1)} collective-permute-done((bf16[2,48,768]{2,1,0:T(8,128)(2,1)S(1)}, bf16[2,48,768]{2,1,0:T(8,128)(2,1)S(1)}, u32[]{:S(2)}, u32[]{:S(2)}) %collective-permute-start.66) | collective-permute-done | bytes 147488 | tf_op jit(solution)/shard_map/ppermute | solution.py:669
  181.9 2.7 %collective-permute-start.67 = (bf16[48,768]{1,0:T(8,128)(2,1)}, bf16[48,768]{1,0:T(8,128)(2,1)S(1)}, u32[]{:S(2)}, u32[]{:S(2)}) collective-permute-start(bf16[48,768]{1,0:T(8,128)(2,1)} %get-tuple-element.252), channel_id=1, source_target_pairs={{0,16},{4,20},{8,24},{12,28},{16,0},{20,4},{24,8},{28,12},{1,17},{... | collective-permute-start | bytes 221192 | tf_op jit(solution)/shard_map/ppermute | solution.py:669
  191.2 6.0 %collective-permute-done.61 = bf16[2,64,768]{2,1,0:T(8,128)(2,1)S(1)} collective-permute-done((bf16[2,64,768]{2,1,0:T(8,128)(2,1)S(1)}, bf16[2,64,768]{2,1,0:T(8,128)(2,1)S(1)}, u32[]{:S(2)}, u32[]{:S(2)}) %collective-permute-start.61) | collective-permute-done | bytes 196640 | tf_op jit(solution)/shard_map/ppermute | solution.py:669
  197.7 11.6 %collective-permute-done.75 = bf16[3,2,2,48,384]{4,3,0,1,2:T(8,128)(2,1)S(1)} collective-permute-done((bf16[3,2,2,48,384]{4,3,0,1,2:T(8,128)(2,1)S(1)}, bf16[3,2,2,48,384]{4,3,0,1,2:T(8,128)(2,1)S(1)}, u32[]{:S(2)}, u32[]{:S(2)}) %collective-permute-start.75) | collective-permute-done | bytes 442400 | tf_op jit(solution)/shard_map/ppermute | solution.py:669
  211.8 13.6 %collective-permute-done.71 = bf16[2,2,2,48,1024]{4,3,0,1,2:T(8,128)(2,1)S(1)} collective-permute-done((bf16[2,2,2,48,1024]{4,3,0,1,2:T(8,128)(2,1)S(1)}, bf16[2,2,2,48,1024]{4,3,0,1,2:T(8,128)(2,1)S(1)}, u32[]{:S(2)}, u32[]{:S(2)}) %collective-permute-start.71) | collective-permute-done | bytes 786464 | tf_op jit(solution)/shard_map/ppermute | solution.py:669
  228.1 9.6 %collective-permute-done.72 = bf16[2,2,48,1024]{3,2,0,1:T(8,128)(2,1)S(1)} collective-permute-done((bf16[2,2,48,1024]{3,2,0,1:T(8,128)(2,1)S(1)}, bf16[2,2,48,1024]{3,2,0,1:T(8,128)(2,1)S(1)}, u32[]{:S(2)}, u32[]{:S(2)}) %collective-permute-start.72) | collective-permute-done | bytes 393248 | tf_op jit(solution)/shard_map/ppermute | solution.py:669
  241.0 2.8 %collective-permute-start.73 = (bf16[2,48,1024]{2,1,0:T(8,128)(2,1)S(1)}, bf16[2,48,1024]{2,1,0:T(8,128)(2,1)S(1)}, u32[]{:S(2)}, u32[]{:S(2)}) collective-permute-start(bf16[2,48,1024]{2,1,0:T(8,128)(2,1)S(1)} %get-tuple-element.244), channel_id=1, source_target_pairs={{0,16},{4,20},{8,24},{12,28},{16,0},{20,4},{24,8},{28,12},{1,17},{... | collective-permute-start | bytes 589832 | tf_op jit(solution)/shard_map/ppermute | solution.py:669
  244.0 6.4 %collective-permute-done.77.cross_recv = bf16[3,48,384]{2,1,0:T(8,128)(2,1)S(1)} collective-permute-done((bf16[3,48,384]{2,1,0:T(8,128)(2,1)S(1)}, bf16[3,48,384]{2,1,0:T(8,128)(2,1)S(1)}, u32[]{:S(2)}, u32[]{:S(2)}) %collective-permute-start.77) | collective-permute-done | bytes 110624 | tf_op jit(solution)/shard_map/ppermute | solution.py:669
  250.4 2.7 collective-permute-done.73.feed_recv
  256.9 3.0 %collective-permute-start.69 = (bf16[112,384]{1,0:T(8,128)(2,1)S(1)}, bf16[112,384]{1,0:T(8,128)(2,1)S(1)}, u32[]{:S(2)}, u32[]{:S(2)}) collective-permute-start(bf16[112,384]{1,0:T(8,128)(2,1)S(1)} %get-tuple-element.201), channel_id=1, source_target_pairs={{0,2},{2,18},{4,0},{6,16},{8,6},{10,22},{12,4},{14,20},{16,10},{18... | collective-permute-start | bytes 258056 | tf_op jit(solution)/shard_map/ppermute | solution.py:900
  260.0 4.8 %collective-permute-start.58 = (bf16[48,576]{1,0:T(8,128)(2,1)S(1)}, bf16[48,576]{1,0:T(8,128)(2,1)S(1)}, u32[]{:S(2)}, u32[]{:S(2)}) collective-permute-start(bf16[48,576]{1,0:T(8,128)(2,1)S(1)} %get-tuple-element.191), channel_id=1, source_target_pairs={{0,2},{2,0},{1,3},{3,1},{4,6},{6,4},{5,7},{7,5},{8,10},{10,8},{9,1... | collective-permute-start | bytes 165896 | tf_op jit(solution)/shard_map/ppermute | solution.py:51
  (248 shorter events, 110.8 us)
Async XLA Ops:
  7.4 9.7 %collective-permute-start.4 = (bf16[96,768]{1,0:T(8,128)(2,1)S(1)}, bf16[96,768]{1,0:T(8,128)(2,1)S(1)}, u32[]{:S(2)}, u32[]{:S(2)}) collective-permute-start(bf16[96,768]{1,0:T(8,128)(2,1)S(1)} %get-tuple-element.120), channel_id=1, source_target_pairs={{0,2},{2,0},{1,3},{3,1},{4,6},{6,4},{5,7},{7,5},{8,10},{10,8},{9,1... | collective-permute-start | bytes 442376 | tf_op jit(solution)/shard_map/ppermute | solution.py:51
  11.2 15.3 %collective-permute-start.28 = (bf16[96,1024]{1,0:T(8,128)(2,1)S(1)}, bf16[96,1024]{1,0:T(8,128)(2,1)S(1)}, u32[]{:S(2)}, u32[]{:S(2)}) collective-permute-start(bf16[96,1024]{1,0:T(8,128)(2,1)S(1)} %get-tuple-element.140), channel_id=1, source_target_pairs={{0,2},{2,0},{1,3},{3,1},{4,6},{6,4},{5,7},{7,5},{8,10},{10,8},{9,1... | collective-permute-start | bytes 589832 | tf_op jit(solution)/shard_map/ppermute | solution.py:51
  26.5 10.3 %collective-permute-start.14 = (bf16[192,768]{1,0:T(8,128)(2,1)S(1)}, bf16[192,768]{1,0:T(8,128)(2,1)S(1)}, u32[]{:S(2)}, u32[]{:S(2)}) collective-permute-start(bf16[192,768]{1,0:T(8,128)(2,1)S(1)} %get-tuple-element.127.own), channel_id=1, source_target_pairs={{0,2},{2,0},{1,3},{3,1},{4,6},{6,4},{5,7},{7,5},{8,10},{10,8},{9,1... | collective-permute-start | bytes 884744 | tf_op jit(solution)/shard_map/ppermute | solution.py:51
  37.0 14.4 %collective-permute-start.3 = (bf16[384,768]{1,0:T(8,128)(2,1)S(1)}, bf16[384,768]{1,0:T(8,128)(2,1)S(1)}, u32[]{:S(2)}, u32[]{:S(2)}) collective-permute-start(bf16[384,768]{1,0:T(8,128)(2,1)S(1)} %get-tuple-element.119.a0), channel_id=1, source_target_pairs={{0,1},{1,0},{2,3},{3,2},{4,5},{5,4},{6,7},{7,6},{8,9},{9,8},{10,11... | collective-permute-start | bytes 1769480 | tf_op jit(solution)/shard_map/ppermute | solution.py:55
  42.6 18.0 %collective-permute-start.17 = (bf16[384,768]{1,0:T(8,128)(2,1)S(1)}, bf16[384,768]{1,0:T(8,128)(2,1)S(1)}, u32[]{:S(2)}, u32[]{:S(2)}) collective-permute-start(bf16[384,768]{1,0:T(8,128)(2,1)S(1)} %get-tuple-element.126.a0), channel_id=1, source_target_pairs={{0,1},{1,0},{2,3},{3,2},{4,5},{5,4},{6,7},{7,6},{8,9},{9,8},{10,11... | collective-permute-start | bytes 1769480 | tf_op jit(solution)/shard_map/ppermute | solution.py:55
  47.2 33.0 %collective-permute-start.44 = (bf16[384,1024]{1,0:T(8,128)(2,1)S(1)}, bf16[384,1024]{1,0:T(8,128)(2,1)S(1)}, u32[]{:S(2)}, u32[]{:S(2)}) collective-permute-start(bf16[384,1024]{1,0:T(8,128)(2,1)S(1)} %get-tuple-element.137.fa0), channel_id=1, source_target_pairs={{0,1},{1,0},{2,3},{3,2},{4,5},{5,4},{6,7},{7,6},{8,9},{9,8},{10,11... | collective-permute-start | bytes 2359304 | tf_op jit(solution)/shard_map/ppermute | solution.py:55
  50.9 25.2 %collective-permute-start.27 = (bf16[512,384]{1,0:T(8,128)(2,1)S(1)}, bf16[512,384]{1,0:T(8,128)(2,1)S(1)}, u32[]{:S(2)}, u32[]{:S(2)}) collective-permute-start(bf16[512,384]{1,0:T(8,128)(2,1)S(1)} %get-tuple-element.139.da0), channel_id=1, source_target_pairs={{0,1},{1,0},{2,3},{3,2},{4,5},{5,4},{6,7},{7,6},{8,9},{9,8},{10,11... | collective-permute-start | bytes 1179656 | tf_op jit(solution)/shard_map/ppermute | solution.py:55
  60.0 9.8 %collective-permute-start.31 = (bf16[96,1024]{1,0:T(8,128)(2,1)S(1)}, bf16[96,1024]{1,0:T(8,128)(2,1)S(1)}, u32[]{:S(2)}, u32[]{:S(2)}) collective-permute-start(bf16[96,1024]{1,0:T(8,128)(2,1)S(1)} %collective-permute-done.29.refs_1_), channel_id=1, source_target_pairs={{0,8},{4,12},{8,0},{12,4},{16,24},{20,28},{24,16},{28,20},{1,9},{5... | collective-permute-start | bytes 589832 | tf_op jit(solution)/shard_map/ppermute | solution.py:669
  66.3 11.3 %collective-permute-start.33 = (bf16[96,1024]{1,0:T(8,128)(2,1)S(1)}, bf16[96,1024]{1,0:T(8,128)(2,1)S(1)}, u32[]{:S(2)}, u32[]{:S(2)}) collective-permute-start(bf16[96,1024]{1,0:T(8,128)(2,1)S(1)} %collective-permute-done.29.refs_1_), channel_id=1, source_target_pairs={{0,1},{1,0},{2,3},{3,2},{4,5},{5,4},{6,7},{7,6},{8,9},{9,8},{10,11... | collective-permute-start | bytes 589832 | tf_op jit(solution)/shard_map/ppermute | solution.py:55
  105.6 30.4 %collective-permute-start.63 = (bf16[192,768]{1,0:T(8,128)(2,1)}, bf16[192,768]{1,0:T(8,128)(2,1)}, u32[]{:S(2)}, u32[]{:S(2)}) collective-permute-start(bf16[192,768]{1,0:T(8,128)(2,1)} %get-tuple-element.197), channel_id=1, source_target_pairs={{0,1},{1,0},{2,3},{3,2},{4,5},{5,4},{6,7},{7,6},{8,9},{9,8},{10,11... | collective-permute-start | bytes 884744 | tf_op jit(solution)/shard_map/ppermute | solution.py:55
  118.0 19.7 %collective-permute-start.52 = (bf16[2,192,512]{2,1,0:T(8,128)(2,1)}, bf16[2,192,512]{2,1,0:T(8,128)(2,1)}, u32[]{:S(2)}, u32[]{:S(2)}) collective-permute-start(bf16[2,192,512]{2,1,0:T(8,128)(2,1)} %get-tuple-element.187), channel_id=1, source_target_pairs={{0,1},{1,0},{2,3},{3,2},{4,5},{5,4},{6,7},{7,6},{8,9},{9,8},{10,11... | collective-permute-start | bytes 1179656 | tf_op jit(solution)/shard_map/ppermute | solution.py:55
  118.5 32.9 %collective-permute-start.59 = (bf16[512,768]{1,0:T(8,128)(2,1)}, bf16[512,768]{1,0:T(8,128)(2,1)S(1)}, u32[]{:S(2)}, u32[]{:S(2)}) collective-permute-start(bf16[512,768]{1,0:T(8,128)(2,1)} %get-tuple-element.195), channel_id=1, source_target_pairs={{0,1},{1,0},{2,3},{3,2},{4,5},{5,4},{6,7},{7,6},{8,9},{9,8},{10,11... | collective-permute-start | bytes 2359304 | tf_op jit(solution)/shard_map/ppermute | solution.py:55
  120.3 67.0 %collective-permute-start.70 = (bf16[768,1024]{1,0:T(8,128)(2,1)}, bf16[768,1024]{1,0:T(8,128)(2,1)}, u32[]{:S(2)}, u32[]{:S(2)}) collective-permute-start(bf16[768,1024]{1,0:T(8,128)(2,1)} %get-tuple-element.207), channel_id=1, source_target_pairs={{0,1},{1,0},{2,3},{3,2},{4,5},{5,4},{6,7},{7,6},{8,9},{9,8},{10,11... | collective-permute-start | bytes 4718600 | tf_op jit(solution)/shard_map/ppermute | solution.py:55
  121.5 47.4 %collective-permute-start.74 = (bf16[1152,384]{1,0:T(8,128)(2,1)}, bf16[1152,384]{1,0:T(8,128)(2,1)}, u32[]{:S(2)}, u32[]{:S(2)}) collective-permute-start(bf16[1152,384]{1,0:T(8,128)(2,1)} %copy-done.14), channel_id=1, source_target_pairs={{0,1},{1,0},{2,3},{3,2},{4,5},{5,4},{6,7},{7,6},{8,9},{9,8},{10,11... | collective-permute-start | bytes 2654216 | tf_op jit(solution)/shard_map/ppermute | solution.py:55
  138.8 46.2 %collective-permute-start.54 = (bf16[1152,384]{1,0:T(8,128)(2,1)}, bf16[1152,384]{1,0:T(8,128)(2,1)}, u32[]{:S(2)}, u32[]{:S(2)}) collective-permute-start(bf16[1152,384]{1,0:T(8,128)(2,1)} %get-tuple-element.189), channel_id=1, source_target_pairs={{0,1},{1,0},{2,3},{3,2},{4,5},{5,4},{6,7},{7,6},{8,9},{9,8},{10,11... | collective-permute-start | bytes 2654216 | tf_op jit(solution)/shard_map/ppermute | solution.py:55
  155.3 11.0 %collective-permute-start.65 = (bf16[2,2,48,768]{3,2,0,1:T(8,128)(2,1)}, bf16[2,2,48,768]{3,2,0,1:T(8,128)(2,1)}, u32[]{:S(2)}, u32[]{:S(2)}) collective-permute-start(bf16[2,2,48,768]{3,2,0,1:T(8,128)(2,1)} %bitcast.113), channel_id=1, source_target_pairs={{0,4},{4,0},{8,12},{12,8},{16,20},{20,16},{24,28},{28,24},{1,5},{5... | collective-permute-start | bytes 884744 | tf_op jit(solution)/shard_map/ppermute | solution.py:669
  165.6 99.2 %collective-permute-start.51 = (f32[192,128]{1,0:T(8,128)S(1)}, f32[192,128]{1,0:T(8,128)}, u32[]{:S(2)}, u32[]{:S(2)}) collective-permute-start(f32[192,128]{1,0:T(8,128)S(1)} %get-tuple-element.179), channel_id=1, source_target_pairs={{0,1},{1,0},{2,3},{3,2},{4,5},{5,4},{6,7},{7,6},{8,9},{9,8},{10,11... | collective-permute-start | bytes 294920 | tf_op jit(solution)/shard_map/ppermute | solution.py:55
  166.3 18.3 %collective-permute-start.60 = (bf16[2,2,64,768]{3,2,1,0:T(8,128)(2,1)}, bf16[2,2,64,768]{3,2,1,0:T(8,128)(2,1)S(1)}, u32[]{:S(2)}, u32[]{:S(2)}) collective-permute-start(bf16[2,2,64,768]{3,2,1,0:T(8,128)(2,1)} %dynamic-slice_bitcast_fusion.1), channel_id=1, source_target_pairs={{0,8},{4,12},{8,0},{12,4},{16,24},{20,28},{24,16},{28,20},{1,9},{5... | collective-permute-start | bytes 1179656 | tf_op jit(solution)/shard_map/ppermute | solution.py:669
  168.9 12.3 %collective-permute-start.66 = (bf16[2,48,768]{2,1,0:T(8,128)(2,1)S(1)}, bf16[2,48,768]{2,1,0:T(8,128)(2,1)S(1)}, u32[]{:S(2)}, u32[]{:S(2)}) collective-permute-start(bf16[2,48,768]{2,1,0:T(8,128)(2,1)S(1)} %dynamic-slice_bitcast_fusion.7), channel_id=1, source_target_pairs={{0,8},{4,12},{8,0},{12,4},{16,24},{20,28},{24,16},{28,20},{1,9},{5... | collective-permute-start | bytes 442376 | tf_op jit(solution)/shard_map/ppermute | solution.py:669
  181.9 74.2 %collective-permute-start.67 = (bf16[48,768]{1,0:T(8,128)(2,1)}, bf16[48,768]{1,0:T(8,128)(2,1)S(1)}, u32[]{:S(2)}, u32[]{:S(2)}) collective-permute-start(bf16[48,768]{1,0:T(8,128)(2,1)} %get-tuple-element.252), channel_id=1, source_target_pairs={{0,16},{4,20},{8,24},{12,28},{16,0},{20,4},{24,8},{28,12},{1,17},{... | collective-permute-start | bytes 221192 | tf_op jit(solution)/shard_map/ppermute | solution.py:669
  184.7 12.4 %collective-permute-start.61 = (bf16[2,64,768]{2,1,0:T(8,128)(2,1)S(1)}, bf16[2,64,768]{2,1,0:T(8,128)(2,1)S(1)}, u32[]{:S(2)}, u32[]{:S(2)}) collective-permute-start(bf16[2,64,768]{2,1,0:T(8,128)(2,1)S(1)} %dynamic-slice_bitcast_fusion.6), channel_id=1, source_target_pairs={{0,16},{4,20},{8,24},{12,28},{16,0},{20,4},{24,8},{28,12},{1,17},{... | collective-permute-start | bytes 589832 | tf_op jit(solution)/shard_map/ppermute | solution.py:669
  186.7 23.2 %collective-permute-start.55 = (bf16[3,2,2,48,384]{4,3,0,1,2:T(8,128)(2,1)S(1)}, bf16[3,2,2,48,384]{4,3,0,1,2:T(8,128)(2,1)S(1)}, u32[]{:S(2)}, u32[]{:S(2)}) collective-permute-start(bf16[3,2,2,48,384]{4,3,0,1,2:T(8,128)(2,1)S(1)} %bitcast.122), channel_id=1, source_target_pairs={{0,4},{4,0},{8,12},{12,8},{16,20},{20,16},{24,28},{28,24},{1,5},{5... | collective-permute-start | bytes 1327112 | tf_op jit(solution)/shard_map/ppermute | solution.py:669
  187.3 22.0 %collective-permute-start.75 = (bf16[3,2,2,48,384]{4,3,0,1,2:T(8,128)(2,1)S(1)}, bf16[3,2,2,48,384]{4,3,0,1,2:T(8,128)(2,1)S(1)}, u32[]{:S(2)}, u32[]{:S(2)}) collective-permute-start(bf16[3,2,2,48,384]{4,3,0,1,2:T(8,128)(2,1)S(1)} %bitcast.123), channel_id=1, source_target_pairs={{0,4},{4,0},{8,12},{12,8},{16,20},{20,16},{24,28},{28,24},{1,5},{5... | collective-permute-start | bytes 1327112 | tf_op jit(solution)/shard_map/ppermute | solution.py:669
  197.1 28.3 %collective-permute-start.71 = (bf16[2,2,2,48,1024]{4,3,0,1,2:T(8,128)(2,1)S(1)}, bf16[2,2,2,48,1024]{4,3,0,1,2:T(8,128)(2,1)S(1)}, u32[]{:S(2)}, u32[]{:S(2)}) collective-permute-start(bf16[2,2,2,48,1024]{4,3,0,1,2:T(8,128)(2,1)S(1)} %bitcast.121), channel_id=1, source_target_pairs={{0,4},{4,0},{8,12},{12,8},{16,20},{20,16},{24,28},{28,24},{1,5},{5... | collective-permute-start | bytes 2359304 | tf_op jit(solution)/shard_map/ppermute | solution.py:669
  209.3 46.8 %collective-permute-start.62 = (bf16[64,768]{1,0:T(8,128)(2,1)S(1)}, bf16[64,768]{1,0:T(8,128)(2,1)S(1)}, u32[]{:S(2)}, u32[]{:S(2)}) collective-permute-start(bf16[64,768]{1,0:T(8,128)(2,1)S(1)} %get-tuple-element.250), channel_id=1, source_target_pairs={{0,4},{4,0},{8,12},{12,8},{16,20},{20,16},{24,28},{28,24},{1,5},{5... | collective-permute-start | bytes 294920 | tf_op jit(solution)/shard_map/ppermute | solution.py:669
  210.0 17.5 %collective-permute-start.76 = (bf16[3,2,48,384]{3,2,0,1:T(8,128)(2,1)S(1)}, bf16[3,2,48,384]{3,2,0,1:T(8,128)(2,1)S(1)}, u32[]{:S(2)}, u32[]{:S(2)}) collective-permute-start(bf16[3,2,48,384]{3,2,0,1:T(8,128)(2,1)S(1)} %dynamic-slice_bitcast_fusion.2), channel_id=1, source_target_pairs={{0,8},{4,12},{8,0},{12,4},{16,24},{20,28},{24,16},{28,20},{1,9},{5... | collective-permute-start | bytes 663560 | tf_op jit(solution)/shard_map/ppermute | solution.py:669
  225.8 11.9 %collective-permute-start.72 = (bf16[2,2,48,1024]{3,2,0,1:T(8,128)(2,1)S(1)}, bf16[2,2,48,1024]{3,2,0,1:T(8,128)(2,1)S(1)}, u32[]{:S(2)}, u32[]{:S(2)}) collective-permute-start(bf16[2,2,48,1024]{3,2,0,1:T(8,128)(2,1)S(1)} %dynamic-slice_bitcast_fusion), channel_id=1, source_target_pairs={{0,8},{4,12},{8,0},{12,4},{16,24},{20,28},{24,16},{28,20},{1,9},{5... | collective-permute-start | bytes 1179656 | tf_op jit(solution)/shard_map/ppermute | solution.py:669
  227.5 13.6 %collective-permute-start.56 = (bf16[3,2,48,384]{3,2,0,1:T(8,128)(2,1)S(1)}, bf16[3,2,48,384]{3,2,0,1:T(8,128)(2,1)S(1)}, u32[]{:S(2)}, u32[]{:S(2)}) collective-permute-start(bf16[3,2,48,384]{3,2,0,1:T(8,128)(2,1)S(1)} %dynamic-slice_bitcast_fusion.3), channel_id=1, source_target_pairs={{0,8},{4,12},{8,0},{12,4},{16,24},{20,28},{24,16},{28,20},{1,9},{5... | collective-permute-start | bytes 663560 | tf_op jit(solution)/shard_map/ppermute | solution.py:669
  237.7 12.7 %collective-permute-start.77 = (bf16[3,48,384]{2,1,0:T(8,128)(2,1)S(1)}, bf16[3,48,384]{2,1,0:T(8,128)(2,1)S(1)}, u32[]{:S(2)}, u32[]{:S(2)}) collective-permute-start(bf16[3,48,384]{2,1,0:T(8,128)(2,1)S(1)} %get-tuple-element.246), channel_id=1, source_target_pairs={{0,16},{4,20},{8,24},{12,28},{16,0},{20,4},{24,8},{28,12},{1,17},{... | collective-permute-start | bytes 331784 | tf_op jit(solution)/shard_map/ppermute | solution.py:669
  241.0 12.1 %collective-permute-start.73 = (bf16[2,48,1024]{2,1,0:T(8,128)(2,1)S(1)}, bf16[2,48,1024]{2,1,0:T(8,128)(2,1)S(1)}, u32[]{:S(2)}, u32[]{:S(2)}) collective-permute-start(bf16[2,48,1024]{2,1,0:T(8,128)(2,1)S(1)} %get-tuple-element.244), channel_id=1, source_target_pairs={{0,16},{4,20},{8,24},{12,28},{16,0},{20,4},{24,8},{28,12},{1,17},{... | collective-permute-start | bytes 589832 | tf_op jit(solution)/shard_map/ppermute | solution.py:669
  253.2 14.8 %collective-permute-start.78 = (bf16[48,1600]{1,0:T(8,128)(2,1)S(1)}, bf16[48,1600]{1,0:T(8,128)(2,1)S(1)}, u32[]{:S(2)}, u32[]{:S(2)}) collective-permute-start(bf16[48,1600]{1,0:T(8,128)(2,1)S(1)} %get-tuple-element.211), channel_id=1, source_target_pairs={{0,2},{2,0},{1,3},{3,1},{4,6},{6,4},{5,7},{7,5},{8,10},{10,8},{9,1... | collective-permute-start | bytes 460808 | tf_op jit(solution)/shard_map/ppermute | solution.py:51
  256.2 10.3 %collective-permute-start.68 = (bf16[112,384]{1,0:T(8,128)(2,1)S(1)}, bf16[112,384]{1,0:T(8,128)(2,1)S(1)}, u32[]{:S(2)}, u32[]{:S(2)}) collective-permute-start(bf16[112,384]{1,0:T(8,128)(2,1)S(1)} %get-tuple-element.200), channel_id=1, source_target_pairs={{0,0},{2,16},{4,2},{6,18},{8,4},{10,20},{12,6},{14,22},{16,8},{18,... | collective-permute-start | bytes 258056 | tf_op jit(solution)/shard_map/ppermute | solution.py:900
  (71 other events, 582.7 us)

commit v3 on v2

--- a/solution.py
+++ b/solution.py
@@ -587,6 +587,47 @@
     small_send[16:, :] = tables[1]
 
 
+def split_blocks(blocks, count, at, bit, mine, send):
+    per = mine.shape[0] * 2 // count
+
+    def body(value):
+        for block in range(count):
+            place = ((block >> (at + 1)) << at) | (block & ((1 << at) - 1))
+            ref = mine if ((block >> at) & 1) == value else send
+            ref[place * per : (place + 1) * per, :] = blocks(block)
+
+    for value in (0, 1):
+        pl.when(((lax.axis_index("dp") >> bit) & 1) == value)(lambda value=value: body(value))
+
+
+def stage_of(count, at, bit):
+    def halve_blocks(keep, recv, mine, send):
+        per = keep.shape[0] // count
+
+        def total(block):
+            lines = slice(block * per, (block + 1) * per)
+            return (keep[lines, :].astype(F32) + recv[lines, :].astype(F32)).astype(BF)
+
+        split_blocks(total, count, at, bit, mine, send)
+
+    return halve_blocks
+
+
+def halve_pair(count, bit):
+    def halve_outs(keep, recv, other_keep, other_recv, mine, send):
+        per = keep.shape[0] // count
+
+        def total(block):
+            lines = slice(block * per, (block + 1) * per)
+            first = keep[lines, :].astype(F32) + recv[lines, :].astype(F32)
+            second = other_keep[lines, :].astype(F32) + other_recv[lines, :].astype(F32)
+            return jnp.concatenate([first, second], axis=0).astype(BF)
+
+        split_blocks(total, count, 0, bit, mine, send)
+
+    return halve_outs
+
+
 def finish_early(feed_keep, feed_recv, cross_keep, cross_recv, mine, send):
     for half, ref in ((0, mine), (1, send)):
         feed = feed_keep[half].astype(F32) + feed_recv[half].astype(F32)
@@ -683,14 +724,27 @@
             values = (keep.astype(F32) + recv.astype(F32)).astype(BF)
         return keep, recv
 
+    def halvings(keep, recv, groups, order):
+        per = keep.shape[0] // (groups * replicas)
+        left = list(range(bits - 1, -1, -1))
+        for bit in order:
+            at = len(left) - 1 - left.index(bit)
+            count = groups << len(left)
+            shape = ((keep.shape[0] // 2, keep.shape[1]), BF)
+            keep, send = call(stage_of(count, at, bit), [shape, shape], keep, recv)
+            left.remove(bit)
+            recv = replica_swap(send, bit)
+        shape = (groups, per, keep.shape[1]) if groups > 1 else (per, keep.shape[1])
+        return keep.reshape(shape), recv.reshape(shape)
+
     def spread(values):
         direct = row_swap(values)
         beside = replica_swap(direct, 0)
         parts = (direct, beside, replica_swap(direct, 1), replica_swap(beside, 1))
         return parts, tuple(col_swap(part) for part in parts)
 
-    def core_sum(keep, send):
-        return (keep.astype(F32) + col_swap(send).astype(F32)).astype(BF)
+    def add(keep, recv):
+        return (keep.astype(F32) + recv.astype(F32)).astype(BF)
 
     def layer(
         hidden_in, encoder_states, token_segments, source_segments, buckets, gain_self, gain_cross,
@@ -784,13 +838,13 @@
         fi_keep, fi_send = call(
             feed_grads, [((768, 1024), BF), ((768, 1024), BF)],
             normed_feed, gate_delta, up_delta,)
-        in_feed = core_sum(fi_keep, fi_send)
+        fi_recv = col_swap(fi_send)
         fo_keep, fo_send, last_keep, last_send = call(
             feed_out,
             [((512, 768), BF), ((512, 768), BF), ((128, 384), F32), ((128, 384), BF)],
             hidden, ec, resid_cross, *dw, hbm=(2,),
         )
-        out_feed = core_sum(fo_keep, fo_send)
+        fo_recv = col_swap(fo_send)
 
         (grad_cross, upstream_cross, gain_feed_sum, cross_delta, dscores, probs, cross_dq, part,
          send) = call(
@@ -807,8 +861,8 @@
              ((2, 192, 512), F32), ((2, 192, 512), BF)],
             ec, normed_cross, cross_q, cross_delta, dscores, probs, cross_dq, cross_mixed,
             upstream_cross, *cw,)
-        in_cross = core_sum(ci_keep, ci_send)
-        out_cross = core_sum(co_keep, co_send)
+        ci_recv = col_swap(ci_send)
+        co_recv = col_swap(co_send)
 
         (grad_attn, gain_cross_sum, dscores, dya, dyb, si_keep, si_send, so_keep, so_send) = call(
             self_backward,
@@ -818,8 +872,8 @@
             xg, gains, part, recv, grad_cross, resid_attn, *sw, normed_self, ya, yb, bias,
             self_lse, self_mixed, hbm=(0, 1),
         )
-        in_self = core_sum(si_keep, si_send)
-        out_self = core_sum(so_keep, so_send)
+        si_recv = col_swap(si_send)
+        so_recv = col_swap(so_send)
         keep, send = call(self_inputs, part_shape, dya, dyb, *sw)
         keep, send = call(self_sum, part_shape, keep, col_swap(send))
         recv = row_swap(send)
@@ -861,13 +915,34 @@
         def blocks_of(values):
             return values.reshape(replicas, values.shape[0] // replicas, 768)
 
-        feed_pair = scatter(in_feed.reshape(2, replicas, per, 1024), 1, forward)
-        out_pair = scatter(blocks_of(out_feed), 0, backward)
-        cross_pair = scatter(in_cross.reshape(3, replicas, per, 384), 1, forward)
-        self_pair = scatter(in_self.reshape(3, replicas, per, 384), 1, forward)
-        rest_pair = scatter(
-            jnp.concatenate((blocks_of(out_cross), blocks_of(out_self)), axis=1), 0, forward
-        )
+        if per % 16 == 0:
+            feed_pair = halvings(fi_keep, fi_recv, 2, forward)
+            out_pair = halvings(fo_keep, fo_recv, 1, backward)
+            cross_pair = halvings(ci_keep, ci_recv, 3, forward)
+            self_pair = halvings(si_keep, si_recv, 3, forward)
+            shape = ((192, 768), BF)
+            keep, send = call(
+                halve_pair(replicas, 0), [shape, shape], co_keep, co_recv, so_keep, so_recv
+            )
+            recv = replica_swap(send, 0)
+            for bit in forward[1:]:
+                shape = ((keep.shape[0] // 2, 768), BF)
+                keep, send = call(
+                    stage_of(replicas >> bit, 0, bit), [shape, shape], keep, recv
+                )
+                recv = replica_swap(send, bit)
+            rest_pair = (keep, recv)
+        else:
+            in_feed, out_feed = add(fi_keep, fi_recv), add(fo_keep, fo_recv)
+            in_cross, in_self = add(ci_keep, ci_recv), add(si_keep, si_recv)
+            out_cross, out_self = add(co_keep, co_recv), add(so_keep, so_recv)
+            feed_pair = scatter(in_feed.reshape(2, replicas, per, 1024), 1, forward)
+            out_pair = scatter(blocks_of(out_feed), 0, backward)
+            cross_pair = scatter(in_cross.reshape(3, replicas, per, 384), 1, forward)
+            self_pair = scatter(in_self.reshape(3, replicas, per, 384), 1, forward)
+            rest_pair = scatter(
+                jnp.concatenate((blocks_of(out_cross), blocks_of(out_self)), axis=1), 0, forward,
+            )
 
         mine, send = call(
             finish_early, [((per, 1600), F32), ((per, 1600), BF)],

time: 270 us -> 222 us (0.82)
  waiting for transfers between devices: 108 us -> 74.3 us
  other arithmetic: 13.3 us -> 4.84 us
  local copies, waits for them, and re-layouts: 7.6 us -> 2.98 us
    ppermute x30, waiting for transfers between devices: 84.6 us -> 50.2 us  [replica_swap(): lax.ppermute(values, 'dp', [(i, i ^ 1 << bit) for i in range(replicas)])]
    convert_element_type x16 -> x0, other arithmetic: 8.34 us -> none  [the longest x6 6.23 us: core_sum(): return (keep.astype(F32) + col_swap(send).astype(F32)).astype(BF)]
    unnamed x42 -> x29, local copies, waits for them, and re-layouts: 4.73 us -> 1.61 us
    pallas_call x25 -> x40, Pallas kernels: 64.4 us -> 67 us  [call(): pl.pallas_call(kernel, out_shape=flat, in_specs=[space] * len(args), out_...]
  transfers between devices with their start and end apart: 83 -> 83, of which waited for: 31 -> 27; matrix products, arithmetic and copies ran while one was open for 7% -> 3% of each run, Pallas kernels for 17% -> 27%
where the time goes in v3:
time: 222 us
  waiting for transfers between devices  74.3 us (33%)
  starting transfers between devices  71.4 us (32%)
  Pallas kernels  67 us (30%)
  other arithmetic  4.84 us (2%)
  local copies, waits for them, and re-layouts  2.98 us (1%)
    pallas_call x40, Pallas kernels, call(): pl.pallas_call(kernel, out_shape=flat, in_specs=[space] * len(args), out_...  67 us
    ppermute x30, waiting for transfers between devices, replica_swap(): lax.ppermute(values, 'dp', [(i, i ^ 1 << bit) for i in range(replicas)])  50.2 us
    ppermute x30, starting transfers between devices, replica_swap(): lax.ppermute(values, 'dp', [(i, i ^ 1 << bit) for i in range(replicas)])  41.6 us
    ppermute x15, starting transfers between devices, row_swap(): return lax.ppermute(values, 'row', SWAP)  21.8 us
    ppermute x15, waiting for transfers between devices, row_swap(): return lax.ppermute(values, 'row', SWAP)  21.6 us
    ppermute x36, starting transfers between devices, col_swap(): return lax.ppermute(values, 'col', SWAP)  4.94 us
  transfers between devices with their start and end apart: 83, of which 27 were waited for; matrix products, arithmetic and copies ran while one was open for 3% of the time, Pallas kernels for 27%

profile of v3, /device:TPU:0, one launch (start us, length us, event | category | flops | bytes accessed | tf_op | source)
XLA Modules:
  0.0 221.6 jit_solution(3684936985452142267)
XLA Ops:
  2.4 3.1 %collective-permute-start.36 = (bf16[128,384]{1,0:T(8,128)(2,1)S(1)}, bf16[128,384]{1,0:T(8,128)(2,1)S(1)}, u32[]{:S(2)}, u32[]{:S(2)}) collective-permute-start(bf16[128,384]{1,0:T(8,128)(2,1)S(1)} %get-tuple-element.171), channel_id=1, source_target_pairs={{0,2},{2,0},{1,3},{3,1},{4,6},{6,4},{5,7},{7,5},{8,10},{10,8},{9,1... | collective-permute-start | bytes 294920 | tf_op jit(solution)/shard_map/ppermute | solution.py:51
  7.4 1.9 collective-permute-start.4
  17.2 3.2 %collective-permute-done.18.p0 = bf16[96,768]{1,0:T(8,128)(2,1)S(1)} collective-permute-done((bf16[96,768]{1,0:T(8,128)(2,1)S(1)}, bf16[96,768]{1,0:T(8,128)(2,1)S(1)}, u32[]{:S(2)}, u32[]{:S(2)}) %collective-permute-start.18) | collective-permute-done | bytes 147488 | tf_op jit(solution)/shard_map/ppermute | solution.py:51
  31.6 1.8 collective-permute-done.20.p2
  43.1 2.5 %collective-permute-done.7.p3 = bf16[96,768]{1,0:T(8,128)(2,1)S(1)} collective-permute-done((bf16[96,768]{1,0:T(8,128)(2,1)S(1)}, bf16[96,768]{1,0:T(8,128)(2,1)S(1)}, u32[]{:S(2)}, u32[]{:S(2)}) %collective-permute-start.7) | collective-permute-done | bytes 147488 | tf_op jit(solution)/shard_map/ppermute | solution.py:710
  47.8 3.2 %collective-permute-done.21.p3 = bf16[96,768]{1,0:T(8,128)(2,1)S(1)} collective-permute-done((bf16[96,768]{1,0:T(8,128)(2,1)S(1)}, bf16[96,768]{1,0:T(8,128)(2,1)S(1)}, u32[]{:S(2)}, u32[]{:S(2)}) %collective-permute-start.21) | collective-permute-done | bytes 147488 | tf_op jit(solution)/shard_map/ppermute | solution.py:710
  51.5 2.7 %shard_map.307 = (f32[6,128,256]{2,1,0:T(8,128)}, f32[128,512]{1,0:T(8,128)}) custom-call(s32[256,256]{1,0:T(8,128)} %buckets.3, f32[8,128]{1,0:T(8,128)S(1)} %pad.4.table, f32[8,128]{1,0:T(8,128)S(1)} %collective-permute-done.12.peer_table, s32[1,256]{1,0:T(1,128)} %segment.1, s32[1,512]{1,0:T(1,128)} %source.1), custom_call_target="tpu_custom_call" | custom-call | tf_op jit(solution)/shard_map/pallas_call | solution.py:40
  54.2 4.3 %shard_map.308 = (bf16[256,768]{1,0:T(8,128)(2,1)}, f32[16,768]{1,0:T(8,128)}, bf16[384,768]{1,0:T(8,128)(2,1)}, bf16[384,768]{1,0:T(8,128)(2,1)}, bf16[256,768]...) custom-call(bf16[192,272]{1,0:T(8,128)(2,1)S(1)} %get-tuple-element., ...), custom_call_target="tpu_custom_call" | custom-call | tf_op jit(solution)/shard_map/pallas_call | solution.py:40
  62.0 2.6 %shard_map.310 = (bf16[768,768]{1,0:T(8,128)(2,1)}, bf16[384,768]{1,0:T(8,128)(2,1)}, bf16[384,768]{1,0:T(8,128)(2,1)}, bf16[512,384]{1,0:T(8,128)(2,1)}, bf16[512,384]{1,0:T(8,128)(2,1)}) custom-call(bf16[192,768]{1,0:T(8,128)(2,1)S(1)} %get-tuple-element.157.own, bf16[192,768]{1,0:T(8,128)(2,1)S(1)} %collective-permute-done.14.recv, ...), custom_call_target="tpu_custom_call" | custom-call | tf_op jit(solution)/shard_map/pallas_call | solution.py:40
  66.4 3.5 %collective-permute-done.31.refs_3_ = bf16[96,1024]{1,0:T(8,128)(2,1)S(1)} collective-permute-done((bf16[96,1024]{1,0:T(8,128)(2,1)S(1)}, bf16[96,1024]{1,0:T(8,128)(2,1)S(1)}, u32[]{:S(2)}, u32[]{:S(2)}) %collective-permute-start.31) | collective-permute-done | bytes 196640 | tf_op jit(solution)/shard_map/ppermute | solution.py:710
  70.4 5.8 %shard_map.311 = (f32[128,768]{1,0:T(8,128)}, bf16[128,768]{1,0:T(8,128)(2,1)}, bf16[128,384]{1,0:T(8,128)(2,1)}, bf16[128,384]{1,0:T(8,128)(2,1)}, f32[6,128,1]...) custom-call(bf16[256,768]{1,0:T(8,128)(2,1)} %get-tuple-element.152.xg, ...), custom_call_target="tpu_custom_call" | custom-call | tf_op jit(solution)/shard_map/pallas_call | solution.py:40
  77.6 2.6 %shard_map.313 = (bf16[384,1024]{1,0:T(8,128)(2,1)S(1)}, bf16[384,1024]{1,0:T(8,128)(2,1)S(1)}, bf16[512,384]{1,0:T(8,128)(2,1)}, bf16[512,384]{1,0:T(8,128)(2,1)}, f32[128,1024]{1,0:T(8,128)S(1)}) custom-call(bf16[768,768]{1,0:T(8,128)(2,1)} %get-tuple-element.168.ec, bf16[512,384]{1,0:T(8,128)(2,1)S(1)} %get-tuple-element.169.da0, ...), custom_call_target="tpu_custom_call" | custom-call | tf_op jit(solution)/shard_map/pallas_call | solution.py:40
  80.3 2.8 %collective-permute-done.26.recv = bf16[128,768]{1,0:T(8,128)(2,1)S(1)} collective-permute-done((bf16[128,768]{1,0:T(8,128)(2,1)S(1)}, bf16[128,768]{1,0:T(8,128)(2,1)S(1)}, u32[]{:S(2)}, u32[]{:S(2)}) %collective-permute-start.26) | collective-permute-done | bytes 196640 | tf_op jit(solution)/shard_map/ppermute | solution.py:51
  83.0 3.7 %shard_map.314 = (f32[128,768]{1,0:T(8,128)}, bf16[128,768]{1,0:T(8,128)(2,1)S(1)}, bf16[128,1024]{1,0:T(8,128)(2,1)}, bf16[128,1024]{1,0:T(8,128)(2,1)S(1)}, bf...) custom-call(bf16[256,768]{1,0:T(8,128)(2,1)} %get-tuple-element.152.xg, ...), custom_call_target="tpu_custom_call" | custom-call | tf_op jit(solution)/shard_map/pallas_call | solution.py:40
  89.4 5.9 %collective-permute-done.47.recv = bf16[128,768]{1,0:T(8,128)(2,1)S(1)} collective-permute-done((bf16[128,768]{1,0:T(8,128)(2,1)S(1)}, bf16[128,768]{1,0:T(8,128)(2,1)S(1)}, u32[]{:S(2)}, u32[]{:S(2)}) %collective-permute-start.47) | collective-permute-done | bytes 196640 | tf_op jit(solution)/shard_map/ppermute | solution.py:51
  95.3 5.3 %shard_map.317 = (f32[128,768]{1,0:T(8,128)}, bf16[128,768]{1,0:T(8,128)(2,1)S(1)}, f32[8,768]{1,0:T(8,128)}, bf16[128,384]{1,0:T(8,128)(2,1)S(1)}, bf16[6,128,5...) custom-call(bf16[256,768]{1,0:T(8,128)(2,1)} %get-tuple-element.152., ...), custom_call_target="tpu_custom_call" | custom-call | tf_op jit(solution)/shard_map/pallas_call | solution.py:40
  100.5 5.3 %shard_map.323 = (bf16[1152,384]{1,0:T(8,128)(2,1)S(1)}, bf16[1152,384]{1,0:T(8,128)(2,1)S(1)}, bf16[192,768]{1,0:T(8,128)(2,1)S(1)}, bf16[192,768]{1,0:T(8,128)...) custom-call(bf16[768,768]{1,0:T(8,128)(2,1)} %get-tuple-element.168.ec, ...), custom_call_target="tpu_custom_call" | custom-call | tf_op jit(solution)/shard_map/pallas_call | solution.py:40
  107.5 3.5 %shard_map.315 = (bf16[512,768]{1,0:T(8,128)(2,1)S(1)}, bf16[512,768]{1,0:T(8,128)(2,1)S(1)}, f32[128,384]{1,0:T(8,128)}, bf16[128,384]{1,0:T(8,128)(2,1)S(1)}) custom-call(bf16[128,1024]{1,0:T(8,128)(2,1)} %get-tuple-element.175.hidden, bf16[768,768]{1,0:T(8,128)(2,1)} %get-tuple-element.168.ec, f32[128,768]{1,0:T(8,128)} %get-tuple-element.176.resid.resid_in, ...), custom_call_target="tpu_custom_call" | custom-call | tf_op jit(solution)/shard_map/pallas_call | solution.py:40
  113.2 6.3 %shard_map.318 = (f32[128,768]{1,0:T(8,128)}, f32[8,768]{1,0:T(8,128)}, f32[6,128,256]{2,1,0:T(8,128)S(1)}, bf16[256,576]{1,0:T(8,128)(2,1)S(1)}, bf16[256,576]{...) custom-call(bf16[256,768]{1,0:T(8,128)(2,1)} %get-tuple-element.152., ...), custom_call_target="tpu_custom_call" | custom-call | tf_op jit(solution)/shard_map/pallas_call | solution.py:40
  119.5 2.6 %shard_map.319 = (f32[128,768]{1,0:T(8,128)S(1)}, bf16[128,768]{1,0:T(8,128)(2,1)S(1)}) custom-call(bf16[256,576]{1,0:T(8,128)(2,1)S(1)} %get-tuple-element.198.dya, bf16[256,576]{1,0:T(8,128)(2,1)S(1)} %get-tuple-element.199.dyb, bf16[384,768]{1,0:T(8,128)(2,1)} %copy-done.2, bf16[384,768]{1,0:T(8,128)(2,1)} %get-tuple-element.191.a1, ...), custom_call_target="tpu_custom_call" | custom-call | tf_op jit(solution)/shard_map/pallas_call | solution.py:40
  125.8 5.3 %collective-permute-done.50.recv = bf16[128,768]{1,0:T(8,128)(2,1)S(1)} collective-permute-done((bf16[128,768]{1,0:T(8,128)(2,1)S(1)}, bf16[128,768]{1,0:T(8,128)(2,1)S(1)}, u32[]{:S(2)}, u32[]{:S(2)}) %collective-permute-start.50) | collective-permute-done | bytes 196640 | tf_op jit(solution)/shard_map/ppermute | solution.py:51
  132.7 3.8 %shard_map.321.tables = f32[2,32,128]{2,1,0:T(8,128)S(1)} custom-call(s32[256,256]{1,0:T(8,128)} %buckets.3, f32[6,128,256]{2,1,0:T(8,128)S(1)} %get-tuple-element.207.dscores), custom_call_target="tpu_custom_call" | custom-call | tf_op jit(solution)/shard_map/pallas_call | solution.py:40
  136.4 2.1 shard_map.322
  142.6 10.4 %collective-permute-done.80 = f32[48,128]{1,0:T(8,128)S(1)} collective-permute-done((f32[48,128]{1,0:T(8,128)S(1)}, f32[48,128]{1,0:T(8,128)S(1)}, u32[]{:S(2)}, u32[]{:S(2)}) %collective-permute-start.80) | collective-permute-done | bytes 24608 | tf_op jit(solution)/shard_map/ppermute | solution.py:710
  161.7 5.8 %collective-permute-done.81 = f32[48,128]{1,0:T(8,128)} collective-permute-done((f32[48,128]{1,0:T(8,128)S(1)}, f32[48,128]{1,0:T(8,128)}, u32[]{:S(2)}, u32[]{:S(2)}) %collective-permute-start.81) | collective-permute-done | bytes 24608 | tf_op jit(solution)/shard_map/ppermute | solution.py:710
  172.0 2.6 %collective-permute-start.82 = (f32[48,128]{1,0:T(8,128)S(1)}, f32[48,128]{1,0:T(8,128)S(1)}, u32[]{:S(2)}, u32[]{:S(2)}) collective-permute-start(f32[48,128]{1,0:T(8,128)S(1)} %add.27), channel_id=1, source_target_pairs={{0,16},{4,20},{8,24},{12,28},{16,0},{20,4},{24,8},{28,12},{1,17},{... | collective-permute-start | bytes 73736 | tf_op jit(solution)/shard_map/ppermute | solution.py:710
  178.7 6.4 %collective-permute-done.72.recv = bf16[192,1024]{1,0:T(8,128)(2,1)S(1)} collective-permute-done((bf16[192,1024]{1,0:T(8,128)(2,1)}, bf16[192,1024]{1,0:T(8,128)(2,1)S(1)}, u32[]{:S(2)}, u32[]{:S(2)}) %collective-permute-start.72) | collective-permute-done | bytes 393248 | tf_op jit(solution)/shard_map/ppermute | solution.py:710
  185.2 4.4 %collective-permute-start.77 = (bf16[144,384]{1,0:T(8,128)(2,1)S(1)}, bf16[144,384]{1,0:T(8,128)(2,1)S(1)}, u32[]{:S(2)}, u32[]{:S(2)}) collective-permute-start(bf16[144,384]{1,0:T(8,128)(2,1)S(1)} %get-tuple-element.269), channel_id=1, source_target_pairs={{0,16},{4,20},{8,24},{12,28},{16,0},{20,4},{24,8},{28,12},{1,17},{... | collective-permute-start | bytes 331784 | tf_op jit(solution)/shard_map/ppermute | solution.py:710
  192.5 2.9 %collective-permute-start.67 = (bf16[48,768]{1,0:T(8,128)(2,1)S(1)}, bf16[48,768]{1,0:T(8,128)(2,1)S(1)}, u32[]{:S(2)}, u32[]{:S(2)}) collective-permute-start(bf16[48,768]{1,0:T(8,128)(2,1)S(1)} %get-tuple-element.247), channel_id=1, source_target_pairs={{0,16},{4,20},{8,24},{12,28},{16,0},{20,4},{24,8},{28,12},{1,17},{... | collective-permute-start | bytes 221192 | tf_op jit(solution)/shard_map/ppermute | solution.py:710
  200.1 8.4 %collective-permute-done.73 = bf16[96,1024]{1,0:T(8,128)(2,1)S(1)} collective-permute-done((bf16[96,1024]{1,0:T(8,128)(2,1)S(1)}, bf16[96,1024]{1,0:T(8,128)(2,1)S(1)}, u32[]{:S(2)}, u32[]{:S(2)}) %collective-permute-start.73) | collective-permute-done | bytes 196640 | tf_op jit(solution)/shard_map/ppermute | solution.py:710
  212.2 2.3 %collective-permute-start.69 = (bf16[112,384]{1,0:T(8,128)(2,1)S(1)}, bf16[112,384]{1,0:T(8,128)(2,1)S(1)}, u32[]{:S(2)}, u32[]{:S(2)}) collective-permute-start(bf16[112,384]{1,0:T(8,128)(2,1)S(1)} %get-tuple-element.249), channel_id=1, source_target_pairs={{0,2},{2,18},{4,0},{6,16},{8,6},{10,22},{12,4},{14,20},{16,10},{18... | collective-permute-start | bytes 258056 | tf_op jit(solution)/shard_map/ppermute | solution.py:975
  214.5 3.2 %collective-permute-start.58 = (bf16[48,576]{1,0:T(8,128)(2,1)S(1)}, bf16[48,576]{1,0:T(8,128)(2,1)S(1)}, u32[]{:S(2)}, u32[]{:S(2)}) collective-permute-start(bf16[48,576]{1,0:T(8,128)(2,1)S(1)} %get-tuple-element.227), channel_id=1, source_target_pairs={{0,2},{2,0},{1,3},{3,1},{4,6},{6,4},{5,7},{7,5},{8,10},{10,8},{9,1... | collective-permute-start | bytes 165896 | tf_op jit(solution)/shard_map/ppermute | solution.py:51
  (217 shorter events, 90.5 us)
Async XLA Ops:
  11.2 15.3 %collective-permute-start.28 = (bf16[96,1024]{1,0:T(8,128)(2,1)S(1)}, bf16[96,1024]{1,0:T(8,128)(2,1)S(1)}, u32[]{:S(2)}, u32[]{:S(2)}) collective-permute-start(bf16[96,1024]{1,0:T(8,128)(2,1)S(1)} %get-tuple-element.170), channel_id=1, source_target_pairs={{0,2},{2,0},{1,3},{3,1},{4,6},{6,4},{5,7},{7,5},{8,10},{10,8},{9,1... | collective-permute-start | bytes 589832 | tf_op jit(solution)/shard_map/ppermute | solution.py:51
  37.0 14.4 %collective-permute-start.3 = (bf16[384,768]{1,0:T(8,128)(2,1)S(1)}, bf16[384,768]{1,0:T(8,128)(2,1)S(1)}, u32[]{:S(2)}, u32[]{:S(2)}) collective-permute-start(bf16[384,768]{1,0:T(8,128)(2,1)S(1)} %get-tuple-element.149.a0), channel_id=1, source_target_pairs={{0,1},{1,0},{2,3},{3,2},{4,5},{5,4},{6,7},{7,6},{8,9},{9,8},{10,11... | collective-permute-start | bytes 1769480 | tf_op jit(solution)/shard_map/ppermute | solution.py:55
  42.6 18.0 %collective-permute-start.17 = (bf16[384,768]{1,0:T(8,128)(2,1)S(1)}, bf16[384,768]{1,0:T(8,128)(2,1)S(1)}, u32[]{:S(2)}, u32[]{:S(2)}) collective-permute-start(bf16[384,768]{1,0:T(8,128)(2,1)S(1)} %get-tuple-element.156.a0), channel_id=1, source_target_pairs={{0,1},{1,0},{2,3},{3,2},{4,5},{5,4},{6,7},{7,6},{8,9},{9,8},{10,11... | collective-permute-start | bytes 1769480 | tf_op jit(solution)/shard_map/ppermute | solution.py:55
  47.2 33.0 %collective-permute-start.44 = (bf16[384,1024]{1,0:T(8,128)(2,1)S(1)}, bf16[384,1024]{1,0:T(8,128)(2,1)S(1)}, u32[]{:S(2)}, u32[]{:S(2)}) collective-permute-start(bf16[384,1024]{1,0:T(8,128)(2,1)S(1)} %get-tuple-element.167.fa0), channel_id=1, source_target_pairs={{0,1},{1,0},{2,3},{3,2},{4,5},{5,4},{6,7},{7,6},{8,9},{9,8},{10,11... | collective-permute-start | bytes 2359304 | tf_op jit(solution)/shard_map/ppermute | solution.py:55
  50.9 25.2 %collective-permute-start.27 = (bf16[512,384]{1,0:T(8,128)(2,1)S(1)}, bf16[512,384]{1,0:T(8,128)(2,1)S(1)}, u32[]{:S(2)}, u32[]{:S(2)}) collective-permute-start(bf16[512,384]{1,0:T(8,128)(2,1)S(1)} %get-tuple-element.169.da0), channel_id=1, source_target_pairs={{0,1},{1,0},{2,3},{3,2},{4,5},{5,4},{6,7},{7,6},{8,9},{9,8},{10,11... | collective-permute-start | bytes 1179656 | tf_op jit(solution)/shard_map/ppermute | solution.py:55
  87.9 34.8 %collective-permute-start.70 = (bf16[768,1024]{1,0:T(8,128)(2,1)S(1)}, bf16[768,1024]{1,0:T(8,128)(2,1)S(1)}, u32[]{:S(2)}, u32[]{:S(2)}) collective-permute-start(bf16[768,1024]{1,0:T(8,128)(2,1)S(1)} %get-tuple-element.255), channel_id=1, source_target_pairs={{0,1},{1,0},{2,3},{3,2},{4,5},{5,4},{6,7},{7,6},{8,9},{9,8},{10,11... | collective-permute-start | bytes 4718600 | tf_op jit(solution)/shard_map/ppermute | solution.py:55
  105.8 18.0 %collective-permute-start.74 = (bf16[1152,384]{1,0:T(8,128)(2,1)S(1)}, bf16[1152,384]{1,0:T(8,128)(2,1)S(1)}, u32[]{:S(2)}, u32[]{:S(2)}) collective-permute-start(bf16[1152,384]{1,0:T(8,128)(2,1)S(1)} %get-tuple-element.263), channel_id=1, source_target_pairs={{0,1},{1,0},{2,3},{3,2},{4,5},{5,4},{6,7},{7,6},{8,9},{9,8},{10,11... | collective-permute-start | bytes 2654216 | tf_op jit(solution)/shard_map/ppermute | solution.py:55
  107.3 15.8 %collective-permute-start.63 = (bf16[192,768]{1,0:T(8,128)(2,1)S(1)}, bf16[192,768]{1,0:T(8,128)(2,1)S(1)}, u32[]{:S(2)}, u32[]{:S(2)}) collective-permute-start(bf16[192,768]{1,0:T(8,128)(2,1)S(1)} %get-tuple-element.239), channel_id=1, source_target_pairs={{0,1},{1,0},{2,3},{3,2},{4,5},{5,4},{6,7},{7,6},{8,9},{9,8},{10,11... | collective-permute-start | bytes 884744 | tf_op jit(solution)/shard_map/ppermute | solution.py:55
  122.2 30.9 %collective-permute-start.54 = (bf16[1152,384]{1,0:T(8,128)(2,1)S(1)}, bf16[1152,384]{1,0:T(8,128)(2,1)S(1)}, u32[]{:S(2)}, u32[]{:S(2)}) collective-permute-start(bf16[1152,384]{1,0:T(8,128)(2,1)S(1)} %get-tuple-element.219), channel_id=1, source_target_pairs={{0,1},{1,0},{2,3},{3,2},{4,5},{5,4},{6,7},{7,6},{8,9},{9,8},{10,11... | collective-permute-start | bytes 2654216 | tf_op jit(solution)/shard_map/ppermute | solution.py:55
  122.6 17.3 %collective-permute-start.59 = (bf16[512,768]{1,0:T(8,128)(2,1)S(1)}, bf16[512,768]{1,0:T(8,128)(2,1)S(1)}, u32[]{:S(2)}, u32[]{:S(2)}) collective-permute-start(bf16[512,768]{1,0:T(8,128)(2,1)S(1)} %get-tuple-element.231), channel_id=1, source_target_pairs={{0,1},{1,0},{2,3},{3,2},{4,5},{5,4},{6,7},{7,6},{8,9},{9,8},{10,11... | collective-permute-start | bytes 2359304 | tf_op jit(solution)/shard_map/ppermute | solution.py:55
  123.1 33.5 %collective-permute-start.71 = (bf16[384,1024]{1,0:T(8,128)(2,1)S(1)}, bf16[384,1024]{1,0:T(8,128)(2,1)S(1)}, u32[]{:S(2)}, u32[]{:S(2)}) collective-permute-start(bf16[384,1024]{1,0:T(8,128)(2,1)S(1)} %get-tuple-element.257), channel_id=1, source_target_pairs={{0,4},{4,0},{8,12},{12,8},{16,20},{20,16},{24,28},{28,24},{1,5},{5... | collective-permute-start | bytes 2359304 | tf_op jit(solution)/shard_map/ppermute | solution.py:710
  123.7 14.9 %collective-permute-start.64 = (bf16[192,768]{1,0:T(8,128)(2,1)S(1)}, bf16[192,768]{1,0:T(8,128)(2,1)S(1)}, u32[]{:S(2)}, u32[]{:S(2)}) collective-permute-start(bf16[192,768]{1,0:T(8,128)(2,1)S(1)} %get-tuple-element.241), channel_id=1, source_target_pairs={{0,1},{1,0},{2,3},{3,2},{4,5},{5,4},{6,7},{7,6},{8,9},{9,8},{10,11... | collective-permute-start | bytes 884744 | tf_op jit(solution)/shard_map/ppermute | solution.py:55
  131.1 25.1 %collective-permute-start.75 = (bf16[576,384]{1,0:T(8,128)(2,1)S(1)}, bf16[576,384]{1,0:T(8,128)(2,1)S(1)}, u32[]{:S(2)}, u32[]{:S(2)}) collective-permute-start(bf16[576,384]{1,0:T(8,128)(2,1)S(1)} %get-tuple-element.265), channel_id=1, source_target_pairs={{0,4},{4,0},{8,12},{12,8},{16,20},{20,16},{24,28},{28,24},{1,5},{5... | collective-permute-start | bytes 1327112 | tf_op jit(solution)/shard_map/ppermute | solution.py:710
  139.8 14.8 %collective-permute-start.52 = (bf16[2,192,512]{2,1,0:T(8,128)(2,1)S(1)}, bf16[2,192,512]{2,1,0:T(8,128)(2,1)S(1)}, u32[]{:S(2)}, u32[]{:S(2)}) collective-permute-start(bf16[2,192,512]{2,1,0:T(8,128)(2,1)S(1)} %get-tuple-element.217), channel_id=1, source_target_pairs={{0,1},{1,0},{2,3},{3,2},{4,5},{5,4},{6,7},{7,6},{8,9},{9,8},{10,11... | collective-permute-start | bytes 1179656 | tf_op jit(solution)/shard_map/ppermute | solution.py:55
  140.0 13.1 %collective-permute-start.80 = (f32[48,128]{1,0:T(8,128)S(1)}, f32[48,128]{1,0:T(8,128)S(1)}, u32[]{:S(2)}, u32[]{:S(2)}) collective-permute-start(f32[48,128]{1,0:T(8,128)S(1)} %add.25), channel_id=1, source_target_pairs={{0,4},{4,0},{8,12},{12,8},{16,20},{20,16},{24,28},{28,24},{1,5},{5... | collective-permute-start | bytes 73736 | tf_op jit(solution)/shard_map/ppermute | solution.py:710
  153.1 16.7 %collective-permute-start.65 = (bf16[192,768]{1,0:T(8,128)(2,1)S(1)}, bf16[192,768]{1,0:T(8,128)(2,1)S(1)}, u32[]{:S(2)}, u32[]{:S(2)}) collective-permute-start(bf16[192,768]{1,0:T(8,128)(2,1)S(1)} %get-tuple-element.243), channel_id=1, source_target_pairs={{0,4},{4,0},{8,12},{12,8},{16,20},{20,16},{24,28},{28,24},{1,5},{5... | collective-permute-start | bytes 884744 | tf_op jit(solution)/shard_map/ppermute | solution.py:710
  154.6 17.4 %collective-permute-start.60 = (bf16[256,768]{1,0:T(8,128)(2,1)}, bf16[256,768]{1,0:T(8,128)(2,1)S(1)}, u32[]{:S(2)}, u32[]{:S(2)}) collective-permute-start(bf16[256,768]{1,0:T(8,128)(2,1)} %get-tuple-element.233), channel_id=1, source_target_pairs={{0,8},{4,12},{8,0},{12,4},{16,24},{20,28},{24,16},{28,20},{1,9},{5... | collective-permute-start | bytes 1179656 | tf_op jit(solution)/shard_map/ppermute | solution.py:710
  156.7 20.3 %collective-permute-start.55 = (bf16[576,384]{1,0:T(8,128)(2,1)}, bf16[576,384]{1,0:T(8,128)(2,1)S(1)}, u32[]{:S(2)}, u32[]{:S(2)}) collective-permute-start(bf16[576,384]{1,0:T(8,128)(2,1)} %get-tuple-element.221), channel_id=1, source_target_pairs={{0,4},{4,0},{8,12},{12,8},{16,20},{20,16},{24,28},{28,24},{1,5},{5... | collective-permute-start | bytes 1327112 | tf_op jit(solution)/shard_map/ppermute | solution.py:710
  160.2 18.1 %collective-permute-start.76 = (bf16[288,384]{1,0:T(8,128)(2,1)}, bf16[288,384]{1,0:T(8,128)(2,1)S(1)}, u32[]{:S(2)}, u32[]{:S(2)}) collective-permute-start(bf16[288,384]{1,0:T(8,128)(2,1)} %get-tuple-element.267), channel_id=1, source_target_pairs={{0,8},{4,12},{8,0},{12,4},{16,24},{20,28},{24,16},{28,20},{1,9},{5... | collective-permute-start | bytes 663560 | tf_op jit(solution)/shard_map/ppermute | solution.py:710
  167.5 17.6 %collective-permute-start.72 = (bf16[192,1024]{1,0:T(8,128)(2,1)}, bf16[192,1024]{1,0:T(8,128)(2,1)S(1)}, u32[]{:S(2)}, u32[]{:S(2)}) collective-permute-start(bf16[192,1024]{1,0:T(8,128)(2,1)} %get-tuple-element.259), channel_id=1, source_target_pairs={{0,8},{4,12},{8,0},{12,4},{16,24},{20,28},{24,16},{28,20},{1,9},{5... | collective-permute-start | bytes 1179656 | tf_op jit(solution)/shard_map/ppermute | solution.py:710
  169.8 15.4 %collective-permute-start.53 = (bf16[192,512]{1,0:T(8,128)(2,1)}, bf16[192,512]{1,0:T(8,128)(2,1)}, u32[]{:S(2)}, u32[]{:S(2)}) collective-permute-start(bf16[192,512]{1,0:T(8,128)(2,1)} %fusion.2), channel_id=1, source_target_pairs={{0,2},{2,0},{1,3},{3,1},{4,6},{6,4},{5,7},{7,5},{8,10},{10,8},{9,1... | collective-permute-start | bytes 589832 | tf_op jit(solution)/shard_map/ppermute | solution.py:51
  172.0 17.6 %collective-permute-start.82 = (f32[48,128]{1,0:T(8,128)S(1)}, f32[48,128]{1,0:T(8,128)S(1)}, u32[]{:S(2)}, u32[]{:S(2)}) collective-permute-start(f32[48,128]{1,0:T(8,128)S(1)} %add.27), channel_id=1, source_target_pairs={{0,16},{4,20},{8,24},{12,28},{16,0},{20,4},{24,8},{28,12},{1,17},{... | collective-permute-start | bytes 73736 | tf_op jit(solution)/shard_map/ppermute | solution.py:710
  177.0 14.5 %collective-permute-start.66 = (bf16[96,768]{1,0:T(8,128)(2,1)}, bf16[96,768]{1,0:T(8,128)(2,1)S(1)}, u32[]{:S(2)}, u32[]{:S(2)}) collective-permute-start(bf16[96,768]{1,0:T(8,128)(2,1)} %get-tuple-element.245), channel_id=1, source_target_pairs={{0,8},{4,12},{8,0},{12,4},{16,24},{20,28},{24,16},{28,20},{1,9},{5... | collective-permute-start | bytes 442376 | tf_op jit(solution)/shard_map/ppermute | solution.py:710
  178.3 14.2 %collective-permute-start.61 = (bf16[128,768]{1,0:T(8,128)(2,1)S(1)}, bf16[128,768]{1,0:T(8,128)(2,1)S(1)}, u32[]{:S(2)}, u32[]{:S(2)}) collective-permute-start(bf16[128,768]{1,0:T(8,128)(2,1)S(1)} %get-tuple-element.235), channel_id=1, source_target_pairs={{0,16},{4,20},{8,24},{12,28},{16,0},{20,4},{24,8},{28,12},{1,17},{... | collective-permute-start | bytes 589832 | tf_op jit(solution)/shard_map/ppermute | solution.py:710
  185.1 11.9 %collective-permute-start.56 = (bf16[288,384]{1,0:T(8,128)(2,1)}, bf16[288,384]{1,0:T(8,128)(2,1)S(1)}, u32[]{:S(2)}, u32[]{:S(2)}) collective-permute-start(bf16[288,384]{1,0:T(8,128)(2,1)} %get-tuple-element.223), channel_id=1, source_target_pairs={{0,8},{4,12},{8,0},{12,4},{16,24},{20,28},{24,16},{28,20},{1,9},{5... | collective-permute-start | bytes 663560 | tf_op jit(solution)/shard_map/ppermute | solution.py:710
  185.2 13.5 %collective-permute-start.77 = (bf16[144,384]{1,0:T(8,128)(2,1)S(1)}, bf16[144,384]{1,0:T(8,128)(2,1)S(1)}, u32[]{:S(2)}, u32[]{:S(2)}) collective-permute-start(bf16[144,384]{1,0:T(8,128)(2,1)S(1)} %get-tuple-element.269), channel_id=1, source_target_pairs={{0,16},{4,20},{8,24},{12,28},{16,0},{20,4},{24,8},{28,12},{1,17},{... | collective-permute-start | bytes 331784 | tf_op jit(solution)/shard_map/ppermute | solution.py:710
  189.6 18.9 %collective-permute-start.73 = (bf16[96,1024]{1,0:T(8,128)(2,1)S(1)}, bf16[96,1024]{1,0:T(8,128)(2,1)S(1)}, u32[]{:S(2)}, u32[]{:S(2)}) collective-permute-start(bf16[96,1024]{1,0:T(8,128)(2,1)S(1)} %get-tuple-element.261), channel_id=1, source_target_pairs={{0,16},{4,20},{8,24},{12,28},{16,0},{20,4},{24,8},{28,12},{1,17},{... | collective-permute-start | bytes 589832 | tf_op jit(solution)/shard_map/ppermute | solution.py:710
  191.5 26.2 %collective-permute-start.51 = (f32[192,128]{1,0:T(8,128)}, f32[192,128]{1,0:T(8,128)S(1)}, u32[]{:S(2)}, u32[]{:S(2)}) collective-permute-start(f32[192,128]{1,0:T(8,128)} %get-tuple-element.209), channel_id=1, source_target_pairs={{0,1},{1,0},{2,3},{3,2},{4,5},{5,4},{6,7},{7,6},{8,9},{9,8},{10,11... | collective-permute-start | bytes 294920 | tf_op jit(solution)/shard_map/ppermute | solution.py:55
  192.5 18.9 %collective-permute-start.67 = (bf16[48,768]{1,0:T(8,128)(2,1)S(1)}, bf16[48,768]{1,0:T(8,128)(2,1)S(1)}, u32[]{:S(2)}, u32[]{:S(2)}) collective-permute-start(bf16[48,768]{1,0:T(8,128)(2,1)S(1)} %get-tuple-element.247), channel_id=1, source_target_pairs={{0,16},{4,20},{8,24},{12,28},{16,0},{20,4},{24,8},{28,12},{1,17},{... | collective-permute-start | bytes 221192 | tf_op jit(solution)/shard_map/ppermute | solution.py:710
  197.0 14.5 %collective-permute-start.62 = (bf16[64,768]{1,0:T(8,128)(2,1)S(1)}, bf16[64,768]{1,0:T(8,128)(2,1)S(1)}, u32[]{:S(2)}, u32[]{:S(2)}) collective-permute-start(bf16[64,768]{1,0:T(8,128)(2,1)S(1)} %get-tuple-element.237), channel_id=1, source_target_pairs={{0,4},{4,0},{8,12},{12,8},{16,20},{20,16},{24,28},{28,24},{1,5},{5... | collective-permute-start | bytes 294920 | tf_op jit(solution)/shard_map/ppermute | solution.py:710
  198.7 15.7 %collective-permute-start.57 = (bf16[144,384]{1,0:T(8,128)(2,1)S(1)}, bf16[144,384]{1,0:T(8,128)(2,1)S(1)}, u32[]{:S(2)}, u32[]{:S(2)}) collective-permute-start(bf16[144,384]{1,0:T(8,128)(2,1)S(1)} %get-tuple-element.225), channel_id=1, source_target_pairs={{0,16},{4,20},{8,24},{12,28},{16,0},{20,4},{24,8},{28,12},{1,17},{... | collective-permute-start | bytes 331784 | tf_op jit(solution)/shard_map/ppermute | solution.py:710
  208.6 12.1 %collective-permute-start.78 = (bf16[48,1600]{1,0:T(8,128)(2,1)S(1)}, bf16[48,1600]{1,0:T(8,128)(2,1)S(1)}, u32[]{:S(2)}, u32[]{:S(2)}) collective-permute-start(bf16[48,1600]{1,0:T(8,128)(2,1)S(1)} %get-tuple-element.271), channel_id=1, source_target_pairs={{0,2},{2,0},{1,3},{3,1},{4,6},{6,4},{5,7},{7,5},{8,10},{10,8},{9,1... | collective-permute-start | bytes 460808 | tf_op jit(solution)/shard_map/ppermute | solution.py:51
  (65 other events, 628.1 us)
